TPU v7x, 32 devices: a whole 2x2x4 slice. The times are simulated.
32 devices in a mesh: groups: 2 (over y), seq: 4 (over z), fsdp: 4 (over x, core).
Axes of the slice: x: 2, y: 2, z: 4, core: 2. Of those that a mesh axis runs over, the one named last changes fastest.
Arguments:
- tokens: bfloat16 [1024, 1024], P(('groups', 'seq')), parts along dimension 0, may hold values from -16 to 16
- qkv_weight: bfloat16 [1024, 1536], P('seq', 'fsdp'), may hold values from -0.125 to 0.125
- covisible: int32 [8, 4], P('groups'), parts along dimension 0, may hold values 0 or 1
- block_drive: int32 [8], P('groups'), parts along dimension 0, may hold values from 0 to 2
- grad_out: bfloat16 [1024, 512], P(('groups', 'seq'), 'fsdp'), parts along dimension 0, may hold values from -6 to 6
Outputs:
- attention: bfloat16 [1024, 512], P(('groups', 'seq'), 'fsdp'), parts along dimension 0
- grad_input: bfloat16 [1024, 1024], P(('groups', 'seq'), 'fsdp'), parts along dimension 0
- grad_weight: float32 [2048, 1536], P(('groups', 'seq'), 'fsdp'), parts along dimension 0
There are 2 independent parts, one for each index of `groups`. A program takes and returns all parts, laid end to end along the dimension named above; an argument that names none is the same for every part. Nothing has to cross between parts.
All inputs are finite; a program needn't handle non-finite values.
Results may differ from a plain program's by a relative error of at most 0.018.
The roundings to bfloat16 on the way count: a program that leaves them out, or rounds other values in their place, can miss the bound.
Values may be sent and summed in bfloat16 or wider, within the bound.
No kernel may reach another device: no remote copies, remote signals or barrier semaphores. Data moves between devices by JAX's collectives and lax.ppermute only.
A program may use at most 64 MiB of HBM per device.

v0:
```python
import jax
import jax.numpy as jnp
from jax import lax
from jax.sharding import PartitionSpec as P

HD = 64
BLOCK = 128


MASKED_SCORE = -1e30


def query_visible(covisible, block_drive, first_block, block_count):
    own_rows = lax.dynamic_slice_in_dim(covisible, first_block, block_count, 0)
    own_drive = lax.dynamic_slice_in_dim(block_drive, first_block, block_count, 0)
    joined = jnp.logical_or(own_rows == 1, own_drive[:, None] == block_drive[None, :])
    return joined.astype(jnp.float32)


def key_visible(covisible, block_drive, first_block, block_count):
    own_columns = lax.dynamic_slice_in_dim(covisible, first_block, block_count, 1)
    own_drive = lax.dynamic_slice_in_dim(block_drive, first_block, block_count, 0)
    joined = jnp.logical_or(own_columns == 1, block_drive[:, None] == own_drive[None, :])
    return joined.astype(jnp.float32)


def block_onehot(length, block_total):
    member = lax.iota(jnp.int32, length) // BLOCK
    return (member[:, None] == lax.iota(jnp.int32, block_total)[None, :]).astype(jnp.float32)


def per_device(tokens, qkv_weight, covisible, block_drive, grad_out):
    local_rows = tokens.shape[0]
    seq_count = lax.axis_size("seq")
    seq_index = lax.axis_index("seq")
    out_width = qkv_weight.shape[1]
    local_heads = out_width // (3 * HD)
    block_count = local_rows // BLOCK
    block_total = covisible.shape[0]
    first_block = seq_index * block_count
    scaling = HD ** (-0.5)
    rows_visible = query_visible(covisible, block_drive, first_block, block_count)
    columns_visible = key_visible(covisible, block_drive, first_block, block_count)
    inputs = tokens
    projected = jnp.dot(
        inputs,
        lax.all_gather(qkv_weight, "seq", axis=0, tiled=True),
        preferred_element_type=jnp.float32,
    )
    projected = projected.astype(jnp.bfloat16).reshape(local_rows, local_heads, 3, HD)
    queries = projected[:, :, 0, :]
    local_keys = projected[:, :, 1, :]
    local_values = projected[:, :, 2, :]
    key_value = projected[:, :, 1:, :].reshape(local_rows, local_heads * 2 * HD)

    def local_visible(length):
        onehot = block_onehot(length, block_total)
        return (jnp.repeat(jnp.dot(rows_visible, onehot.T), BLOCK, axis=0) > 0.5)[None]

    panel = lax.all_gather(key_value, "seq", axis=0, tiled=True)
    running_max = jnp.full((local_heads, local_rows), MASKED_SCORE, jnp.float32)
    length = panel.shape[0]
    visible = local_visible(length)
    split_panel = panel.reshape(length, local_heads, 2, HD)
    scores = (
        jnp.einsum(
            "qhd,khd->hqk", queries, split_panel[:, :, 0, :], preferred_element_type=jnp.float32
        )
        * scaling
    )
    new_max = jnp.maximum(running_max, jnp.where(visible, scores, MASKED_SCORE).max(axis=2))
    shifted = jnp.exp(jnp.where(visible, scores - new_max[:, :, None], MASKED_SCORE))
    running_sum = shifted.sum(axis=2)
    wide_values = split_panel[:, :, 1, :].astype(jnp.float32)
    weighted = jnp.einsum(
        "hqk,khd->hqd",
        shifted,
        wide_values,
        precision=lax.Precision.HIGHEST,
        preferred_element_type=jnp.float32,
    )
    running_max, running_sum, weighted = (new_max, running_sum, weighted)
    attention_heads = (weighted / running_sum[:, :, None]).astype(jnp.bfloat16)
    attention = jnp.transpose(attention_heads, (1, 0, 2)).reshape(local_rows, local_heads * HD)
    log_total = running_max + jnp.log(running_sum)
    grad_heads = grad_out.reshape(local_rows, local_heads, HD)
    grad_dot_rows = jnp.sum(
        grad_heads.astype(jnp.float32)
        * attention.reshape(local_rows, local_heads, HD).astype(jnp.float32),
        axis=2,
    )
    grad_dot = jnp.transpose(grad_dot_rows)
    log_total_rows = jnp.transpose(log_total)
    all_log_total, all_grad_dot = (
        lax.all_gather(log_total_rows, "seq", axis=0, tiled=True),
        lax.all_gather(grad_dot_rows, "seq", axis=0, tiled=True),
    )
    query_rows = queries.reshape(local_rows, local_heads * HD)
    far_queries = lax.all_gather(query_rows, "seq", axis=0, tiled=True)
    far_grads = lax.all_gather(grad_out, "seq", axis=0, tiled=True)
    length = far_queries.shape[0]
    onehot = block_onehot(length, block_total)
    visible = (jnp.repeat(jnp.dot(onehot, columns_visible), BLOCK, axis=1) > 0.5)[None]
    far_heads = far_queries.reshape(length, local_heads, HD)
    far_grad_heads = far_grads.reshape(length, local_heads, HD)
    far_log_total = jnp.transpose(all_log_total)
    far_grad_dot = jnp.transpose(all_grad_dot)
    scores = (
        jnp.einsum("qhd,khd->hqk", far_heads, local_keys, preferred_element_type=jnp.float32)
        * scaling
    )
    probabilities = jnp.exp(jnp.where(visible, scores - far_log_total[:, :, None], MASKED_SCORE))
    grad_prob = jnp.einsum(
        "qhd,khd->hqk", far_grad_heads, local_values, preferred_element_type=jnp.float32
    )
    grad_score = (probabilities * (grad_prob - far_grad_dot[:, :, None]) * scaling).astype(
        jnp.bfloat16
    )
    grad_keys = jnp.einsum(
        "hqk,qhd->khd", grad_score, far_heads, preferred_element_type=jnp.float32
    )
    grad_values = jnp.einsum(
        "hqk,qhd->khd",
        probabilities.astype(jnp.bfloat16),
        far_grad_heads,
        preferred_element_type=jnp.float32,
    )
    grad_keys, grad_values = (grad_keys, grad_values)
    panel = lax.all_gather(key_value, "seq", axis=0, tiled=True)
    length = panel.shape[0]
    visible = local_visible(length)
    split_panel = panel.reshape(length, local_heads, 2, HD)
    panel_keys = split_panel[:, :, 0, :]
    scores = (
        jnp.einsum("qhd,khd->hqk", queries, panel_keys, preferred_element_type=jnp.float32)
        * scaling
    )
    probabilities = jnp.exp(jnp.where(visible, scores - log_total[:, :, None], MASKED_SCORE))
    grad_prob = jnp.einsum(
        "qhd,khd->hqk", grad_heads, split_panel[:, :, 1, :], preferred_element_type=jnp.float32
    )
    grad_score = (probabilities * (grad_prob - grad_dot[:, :, None]) * scaling).astype(jnp.bfloat16)
    grad_queries = jnp.einsum(
        "hqk,khd->qhd", grad_score, panel_keys, preferred_element_type=jnp.float32
    )
    grad_qkv = (
        jnp.stack([grad_queries, grad_keys, grad_values], axis=2)
        .astype(jnp.bfloat16)
        .reshape(local_rows, out_width)
    )
    partial_input = lax.dot_general(
        grad_qkv,
        lax.all_gather(qkv_weight, "seq", axis=0, tiled=True),
        (((1,), (1,)), ((), ())),
        preferred_element_type=jnp.float32,
    )
    grad_input = lax.psum_scatter(partial_input, "fsdp", scatter_dimension=1, tiled=True).astype(
        jnp.bfloat16
    )
    token_scale = (local_rows * seq_count) ** (-0.5)
    column_tokens = lax.all_to_all(tokens, "seq", split_axis=1, concat_axis=0, tiled=True)
    inputs = column_tokens
    summed_rows = lax.dot_general(
        inputs,
        lax.all_gather(grad_qkv, "seq", axis=0, tiled=True),
        (((0,), (0,)), ((), ())),
        preferred_element_type=jnp.float32,
    )
    grad_weight = summed_rows * token_scale
    return (attention, grad_input, grad_weight)


def solution(mesh):
    in_specs = (
        P(("groups", "seq"), None),
        P("seq", "fsdp"),
        P("groups", None),
        P("groups"),
        P(("groups", "seq"), "fsdp"),
    )
    out_specs = (
        P(("groups", "seq"), "fsdp"),
        P(("groups", "seq"), "fsdp"),
        P(("groups", "seq"), "fsdp"),
    )
    return jax.shard_map(
        per_device, mesh=mesh, in_specs=in_specs, out_specs=out_specs, check_vma=False
    )
```

profile of v0, /device:TPU:0, one launch (start us, length us, event | category | flops | bytes accessed | tf_op | source)
XLA Modules:
  0.0 121.6 jit_solution(15169649852441177908)
XLA Ops:
  7.2 0.0 reduce-scatter.2.cloned.1.call-start
  7.2 0.0 copy-start.3
  7.2 0.6 copy-done.3
  7.9 0.0 copy-start.2
  7.9 0.6 dynamic_slice.11
  8.5 0.1 copy-done.2
  8.6 0.9 fusion.35
  9.5 0.0 copy-start
  9.5 21.6 %all_gather.23 = bf16[1024,384]{1,0:T(8,128)(2,1)S(1)} all-gather(bf16[256,384]{1,0:T(8,128)(2,1)} %param.6), channel_id=1, replica_groups=mesh['groups'=2,'seq'=4,'fsdp'=4] {'seq'}, dimensions={0}, use_global_device_ids=true | all-gather | bytes 983040 | tf_op jit(solution)/shard_map/all_gather | solution.py:47
  31.1 0.0 copy-done
  31.1 0.3 convolution_convert_fusion
  31.4 0.1 copy.26
  31.6 12.8 %all_gather.24 = bf16[512,256]{0,1:T(8,128)(2,1)S(1)} all-gather(bf16[128,256]{0,1:T(8,128)(2,1)S(1)} %bitcast.145), channel_id=1, replica_groups=mesh['groups'=2,'seq'=4,'fsdp'=4] {'seq'}, dimensions={0}, use_global_device_ids=true | all-gather | bytes 327680 | tf_op jit(solution)/shard_map/all_gather | solution.py:60
  44.4 0.3 select_reduce_fusion
  44.7 0.2 fusion.24
  45.0 0.1 constant_dynamic-slice_fusion
  45.1 0.0 copy-start.1
  45.1 0.8 copy-done.1
  45.8 0.1 copy.30
  45.9 13.3 %all_gather.27 = bf16[512,128]{1,0:T(8,128)(2,1)S(1)} all-gather(bf16[128,128]{1,0:T(8,128)(2,1)S(1)} %copy-done.1), channel_id=1, replica_groups=mesh['groups'=2,'seq'=4,'fsdp'=4] {'seq'}, dimensions={0}, use_global_device_ids=true | all-gather | bytes 163840 | tf_op jit(solution)/shard_map/all_gather | solution.py:100
  59.3 8.2 %all_gather.26 = f32[512,2]{0,1:T(2,128)S(1)} all-gather(f32[128,2]{0,1:T(2,128)S(1)} %bitcast_add_fusion), channel_id=1, replica_groups=mesh['groups'=2,'seq'=4,'fsdp'=4] {'seq'}, dimensions={0}, use_global_device_ids=true | all-gather | bytes 5120 | tf_op jit(solution)/shard_map/all_gather | solution.py:95
  67.5 0.1 copy.46
  67.6 0.9 fusion.34
  68.5 12.3 %all_gather.25 = bf16[512,128]{0,1:T(8,128)(2,1)S(1)} all-gather(bf16[128,128]{0,1:T(8,128)(2,1)S(1)} %bitcast.146), channel_id=1, replica_groups=mesh['groups'=2,'seq'=4,'fsdp'=4] {'seq'}, dimensions={0}, use_global_device_ids=true | all-gather | bytes 163840 | tf_op jit(solution)/shard_map/all_gather | solution.py:99
  80.8 0.6 multiply_reduce_fusion
  81.3 8.0 %all_gather.28 = f32[512,2]{0,1:T(2,128)S(1)} all-gather(f32[128,2]{0,1:T(2,128)S(1)} %get-tuple-element.14), channel_id=1, replica_groups=mesh['groups'=2,'seq'=4,'fsdp'=4] {'seq'}, dimensions={0}, use_global_device_ids=true | all-gather | bytes 5120 | tf_op jit(solution)/shard_map/all_gather | solution.py:96
  89.4 0.1 copy.34
  89.5 0.4 fusion.6
  89.9 0.2 fusion.20
  90.1 0.4 fusion.19
  90.5 0.5 fusion.18
  91.0 1.2 fusion.62
  92.2 0.0 reduce-scatter.2.cloned.1.call-update
  92.2 0.8 copy.37
  93.0 3.4 %all-to-all-start = ((bf16[128,4,256]{0,2,1:T(8,128)(2,1)}), bf16[128,4,256]{0,2,1:T(8,128)(2,1)S(1)}, u32[]{:S(2)}, u32[]{:S(2)}) async-start(bf16[128,4,256]{0,2,1:T(8,128)(2,1)} %bitcast.36), calls=%async_computation.1 | async-start | bytes 524288 | tf_op jit(solution)/shard_map/all_to_all | solution.py:161
  96.5 0.7 copy.39
  97.2 14.2 %all_gather.29 = bf16[512,384]{0,1:T(8,128)(2,1)S(1)} all-gather(bf16[128,384]{0,1:T(8,128)(2,1)S(1)} %bitcast.134), channel_id=1, replica_groups=mesh['groups'=2,'seq'=4,'fsdp'=4] {'seq'}, dimensions={0}, use_global_device_ids=true | all-gather | bytes 491520 | tf_op jit(solution)/shard_map/all_gather | solution.py:165
  111.4 0.0 all-to-all-done
  111.4 0.1 copy.38
  111.6 0.3 fusion.11
  111.8 0.9 copy.40
  112.7 0.5 reduce-scatter.2.cloned.1.call-done
  113.2 1.5 %convert_element_type.44 = bf16[128,256]{1,0:T(8,128)(2,1)} convert(f32[128,256]{1,0:T(8,128)} %reduce-scatter.2.cloned.1.call-done) | non-fusion elementwise | flops 32768 | bytes 196608 | tf_op jit(solution)/shard_map/convert_element_type | solution.py:157
  (10 shorter events, 0.1 us)
Async XLA Ops:
  7.2 106.1 %reduce-scatter.2.cloned.1.call-start = ((), (), s32[]{:S(2)}) async-start(), calls=%async_computation.2 | async-start | bytes 655360 | tf_op jit(solution)/shard_map/reduce_scatter | solution.py:157
  7.2 0.7 copy-start.3
  7.9 0.7 copy-start.2
  9.5 21.6 %copy-start = (bf16[128,1024]{1,0:T(8,128)(2,1)S(1)}, bf16[128,1024]{1,0:T(8,128)(2,1)}, u32[]{:S(2)}) copy-start(bf16[128,1024]{1,0:T(8,128)(2,1)} %param.5) | copy-start | bytes 786436
  45.1 0.8 copy-start.1
  93.0 18.4 %all-to-all-start = ((bf16[128,4,256]{0,2,1:T(8,128)(2,1)}), bf16[128,4,256]{0,2,1:T(8,128)(2,1)S(1)}, u32[]{:S(2)}, u32[]{:S(2)}) async-start(bf16[128,4,256]{0,2,1:T(8,128)(2,1)} %bitcast.36), calls=%async_computation.1 | async-start | bytes 524288 | tf_op jit(solution)/shard_map/all_to_all | solution.py:161
Sparse Core Ops, SparseCore 0:
  92.3 20.8 reduce-scatter.1
where the time goes:
time: 122 us
  blocking collectives  90.5 us (74%)
  between operations  14.2 us (12%)
  matrix products  5.87 us (5%)
  local copies, waits for them, and re-layouts  5.24 us (4%)
  starting transfers between devices  3.44 us (3%)
  other arithmetic  1.84 us (2%)
    all_gather x1, blocking collectives, per_device(): lax.all_gather(qkv_weight, 'seq', axis=0, tiled=True)  21.6 us
    all_gather x1, blocking collectives, per_device(): lax.all_gather(grad_qkv, 'seq', axis=0, tiled=True)  14.2 us
    all_gather x1, blocking collectives, per_device(): far_grads = lax.all_gather(grad_out, 'seq', axis=0, tiled=True)  13.3 us
    all_gather x1, blocking collectives, per_device(): panel = lax.all_gather(key_value, 'seq', axis=0, tiled=True)  12.8 us
    all_gather x1, blocking collectives, per_device(): far_queries = lax.all_gather(query_rows, 'seq', axis=0, tiled=True)  12.3 us
    all_gather x1, blocking collectives, per_device(): lax.all_gather(log_total_rows, 'seq', axis=0, tiled=True)  8.22 us
    all_gather x1, blocking collectives, per_device(): lax.all_gather(grad_dot_rows, 'seq', axis=0, tiled=True)  8.03 us
    unnamed x13, local copies, waits for them, and re-layouts  4.19 us
  transfers between devices with their start and end apart: 2, of which 1 were waited for; matrix products, arithmetic and copies ran while one was open for 2% of the time, Pallas kernels for 0%

commit v1 on v0

--- a/solution.py
+++ b/solution.py
@@ -1,13 +1,16 @@
+import functools
 import jax
 import jax.numpy as jnp
 from jax import lax
+from jax.experimental import pallas as pl
+from jax.experimental.pallas import tpu as pltpu
 from jax.sharding import PartitionSpec as P
 
 HD = 64
 BLOCK = 128
-
-
 MASKED_SCORE = -1e30
+BF = jnp.bfloat16
+F32 = jnp.float32
 
 
 def query_visible(covisible, block_drive, first_block, block_count):
@@ -29,7 +32,7 @@
     return (member[:, None] == lax.iota(jnp.int32, block_total)[None, :]).astype(jnp.float32)
 
 
-def per_device(tokens, qkv_weight, covisible, block_drive, grad_out):
+def general(tokens, qkv_weight, covisible, block_drive, grad_out):
     local_rows = tokens.shape[0]
     seq_count = lax.axis_size("seq")
     seq_index = lax.axis_index("seq")
@@ -41,35 +44,25 @@
     scaling = HD ** (-0.5)
     rows_visible = query_visible(covisible, block_drive, first_block, block_count)
     columns_visible = key_visible(covisible, block_drive, first_block, block_count)
-    inputs = tokens
-    projected = jnp.dot(
-        inputs,
-        lax.all_gather(qkv_weight, "seq", axis=0, tiled=True),
-        preferred_element_type=jnp.float32,
-    )
+    weight = lax.all_gather(qkv_weight, "seq", axis=0, tiled=True)
+    projected = jnp.dot(tokens, weight, preferred_element_type=jnp.float32)
     projected = projected.astype(jnp.bfloat16).reshape(local_rows, local_heads, 3, HD)
     queries = projected[:, :, 0, :]
     local_keys = projected[:, :, 1, :]
     local_values = projected[:, :, 2, :]
     key_value = projected[:, :, 1:, :].reshape(local_rows, local_heads * 2 * HD)
-
-    def local_visible(length):
-        onehot = block_onehot(length, block_total)
-        return (jnp.repeat(jnp.dot(rows_visible, onehot.T), BLOCK, axis=0) > 0.5)[None]
-
     panel = lax.all_gather(key_value, "seq", axis=0, tiled=True)
-    running_max = jnp.full((local_heads, local_rows), MASKED_SCORE, jnp.float32)
     length = panel.shape[0]
-    visible = local_visible(length)
+    onehot = block_onehot(length, block_total)
+    visible = (jnp.repeat(jnp.dot(rows_visible, onehot.T), BLOCK, axis=0) > 0.5)[None]
     split_panel = panel.reshape(length, local_heads, 2, HD)
+    panel_keys = split_panel[:, :, 0, :]
     scores = (
-        jnp.einsum(
-            "qhd,khd->hqk", queries, split_panel[:, :, 0, :], preferred_element_type=jnp.float32
-        )
+        jnp.einsum("qhd,khd->hqk", queries, panel_keys, preferred_element_type=jnp.float32)
         * scaling
     )
-    new_max = jnp.maximum(running_max, jnp.where(visible, scores, MASKED_SCORE).max(axis=2))
-    shifted = jnp.exp(jnp.where(visible, scores - new_max[:, :, None], MASKED_SCORE))
+    running_max = jnp.where(visible, scores, MASKED_SCORE).max(axis=2)
+    shifted = jnp.exp(jnp.where(visible, scores - running_max[:, :, None], MASKED_SCORE))
     running_sum = shifted.sum(axis=2)
     wide_values = split_panel[:, :, 1, :].astype(jnp.float32)
     weighted = jnp.einsum(
@@ -79,7 +72,6 @@
         precision=lax.Precision.HIGHEST,
         preferred_element_type=jnp.float32,
     )
-    running_max, running_sum, weighted = (new_max, running_sum, weighted)
     attention_heads = (weighted / running_sum[:, :, None]).astype(jnp.bfloat16)
     attention = jnp.transpose(attention_heads, (1, 0, 2)).reshape(local_rows, local_heads * HD)
     log_total = running_max + jnp.log(running_sum)
@@ -91,16 +83,12 @@
     )
     grad_dot = jnp.transpose(grad_dot_rows)
     log_total_rows = jnp.transpose(log_total)
-    all_log_total, all_grad_dot = (
-        lax.all_gather(log_total_rows, "seq", axis=0, tiled=True),
-        lax.all_gather(grad_dot_rows, "seq", axis=0, tiled=True),
-    )
+    all_log_total = lax.all_gather(log_total_rows, "seq", axis=0, tiled=True)
+    all_grad_dot = lax.all_gather(grad_dot_rows, "seq", axis=0, tiled=True)
     query_rows = queries.reshape(local_rows, local_heads * HD)
     far_queries = lax.all_gather(query_rows, "seq", axis=0, tiled=True)
     far_grads = lax.all_gather(grad_out, "seq", axis=0, tiled=True)
-    length = far_queries.shape[0]
-    onehot = block_onehot(length, block_total)
-    visible = (jnp.repeat(jnp.dot(onehot, columns_visible), BLOCK, axis=1) > 0.5)[None]
+    visible_columns = (jnp.repeat(jnp.dot(onehot, columns_visible), BLOCK, axis=1) > 0.5)[None]
     far_heads = far_queries.reshape(length, local_heads, HD)
     far_grad_heads = far_grads.reshape(length, local_heads, HD)
     far_log_total = jnp.transpose(all_log_total)
@@ -109,7 +97,9 @@
         jnp.einsum("qhd,khd->hqk", far_heads, local_keys, preferred_element_type=jnp.float32)
         * scaling
     )
-    probabilities = jnp.exp(jnp.where(visible, scores - far_log_total[:, :, None], MASKED_SCORE))
+    probabilities = jnp.exp(
+        jnp.where(visible_columns, scores - far_log_total[:, :, None], MASKED_SCORE)
+    )
     grad_prob = jnp.einsum(
         "qhd,khd->hqk", far_grad_heads, local_values, preferred_element_type=jnp.float32
     )
@@ -125,12 +115,6 @@
         far_grad_heads,
         preferred_element_type=jnp.float32,
     )
-    grad_keys, grad_values = (grad_keys, grad_values)
-    panel = lax.all_gather(key_value, "seq", axis=0, tiled=True)
-    length = panel.shape[0]
-    visible = local_visible(length)
-    split_panel = panel.reshape(length, local_heads, 2, HD)
-    panel_keys = split_panel[:, :, 0, :]
     scores = (
         jnp.einsum("qhd,khd->hqk", queries, panel_keys, preferred_element_type=jnp.float32)
         * scaling
@@ -149,25 +133,222 @@
         .reshape(local_rows, out_width)
     )
     partial_input = lax.dot_general(
-        grad_qkv,
-        lax.all_gather(qkv_weight, "seq", axis=0, tiled=True),
-        (((1,), (1,)), ((), ())),
-        preferred_element_type=jnp.float32,
+        grad_qkv, weight, (((1,), (1,)), ((), ())), preferred_element_type=jnp.float32
     )
     grad_input = lax.psum_scatter(partial_input, "fsdp", scatter_dimension=1, tiled=True).astype(
         jnp.bfloat16
     )
     token_scale = (local_rows * seq_count) ** (-0.5)
     column_tokens = lax.all_to_all(tokens, "seq", split_axis=1, concat_axis=0, tiled=True)
-    inputs = column_tokens
     summed_rows = lax.dot_general(
-        inputs,
+        column_tokens,
         lax.all_gather(grad_qkv, "seq", axis=0, tiled=True),
         (((0,), (0,)), ((), ())),
         preferred_element_type=jnp.float32,
     )
-    grad_weight = summed_rows * token_scale
-    return (attention, grad_input, grad_weight)
+    return (attention, grad_input, summed_rows * token_scale)
+
+
+def dot(a, b):
+    return lax.dot_general(a, b, (((1,), (0,)), ((), ())), preferred_element_type=F32)
+
+
+def dot_nt(a, b):
+    return lax.dot_general(a, b, (((1,), (1,)), ((), ())), preferred_element_type=F32)
+
+
+def heads_kernel(slots, refs_of, *refs):
+    named = dict(zip(refs_of, refs))
+    covis, drive = named["covis"], named["drive"]
+    t_all, w_all, gq = named["t_all"], named["w_all"], named["gq"]
+    rows = BLOCK
+    length = slots * rows
+    z = lax.axis_index("seq")
+    f = lax.axis_index("fsdp")
+    y = lax.axis_index("groups")
+    depth = w_all.shape[0] // slots
+    half = depth // 2
+    quarter = t_all.shape[1] // 4
+
+    t_all[0:rows, :] = named["t0"][...]
+    w_all[pl.ds(pl.multiple_of(z * depth, depth), depth), :] = named["w0"][...]
+    width = w_all.shape[1]
+    for k in range(1, slots):
+        block = named["r%d" % k]
+        first = (z ^ k) * depth
+        w_all[pl.ds(pl.multiple_of(first + y * half, half), half), :] = block[:, 0:width]
+        w_all[pl.ds(pl.multiple_of(first + (1 - y) * half, half), half), :] = named["v%d" % k][...]
+        here = pl.ds(k * rows, rows)
+        t_all[here, pl.ds(pl.multiple_of(f * quarter, quarter), quarter)] = block[
+            :, width : width + quarter
+        ]
+        for m in range(1, 4):
+            t_all[here, pl.ds(pl.multiple_of((f ^ m) * quarter, quarter), quarter)] = named[
+                "t%d_%d" % (k, m)
+            ][...]
+    grads = jnp.concatenate(
+        [named["g0"][...]] + [named["r%d" % k][:, width + quarter :] for k in range(1, slots)],
+        axis=0,
+    )
+    projected = dot(t_all[...], w_all[...]).astype(BF)
+    grads_t = jnp.transpose(grads)
+
+    bias = {}
+    for a in range(slots):
+        for b in range(slots):
+            i, j = z ^ a, z ^ b
+            seen = jnp.logical_or(covis[i, j] == 1, drive[i] == drive[j])
+            bias[a, b] = jnp.where(seen, 0.0, MASKED_SCORE).astype(F32)
+
+    heads = width // (3 * HD)
+    span = 2 * rows
+    out_columns = []
+    attention_t = []
+    for h in range(heads):
+        base = 3 * HD * h
+        q8 = projected[:, base : base + HD] * jnp.asarray(HD ** (-0.5), BF)
+        k_h = projected[:, base + HD : base + 2 * HD]
+        v_h = projected[:, base + 2 * HD : base + 3 * HD]
+        k_t = jnp.transpose(k_h)
+        v_t = jnp.transpose(v_h)
+        g_h = grads[:, HD * h : HD * (h + 1)]
+        g_t = grads_t[HD * h : HD * (h + 1), :]
+        d_k = jnp.zeros((length, HD), F32)
+        d_v = jnp.zeros((length, HD), F32)
+        d_q_t = []
+        for part in range(length // span):
+            at = slice(part * span, (part + 1) * span)
+            s_t = dot_nt(k_h, q8[at])
+            masked = []
+            for b in range(slots):
+                masked.append(
+                    jnp.concatenate(
+                        [
+                            s_t[b * rows : (b + 1) * rows, e * rows : (e + 1) * rows]
+                            + bias[part * 2 + e, b]
+                            for e in range(span // rows)
+                        ],
+                        axis=1,
+                    )
+                )
+            s_t = jnp.concatenate(masked, axis=0)
+            top = jnp.max(s_t, axis=0, keepdims=True)
+            e_t = jnp.exp(s_t - top)
+            total = jnp.sum(e_t, axis=0, keepdims=True)
+            p_t = e_t * (1.0 / total)
+            p_b = p_t.astype(BF)
+            p_rest = (p_t - p_b.astype(F32)).astype(BF)
+            o_t = (dot(v_t, p_b) + dot(v_t, p_rest)).astype(BF)
+            if part == 0:
+                attention_t.append(o_t[:, 0:rows])
+            grad_dot = jnp.sum(
+                g_t[:, at].astype(F32) * o_t.astype(F32), axis=0, keepdims=True
+            )
+            dp_t = dot_nt(v_h, g_h[at])
+            ds_t = (p_t * (dp_t - grad_dot)).astype(BF)
+            d_v = d_v + dot(p_b, g_h[at])
+            d_k = d_k + dot(ds_t, q8[at])
+            d_q_t.append(dot(k_t, ds_t))
+        d_q = jnp.transpose(jnp.concatenate(d_q_t, axis=1)) * (HD ** (-0.5))
+        out_columns += [d_q, d_k, d_v]
+    grad_qkv = jnp.concatenate(out_columns, axis=1).astype(BF)
+    gq[...] = grad_qkv
+    named["attention"][...] = jnp.transpose(jnp.concatenate(attention_t, axis=0))
+    own = grad_qkv[0:rows]
+    for m in range(4):
+        out = named["part%d" % m]
+        w_rows = w_all[pl.ds(pl.multiple_of((f ^ m) * depth, depth), depth), :]
+        out[...] = dot_nt(own, w_rows).astype(out.dtype)
+    named["t_d"][...] = t_all[:, pl.ds(pl.multiple_of(z * depth, depth), depth)]
+
+
+def short(tokens, qkv_weight, covisible, block_drive, grad_out):
+    rows, features = tokens.shape
+    slots = lax.axis_size("seq")
+    z = lax.axis_index("seq")
+    f = lax.axis_index("fsdp")
+    y = lax.axis_index("groups")
+    depth, width = qkv_weight.shape
+    quarter = features // 4
+    half = depth // 2
+
+    def swap(x, axis, bit):
+        n = lax.axis_size(axis)
+        return lax.ppermute(x, axis, [(i, i ^ bit) for i in range(n)])
+
+    packed = jnp.concatenate(
+        [
+            lax.dynamic_slice_in_dim(qkv_weight, y * half, half, 0),
+            lax.dynamic_slice_in_dim(tokens, f * quarter, quarter, 1),
+            grad_out,
+        ],
+        axis=1,
+    )
+    got = {}
+    got[2] = swap(packed, "seq", 2)
+    got[1] = swap(packed, "seq", 1)
+    got[3] = swap(got[2], "seq", 1)
+    names, values = ["covis", "drive", "t0", "w0", "g0"], []
+    values = [covisible, block_drive, tokens, qkv_weight, grad_out]
+    for k in (2, 1, 3):
+        piece = got[k][:, width : width + quarter]
+        far = swap(piece, "fsdp", 2)
+        names += ["r%d" % k, "v%d" % k, "t%d_1" % k, "t%d_2" % k, "t%d_3" % k]
+        values += [
+            got[k],
+            swap(got[k][:, :width], "groups", 1),
+            swap(piece, "fsdp", 1),
+            far,
+            swap(far, "fsdp", 1),
+        ]
+    outs = [
+        ("attention", (rows, grad_out.shape[1]), BF),
+        ("gq", (rows * slots, width), BF),
+        ("t_d", (rows * slots, depth), BF),
+        ("part0", (rows, depth), F32),
+        ("part1", (rows, depth), BF),
+        ("part2", (rows, depth), BF),
+        ("part3", (rows, depth), BF),
+    ]
+    scratch = [
+        ("t_all", pltpu.VMEM((rows * slots, features), BF)),
+        ("w_all", pltpu.VMEM((depth * slots, width), BF)),
+    ]
+    vmem = pl.BlockSpec(memory_space=pltpu.VMEM)
+    smem = pl.BlockSpec(memory_space=pltpu.SMEM)
+    refs_of = names + [n for n, _, _ in outs] + [n for n, _ in scratch]
+    attention, gq, t_d, *parts = pl.pallas_call(
+        functools.partial(heads_kernel, slots, refs_of),
+        out_shape=[jax.ShapeDtypeStruct(s, d) for _, s, d in outs],
+        in_specs=[smem, smem] + [vmem] * (len(names) - 2),
+        out_specs=[vmem] * len(outs),
+        scratch_shapes=[s for _, s in scratch],
+        compiler_params=pltpu.CompilerParams(vmem_limit_bytes=48 << 20),
+        name="heads",
+    )(*values)
+    total = parts[0]
+    for m in (1, 2, 3):
+        total = total + swap(parts[m], "fsdp", m).astype(F32)
+    grad_input = total.astype(BF)
+    grad_weight = lax.dot_general(
+        t_d, gq, (((0,), (0,)), ((), ())), preferred_element_type=F32
+    ) * ((rows * slots) ** (-0.5))
+    return attention, grad_input, grad_weight
+
+
+def per_device(tokens, qkv_weight, covisible, block_drive, grad_out):
+    rows, features = tokens.shape
+    depth = qkv_weight.shape[0]
+    fits = (
+        lax.axis_size("seq") == 4
+        and lax.axis_size("fsdp") == 4
+        and lax.axis_size("groups") == 2
+        and rows == BLOCK
+        and depth * 4 == features
+        and depth == 2 * rows
+    )
+    body = short if fits else general
+    return body(tokens, qkv_weight, covisible, block_drive, grad_out)
 
 
 def solution(mesh):

time: 122 us -> 42.4 us (0.35)
  blocking collectives: 90.5 us -> 0 us
  waiting for transfers between devices: 0.52 us -> 15 us
  starting transfers between devices: 3.44 us -> 16.9 us
  between operations: 14.2 us -> 0.74 us
  Pallas kernels: 0 us -> 5.97 us
  matrix products: 5.87 us -> 1.07 us
  local copies, waits for them, and re-layouts: 5.24 us -> 1.83 us
    all_gather x7 -> x0, blocking collectives: 90.5 us -> none  [the longest x1 21.6 us: per_device(): lax.all_gather(qkv_weight, 'seq', axis=0, tiled=True)]
    ppermute x0 -> x18, starting transfers between devices: none -> 16.9 us  [swap(): return lax.ppermute(x, axis, [(i, i ^ bit) for i in range(n)])]
    ppermute x0 -> x18, waiting for transfers between devices: none -> 15 us  [swap(): return lax.ppermute(x, axis, [(i, i ^ bit) for i in range(n)])]
    pallas_call x0 -> x1, Pallas kernels: none -> 5.97 us  [short(): pl.pallas_call(functools.partial(heads_kernel, slots, refs_of), out_shape...]
    dot_general x11 -> x1, matrix products: 5.87 us -> 1.07 us  [short(): lax.dot_general(t_d, gq, (((0,), (0,)), ((), ())), preferred_element_type...]
    unnamed x13 -> x10, local copies, waits for them, and re-layouts: 4.19 us -> 0.02 us
    all_to_all x1 -> x0, starting transfers between devices: 3.41 us -> none  [per_device(): lax.all_to_all(tokens, 'seq', split_axis=1, concat_axis=0, tiled=True)]
  transfers between devices with their start and end apart: 2 -> 18, of which waited for: 1 -> 9; matrix products, arithmetic and copies ran while one was open for 2% -> 3% of each run, Pallas kernels for 0% -> 0%
where the time goes in v1:
time: 42.4 us; the launch traced here: 42.2 us
  starting transfers between devices  16.9 us (40%)
  waiting for transfers between devices  15 us (35%)
  Pallas kernels  5.97 us (14%)
  local copies, waits for them, and re-layouts  1.83 us (4%)
  matrix products  1.07 us (3%)
  between operations  0.74 us (2%)
  other arithmetic  0.69 us (2%)
    ppermute x18, starting transfers between devices, swap(): return lax.ppermute(x, axis, [(i, i ^ bit) for i in range(n)])  16.9 us
    ppermute x18, waiting for transfers between devices, swap(): return lax.ppermute(x, axis, [(i, i ^ bit) for i in range(n)])  15 us
    pallas_call x1, Pallas kernels, short(): pl.pallas_call(functools.partial(heads_kernel, slots, refs_of), out_shape...  5.97 us
    dot_general x1, matrix products, short(): lax.dot_general(t_d, gq, (((0,), (0,)), ((), ())), preferred_element_type...  1.07 us
    dynamic_slice x1, local copies, waits for them, and re-layouts, short(): lax.dynamic_slice_in_dim(qkv_weight, y * half, half, 0)  0.91 us
    dynamic_slice x1, local copies, waits for them, and re-layouts, short(): lax.dynamic_slice_in_dim(tokens, f * quarter, quarter, 1)  0.85 us
  transfers between devices with their start and end apart: 18, of which 9 were waited for; matrix products, arithmetic and copies ran while one was open for 3% of the time, Pallas kernels for 0%

profile of v1, /device:TPU:0, one launch (start us, length us, event | category | flops | bytes accessed | tf_op | source)
XLA Modules:
  0.0 42.2 jit_solution(6031137641850675608)
XLA Ops:
  0.6 0.8 %constant_dynamic-slice_fusion = bf16[128,256]{1,0:T(8,128)(2,1)S(1)} fusion(bf16[128,1024]{1,0:T(8,128)(2,1)} %refs_2_.1, s32[]{:T(128)S(6)} %select_n.7), kind=kLoop, calls=%fused_computation.3 | loop fusion | bytes 131076 | tf_op jit(solution)/shard_map/dynamic_slice | solution.py:282
  1.5 0.0 copy-start.2
  1.5 0.9 %constant_dynamic-slice_fusion.1 = bf16[128,384]{1,0:T(8,128)(2,1)S(1)} fusion(bf16[256,384]{1,0:T(8,128)(2,1)} %refs_3_.1, s32[]{:T(128)S(6)} %select_n.6), kind=kLoop, calls=%fused_computation.4 | loop fusion | bytes 196612 | tf_op jit(solution)/shard_map/dynamic_slice | solution.py:281
  2.4 0.0 copy-done.2
  2.4 4.1 %collective-permute-start = (bf16[128,768]{1,0:T(8,128)(2,1)S(1)}, bf16[128,768]{1,0:T(8,128)(2,1)S(1)}, u32[]{:S(2)}, u32[]{:S(2)}) collective-permute-start(bf16[128,768]{1,0:T(8,128)(2,1)S(1)} %pad_maximum_fusion), channel_id=1, source_target_pairs={{0,8},{4,12},{8,0},{12,4},{1,9},{5,13},{9,1},{13,5},{2,10},{6,14},... | collective-permute-start | bytes 589832 | tf_op jit(solution)/shard_map/ppermute | solution.py:277
  6.5 1.6 %collective-permute-start.5 = (bf16[128,768]{1,0:T(8,128)(2,1)S(1)}, bf16[128,768]{1,0:T(8,128)(2,1)S(1)}, u32[]{:S(2)}, u32[]{:S(2)}) collective-permute-start(bf16[128,768]{1,0:T(8,128)(2,1)S(1)} %pad_maximum_fusion), channel_id=1, source_target_pairs={{0,4},{4,0},{8,12},{12,8},{1,5},{5,1},{9,13},{13,9},{2,6},{6,2},{1... | collective-permute-start | bytes 589832 | tf_op jit(solution)/shard_map/ppermute | solution.py:277
  8.1 7.6 %collective-permute-done.refs_5_ = bf16[128,768]{1,0:T(8,128)(2,1)S(1)} collective-permute-done((bf16[128,768]{1,0:T(8,128)(2,1)S(1)}, bf16[128,768]{1,0:T(8,128)(2,1)S(1)}, u32[]{:S(2)}, u32[]{:S(2)}) %collective-permute-start) | collective-permute-done | bytes 196640 | tf_op jit(solution)/shard_map/ppermute | solution.py:277
  15.8 0.6 %collective-permute-start.10 = (bf16[128,768]{1,0:T(8,128)(2,1)S(1)}, bf16[128,768]{1,0:T(8,128)(2,1)S(1)}, u32[]{:S(2)}, u32[]{:S(2)}) collective-permute-start(bf16[128,768]{1,0:T(8,128)(2,1)S(1)} %collective-permute-done.refs_5_), channel_id=1, source_target_pairs={{0,4},{4,0},{8,12},{12,8},{1,5},{5,1},{9,13},{13,9},{2,6},{6,2},{1... | collective-permute-start | bytes 589832 | tf_op jit(solution)/shard_map/ppermute | solution.py:277
  16.4 0.0 collective-permute-done.5.refs_10_
  16.4 1.6 %collective-permute-start.8 = (bf16[128,256]{1,0:T(8,128)(2,1)S(1)}, bf16[128,256]{1,0:T(8,128)(2,1)S(1)}, u32[]{:S(2)}, u32[]{:S(2)}) collective-permute-start(bf16[128,256]{1,0:T(8,128)(2,1)S(1)} %slice.27), channel_id=1, source_target_pairs={{0,2},{1,3},{2,0},{3,1},{4,6},{5,7},{6,4},{7,5},{8,10},{9,11},{10,... | collective-permute-start | bytes 196616 | tf_op jit(solution)/shard_map/ppermute | solution.py:277
  17.9 0.0 collective-permute-start.7
  18.0 1.6 %collective-permute-start.6 = (bf16[128,384]{1,0:T(8,128)(2,1)S(1)}, bf16[128,384]{1,0:T(8,128)(2,1)S(1)}, u32[]{:S(2)}, u32[]{:S(2)}) collective-permute-start(bf16[128,384]{1,0:T(8,128)(2,1)S(1)} %slice.26), channel_id=1, source_target_pairs={{0,16},{16,0},{1,17},{17,1},{2,18},{18,2},{3,19},{19,3},{4,20},{20... | collective-permute-start | bytes 294920 | tf_op jit(solution)/shard_map/ppermute | solution.py:277
  19.6 0.0 copy-start.1
  19.6 0.6 %collective-permute-start.1 = (bf16[128,384]{1,0:T(8,128)(2,1)S(1)}, bf16[128,384]{1,0:T(8,128)(2,1)S(1)}, u32[]{:S(2)}, u32[]{:S(2)}) collective-permute-start(bf16[128,384]{1,0:T(8,128)(2,1)S(1)} %slice.24), channel_id=1, source_target_pairs={{0,16},{16,0},{1,17},{17,1},{2,18},{18,2},{3,19},{19,3},{4,20},{20... | collective-permute-start | bytes 294920 | tf_op jit(solution)/shard_map/ppermute | solution.py:277
  20.1 0.0 copy-start
  20.1 0.6 %collective-permute-done.8.refs_13_ = bf16[128,256]{1,0:T(8,128)(2,1)S(1)} collective-permute-done((bf16[128,256]{1,0:T(8,128)(2,1)S(1)}, bf16[128,256]{1,0:T(8,128)(2,1)S(1)}, u32[]{:S(2)}, u32[]{:S(2)}) %collective-permute-start.8) | collective-permute-done | bytes 65568 | tf_op jit(solution)/shard_map/ppermute | solution.py:277
  20.7 1.5 %collective-permute-start.3 = (bf16[128,256]{1,0:T(8,128)(2,1)S(1)}, bf16[128,256]{1,0:T(8,128)(2,1)S(1)}, u32[]{:S(2)}, u32[]{:S(2)}) collective-permute-start(bf16[128,256]{1,0:T(8,128)(2,1)S(1)} %slice.25), channel_id=1, source_target_pairs={{0,2},{1,3},{2,0},{3,1},{4,6},{5,7},{6,4},{7,5},{8,10},{9,11},{10,... | collective-permute-start | bytes 196616 | tf_op jit(solution)/shard_map/ppermute | solution.py:277
  22.2 0.0 collective-permute-done.10.refs_15_
  22.2 0.0 collective-permute-start.2
  22.2 0.0 copy-start.3
  22.2 0.0 copy-start.4
  22.3 0.0 collective-permute-done.7.refs_12_
  22.3 0.8 %collective-permute-start.13 = (bf16[128,256]{1,0:T(8,128)(2,1)S(1)}, bf16[128,256]{1,0:T(8,128)(2,1)S(1)}, u32[]{:S(2)}, u32[]{:S(2)}) collective-permute-start(bf16[128,256]{1,0:T(8,128)(2,1)S(1)} %slice.29), channel_id=1, source_target_pairs={{0,2},{1,3},{2,0},{3,1},{4,6},{5,7},{6,4},{7,5},{8,10},{9,11},{10,... | collective-permute-start | bytes 196616 | tf_op jit(solution)/shard_map/ppermute | solution.py:277
  23.1 1.9 %collective-permute-done.3.refs_8_ = bf16[128,256]{1,0:T(8,128)(2,1)S(1)} collective-permute-done((bf16[128,256]{1,0:T(8,128)(2,1)S(1)}, bf16[128,256]{1,0:T(8,128)(2,1)S(1)}, u32[]{:S(2)}, u32[]{:S(2)}) %collective-permute-start.3) | collective-permute-done | bytes 65568 | tf_op jit(solution)/shard_map/ppermute | solution.py:277
  25.0 1.5 %collective-permute-start.11 = (bf16[128,384]{1,0:T(8,128)(2,1)S(1)}, bf16[128,384]{1,0:T(8,128)(2,1)S(1)}, u32[]{:S(2)}, u32[]{:S(2)}) collective-permute-start(bf16[128,384]{1,0:T(8,128)(2,1)S(1)} %slice.28), channel_id=1, source_target_pairs={{0,16},{16,0},{1,17},{17,1},{2,18},{18,2},{3,19},{19,3},{4,20},{20... | collective-permute-start | bytes 294920 | tf_op jit(solution)/shard_map/ppermute | solution.py:277
  26.5 0.0 collective-permute-done.2.refs_7_
  26.5 0.0 collective-permute-start.9
  26.5 0.0 collective-permute-done.6.refs_11_
  26.5 0.5 %collective-permute-start.4 = (bf16[128,256]{1,0:T(8,128)(2,1)S(1)}, bf16[128,256]{1,0:T(8,128)(2,1)S(1)}, u32[]{:S(2)}, u32[]{:S(2)}) collective-permute-start(bf16[128,256]{1,0:T(8,128)(2,1)S(1)} %collective-permute-done.3.refs_8_), channel_id=1, source_target_pairs={{0,1},{1,0},{2,3},{3,2},{4,5},{5,4},{6,7},{7,6},{8,9},{9,8},{10,11... | collective-permute-start | bytes 196616 | tf_op jit(solution)/shard_map/ppermute | solution.py:277
  27.0 0.0 collective-permute-done.1.refs_6_
  27.0 0.1 collective-permute-start.12
  27.1 0.0 collective-permute-done.13.refs_18_
  27.1 0.4 %collective-permute-start.14 = (bf16[128,256]{1,0:T(8,128)(2,1)S(1)}, bf16[128,256]{1,0:T(8,128)(2,1)S(1)}, u32[]{:S(2)}, u32[]{:S(2)}) collective-permute-start(bf16[128,256]{1,0:T(8,128)(2,1)S(1)} %collective-permute-done.13.refs_18_), channel_id=1, source_target_pairs={{0,1},{1,0},{2,3},{3,2},{4,5},{5,4},{6,7},{7,6},{8,9},{9,8},{10,11... | collective-permute-start | bytes 196616 | tf_op jit(solution)/shard_map/ppermute | solution.py:277
  27.5 0.2 collective-permute-done.9.refs_14_
  27.8 0.2 collective-permute-done.4.refs_9_
  27.9 0.4 collective-permute-done.12.refs_17_
  28.3 1.3 %collective-permute-done.11.refs_16_ = bf16[128,384]{1,0:T(8,128)(2,1)S(1)} collective-permute-done((bf16[128,384]{1,0:T(8,128)(2,1)S(1)}, bf16[128,384]{1,0:T(8,128)(2,1)S(1)}, u32[]{:S(2)}, u32[]{:S(2)}) %collective-permute-start.11) | collective-permute-done | bytes 98336 | tf_op jit(solution)/shard_map/ppermute | solution.py:277
  29.6 0.0 collective-permute-done.14.refs_19_
  29.6 0.0 copy-done.1
  29.6 0.0 copy-done
  29.6 0.0 copy-done.3
  29.6 0.0 copy-done.4
  29.6 6.0 %heads.1 = (bf16[128,128]{1,0:T(8,128)(2,1)}, bf16[512,384]{1,0:T(8,128)(2,1)S(1)}, bf16[512,256]{1,0:T(8,128)(2,1)S(1)}, f32[128,256]{1,0:T(8,128)S(1)}, bf16[1...) custom-call(s32[4,4]{1,0:T(4,128)S(1)} %copy-done.3, s32[4]{0:T(128)S(1)} %copy-done.4, ...), custom_call_target="tpu_custom_call" | custom-call | tf_op jit(solution)/shard_map/heads/pallas_call | solution.py:320
  35.6 0.0 collective-permute-start.15
  35.6 1.9 %collective-permute-start.16 = (bf16[128,256]{1,0:T(8,128)(2,1)S(1)}, bf16[128,256]{1,0:T(8,128)(2,1)S(1)}, u32[]{:S(2)}, u32[]{:S(2)}) collective-permute-start(bf16[128,256]{1,0:T(8,128)(2,1)S(1)} %get-tuple-element.13), channel_id=1, source_target_pairs={{0,2},{1,3},{2,0},{3,1},{4,6},{5,7},{6,4},{7,5},{8,10},{9,11},{10,... | collective-permute-start | bytes 196616 | tf_op jit(solution)/shard_map/ppermute | solution.py:277
  37.5 0.1 collective-permute-start.17
  37.6 1.1 %convolution_multiply_fusion = f32[256,384]{1,0:T(8,128)} fusion(bf16[512,256]{1,0:T(8,128)(2,1)S(1)} %get-tuple-element.15, bf16[512,384]{1,0:T(8,128)(2,1)S(1)} %get-tuple-element.16), kind=kOutput, calls=%fused_computation | convolution fusion | flops 100761600 | bytes 1048576 | tf_op jit(solution)/shard_map/dot_general | solution.py:333
  38.7 0.0 collective-permute-done.15
  38.7 1.5 %collective-permute-done.16 = bf16[128,256]{1,0:T(8,128)(2,1)S(1)} collective-permute-done((bf16[128,256]{1,0:T(8,128)(2,1)S(1)}, bf16[128,256]{1,0:T(8,128)(2,1)S(1)}, u32[]{:S(2)}, u32[]{:S(2)}) %collective-permute-start.16) | collective-permute-done | bytes 65568 | tf_op jit(solution)/shard_map/ppermute | solution.py:277
  40.2 1.3 %collective-permute-done.17 = bf16[128,256]{1,0:T(8,128)(2,1)S(1)} collective-permute-done((bf16[128,256]{1,0:T(8,128)(2,1)S(1)}, bf16[128,256]{1,0:T(8,128)(2,1)S(1)}, u32[]{:S(2)}, u32[]{:S(2)}) %collective-permute-start.17) | collective-permute-done | bytes 65568 | tf_op jit(solution)/shard_map/ppermute | solution.py:277
  41.6 0.7 %add_convert_fusion = bf16[128,256]{1,0:T(8,128)(2,1)} fusion(bf16[128,256]{1,0:T(8,128)(2,1)S(1)} %collective-permute-done.17, bf16[128,256]{1,0:T(8,128)(2,1)S(1)} %collective-permute-done.16, f32[128,256]{1,0:T(8,128)S(1)} %get-tuple-element.11, bf16[128,256]{1,0:T(8,128)(2,1)S(1)} %collective-permute-done.15), kind=kLoop, calls=%fused_computation.2 | loop fusion | flops 229376 | bytes 393216 | tf_op jit(solution)/shard_map/convert_element_type | solution.py:332
  (7 shorter events, 0.1 us)
Async XLA Ops:
  1.5 0.9 %copy-start.2 = (bf16[128,128]{1,0:T(8,128)(2,1)S(1)}, bf16[128,128]{1,0:T(8,128)(2,1)}, u32[]{:S(2)}) copy-start(bf16[128,128]{1,0:T(8,128)(2,1)} %refs_4_.1) | copy-start | bytes 98308
  2.4 13.3 %collective-permute-start = (bf16[128,768]{1,0:T(8,128)(2,1)S(1)}, bf16[128,768]{1,0:T(8,128)(2,1)S(1)}, u32[]{:S(2)}, u32[]{:S(2)}) collective-permute-start(bf16[128,768]{1,0:T(8,128)(2,1)S(1)} %pad_maximum_fusion), channel_id=1, source_target_pairs={{0,8},{4,12},{8,0},{12,4},{1,9},{5,13},{9,1},{13,5},{2,10},{6,14},... | collective-permute-start | bytes 589832 | tf_op jit(solution)/shard_map/ppermute | solution.py:277
  6.5 9.8 %collective-permute-start.5 = (bf16[128,768]{1,0:T(8,128)(2,1)S(1)}, bf16[128,768]{1,0:T(8,128)(2,1)S(1)}, u32[]{:S(2)}, u32[]{:S(2)}) collective-permute-start(bf16[128,768]{1,0:T(8,128)(2,1)S(1)} %pad_maximum_fusion), channel_id=1, source_target_pairs={{0,4},{4,0},{8,12},{12,8},{1,5},{5,1},{9,13},{13,9},{2,6},{6,2},{1... | collective-permute-start | bytes 589832 | tf_op jit(solution)/shard_map/ppermute | solution.py:277
  15.8 6.5 %collective-permute-start.10 = (bf16[128,768]{1,0:T(8,128)(2,1)S(1)}, bf16[128,768]{1,0:T(8,128)(2,1)S(1)}, u32[]{:S(2)}, u32[]{:S(2)}) collective-permute-start(bf16[128,768]{1,0:T(8,128)(2,1)S(1)} %collective-permute-done.refs_5_), channel_id=1, source_target_pairs={{0,4},{4,0},{8,12},{12,8},{1,5},{5,1},{9,13},{13,9},{2,6},{6,2},{1... | collective-permute-start | bytes 589832 | tf_op jit(solution)/shard_map/ppermute | solution.py:277
  16.4 4.3 %collective-permute-start.8 = (bf16[128,256]{1,0:T(8,128)(2,1)S(1)}, bf16[128,256]{1,0:T(8,128)(2,1)S(1)}, u32[]{:S(2)}, u32[]{:S(2)}) collective-permute-start(bf16[128,256]{1,0:T(8,128)(2,1)S(1)} %slice.27), channel_id=1, source_target_pairs={{0,2},{1,3},{2,0},{3,1},{4,6},{5,7},{6,4},{7,5},{8,10},{9,11},{10,... | collective-permute-start | bytes 196616 | tf_op jit(solution)/shard_map/ppermute | solution.py:277
  17.9 4.3 %collective-permute-start.7 = (bf16[128,256]{1,0:T(8,128)(2,1)S(1)}, bf16[128,256]{1,0:T(8,128)(2,1)S(1)}, u32[]{:S(2)}, u32[]{:S(2)}) collective-permute-start(bf16[128,256]{1,0:T(8,128)(2,1)S(1)} %slice.27), channel_id=1, source_target_pairs={{0,1},{1,0},{2,3},{3,2},{4,5},{5,4},{6,7},{7,6},{8,9},{9,8},{10,11... | collective-permute-start | bytes 196616 | tf_op jit(solution)/shard_map/ppermute | solution.py:277
  18.0 8.6 %collective-permute-start.6 = (bf16[128,384]{1,0:T(8,128)(2,1)S(1)}, bf16[128,384]{1,0:T(8,128)(2,1)S(1)}, u32[]{:S(2)}, u32[]{:S(2)}) collective-permute-start(bf16[128,384]{1,0:T(8,128)(2,1)S(1)} %slice.26), channel_id=1, source_target_pairs={{0,16},{16,0},{1,17},{17,1},{2,18},{18,2},{3,19},{19,3},{4,20},{20... | collective-permute-start | bytes 294920 | tf_op jit(solution)/shard_map/ppermute | solution.py:277
  19.6 10.1 %copy-start.1 = (bf16[128,1024]{1,0:T(8,128)(2,1)S(1)}, bf16[128,1024]{1,0:T(8,128)(2,1)}, u32[]{:S(2)}) copy-start(bf16[128,1024]{1,0:T(8,128)(2,1)} %refs_2_.1) | copy-start | bytes 786436
  19.6 7.5 %collective-permute-start.1 = (bf16[128,384]{1,0:T(8,128)(2,1)S(1)}, bf16[128,384]{1,0:T(8,128)(2,1)S(1)}, u32[]{:S(2)}, u32[]{:S(2)}) collective-permute-start(bf16[128,384]{1,0:T(8,128)(2,1)S(1)} %slice.24), channel_id=1, source_target_pairs={{0,16},{16,0},{1,17},{17,1},{2,18},{18,2},{3,19},{19,3},{4,20},{20... | collective-permute-start | bytes 294920 | tf_op jit(solution)/shard_map/ppermute | solution.py:277
  20.1 9.5 %copy-start = (bf16[256,384]{1,0:T(8,128)(2,1)S(1)}, bf16[256,384]{1,0:T(8,128)(2,1)}, u32[]{:S(2)}) copy-start(bf16[256,384]{1,0:T(8,128)(2,1)} %refs_3_.1) | copy-start | bytes 589828
  20.7 4.3 %collective-permute-start.3 = (bf16[128,256]{1,0:T(8,128)(2,1)S(1)}, bf16[128,256]{1,0:T(8,128)(2,1)S(1)}, u32[]{:S(2)}, u32[]{:S(2)}) collective-permute-start(bf16[128,256]{1,0:T(8,128)(2,1)S(1)} %slice.25), channel_id=1, source_target_pairs={{0,2},{1,3},{2,0},{3,1},{4,6},{5,7},{6,4},{7,5},{8,10},{9,11},{10,... | collective-permute-start | bytes 196616 | tf_op jit(solution)/shard_map/ppermute | solution.py:277
  22.2 4.3 %collective-permute-start.2 = (bf16[128,256]{1,0:T(8,128)(2,1)S(1)}, bf16[128,256]{1,0:T(8,128)(2,1)S(1)}, u32[]{:S(2)}, u32[]{:S(2)}) collective-permute-start(bf16[128,256]{1,0:T(8,128)(2,1)S(1)} %slice.25), channel_id=1, source_target_pairs={{0,1},{1,0},{2,3},{3,2},{4,5},{5,4},{6,7},{7,6},{8,9},{9,8},{10,11... | collective-permute-start | bytes 196616 | tf_op jit(solution)/shard_map/ppermute | solution.py:277
  22.2 7.4 %copy-start.3 = (s32[4,4]{1,0:T(4,128)S(1)}, s32[4,4]{1,0:T(4,128)}, u32[]{:S(2)}) copy-start(s32[4,4]{1,0:T(4,128)} %refs_0_.1) | copy-start | bytes 196
  22.2 7.4 %copy-start.4 = (s32[4]{0:T(128)S(1)}, s32[4]{0:T(128)}, u32[]{:S(2)}) copy-start(s32[4]{0:T(128)} %refs_1_.1) | copy-start | bytes 52
  22.3 4.8 %collective-permute-start.13 = (bf16[128,256]{1,0:T(8,128)(2,1)S(1)}, bf16[128,256]{1,0:T(8,128)(2,1)S(1)}, u32[]{:S(2)}, u32[]{:S(2)}) collective-permute-start(bf16[128,256]{1,0:T(8,128)(2,1)S(1)} %slice.29), channel_id=1, source_target_pairs={{0,2},{1,3},{2,0},{3,1},{4,6},{5,7},{6,4},{7,5},{8,10},{9,11},{10,... | collective-permute-start | bytes 196616 | tf_op jit(solution)/shard_map/ppermute | solution.py:277
  25.0 4.6 %collective-permute-start.11 = (bf16[128,384]{1,0:T(8,128)(2,1)S(1)}, bf16[128,384]{1,0:T(8,128)(2,1)S(1)}, u32[]{:S(2)}, u32[]{:S(2)}) collective-permute-start(bf16[128,384]{1,0:T(8,128)(2,1)S(1)} %slice.28), channel_id=1, source_target_pairs={{0,16},{16,0},{1,17},{17,1},{2,18},{18,2},{3,19},{19,3},{4,20},{20... | collective-permute-start | bytes 294920 | tf_op jit(solution)/shard_map/ppermute | solution.py:277
  26.5 1.3 %collective-permute-start.9 = (bf16[128,256]{1,0:T(8,128)(2,1)S(1)}, bf16[128,256]{1,0:T(8,128)(2,1)S(1)}, u32[]{:S(2)}, u32[]{:S(2)}) collective-permute-start(bf16[128,256]{1,0:T(8,128)(2,1)S(1)} %collective-permute-done.8.refs_13_), channel_id=1, source_target_pairs={{0,1},{1,0},{2,3},{3,2},{4,5},{5,4},{6,7},{7,6},{8,9},{9,8},{10,11... | collective-permute-start | bytes 196616 | tf_op jit(solution)/shard_map/ppermute | solution.py:277
  26.5 1.4 %collective-permute-start.4 = (bf16[128,256]{1,0:T(8,128)(2,1)S(1)}, bf16[128,256]{1,0:T(8,128)(2,1)S(1)}, u32[]{:S(2)}, u32[]{:S(2)}) collective-permute-start(bf16[128,256]{1,0:T(8,128)(2,1)S(1)} %collective-permute-done.3.refs_8_), channel_id=1, source_target_pairs={{0,1},{1,0},{2,3},{3,2},{4,5},{5,4},{6,7},{7,6},{8,9},{9,8},{10,11... | collective-permute-start | bytes 196616 | tf_op jit(solution)/shard_map/ppermute | solution.py:277
  27.0 1.3 %collective-permute-start.12 = (bf16[128,256]{1,0:T(8,128)(2,1)S(1)}, bf16[128,256]{1,0:T(8,128)(2,1)S(1)}, u32[]{:S(2)}, u32[]{:S(2)}) collective-permute-start(bf16[128,256]{1,0:T(8,128)(2,1)S(1)} %slice.29), channel_id=1, source_target_pairs={{0,1},{1,0},{2,3},{3,2},{4,5},{5,4},{6,7},{7,6},{8,9},{9,8},{10,11... | collective-permute-start | bytes 196616 | tf_op jit(solution)/shard_map/ppermute | solution.py:277
  27.1 2.5 %collective-permute-start.14 = (bf16[128,256]{1,0:T(8,128)(2,1)S(1)}, bf16[128,256]{1,0:T(8,128)(2,1)S(1)}, u32[]{:S(2)}, u32[]{:S(2)}) collective-permute-start(bf16[128,256]{1,0:T(8,128)(2,1)S(1)} %collective-permute-done.13.refs_18_), channel_id=1, source_target_pairs={{0,1},{1,0},{2,3},{3,2},{4,5},{5,4},{6,7},{7,6},{8,9},{9,8},{10,11... | collective-permute-start | bytes 196616 | tf_op jit(solution)/shard_map/ppermute | solution.py:277
  35.6 3.1 %collective-permute-start.15 = (bf16[128,256]{1,0:T(8,128)(2,1)S(1)}, bf16[128,256]{1,0:T(8,128)(2,1)S(1)}, u32[]{:S(2)}, u32[]{:S(2)}) collective-permute-start(bf16[128,256]{1,0:T(8,128)(2,1)S(1)} %get-tuple-element.12), channel_id=1, source_target_pairs={{0,1},{1,0},{2,3},{3,2},{4,5},{5,4},{6,7},{7,6},{8,9},{9,8},{10,11... | collective-permute-start | bytes 196616 | tf_op jit(solution)/shard_map/ppermute | solution.py:277
  35.6 4.6 %collective-permute-start.16 = (bf16[128,256]{1,0:T(8,128)(2,1)S(1)}, bf16[128,256]{1,0:T(8,128)(2,1)S(1)}, u32[]{:S(2)}, u32[]{:S(2)}) collective-permute-start(bf16[128,256]{1,0:T(8,128)(2,1)S(1)} %get-tuple-element.13), channel_id=1, source_target_pairs={{0,2},{1,3},{2,0},{3,1},{4,6},{5,7},{6,4},{7,5},{8,10},{9,11},{10,... | collective-permute-start | bytes 196616 | tf_op jit(solution)/shard_map/ppermute | solution.py:277
  37.5 4.1 %collective-permute-start.17 = (bf16[128,256]{1,0:T(8,128)(2,1)S(1)}, bf16[128,256]{1,0:T(8,128)(2,1)S(1)}, u32[]{:S(2)}, u32[]{:S(2)}) collective-permute-start(bf16[128,256]{1,0:T(8,128)(2,1)S(1)} %get-tuple-element.14), channel_id=1, source_target_pairs={{0,3},{1,2},{2,1},{3,0},{4,7},{5,6},{6,5},{7,4},{8,11},{9,10},{10,... | collective-permute-start | bytes 196616 | tf_op jit(solution)/shard_map/ppermute | solution.py:277

commit v2 on v1

--- a/solution.py
+++ b/solution.py
@@ -157,7 +157,7 @@
     return lax.dot_general(a, b, (((1,), (1,)), ((), ())), preferred_element_type=F32)
 
 
-def heads_kernel(slots, refs_of, *refs):
+def heads_kernel(slots, refs_of, where, *refs):
     named = dict(zip(refs_of, refs))
     covis, drive = named["covis"], named["drive"]
     t_all, w_all, gq = named["t_all"], named["w_all"], named["gq"]
@@ -173,23 +173,24 @@
     t_all[0:rows, :] = named["t0"][...]
     w_all[pl.ds(pl.multiple_of(z * depth, depth), depth), :] = named["w0"][...]
     width = w_all.shape[1]
+    grads = [named["g0"][...]]
     for k in range(1, slots):
-        block = named["r%d" % k]
+        name, at = where[k, "r"]
+        r = named[name].at[pl.ds(at, rows), :]
+        name, at = where[k, "v"]
+        v = named[name].at[pl.ds(at, rows), :]
         first = (z ^ k) * depth
-        w_all[pl.ds(pl.multiple_of(first + y * half, half), half), :] = block[:, 0:width]
-        w_all[pl.ds(pl.multiple_of(first + (1 - y) * half, half), half), :] = named["v%d" % k][...]
-        here = pl.ds(k * rows, rows)
-        t_all[here, pl.ds(pl.multiple_of(f * quarter, quarter), quarter)] = block[
-            :, width : width + quarter
-        ]
+        w_all[pl.ds(pl.multiple_of(first + y * half, half), half), :] = r[:, 0:width]
+        w_all[pl.ds(pl.multiple_of(first + (1 - y) * half, half), half), :] = v[...]
+        pieces = [r[:, width : width + quarter]]
         for m in range(1, 4):
-            t_all[here, pl.ds(pl.multiple_of((f ^ m) * quarter, quarter), quarter)] = named[
-                "t%d_%d" % (k, m)
-            ][...]
-    grads = jnp.concatenate(
-        [named["g0"][...]] + [named["r%d" % k][:, width + quarter :] for k in range(1, slots)],
-        axis=0,
-    )
+            name, at = where[k, m]
+            pieces.append(named[name][pl.ds(at, rows), :])
+        for m, piece in enumerate(pieces):
+            columns = pl.ds(pl.multiple_of((f ^ m) * quarter, quarter), quarter)
+            t_all[pl.ds(k * rows, rows), columns] = piece
+        grads.append(r[:, width + quarter :])
+    grads = jnp.concatenate(grads, axis=0)
     projected = dot(t_all[...], w_all[...]).astype(BF)
     grads_t = jnp.transpose(grads)
 
@@ -201,7 +202,7 @@
             bias[a, b] = jnp.where(seen, 0.0, MASKED_SCORE).astype(F32)
 
     heads = width // (3 * HD)
-    span = 2 * rows
+    span = 4 * rows
     out_columns = []
     attention_t = []
     for h in range(heads):
@@ -225,7 +226,7 @@
                     jnp.concatenate(
                         [
                             s_t[b * rows : (b + 1) * rows, e * rows : (e + 1) * rows]
-                            + bias[part * 2 + e, b]
+                            + bias[part * (span // rows) + e, b]
                             for e in range(span // rows)
                         ],
                         axis=1,
@@ -262,6 +263,45 @@
     named["t_d"][...] = t_all[:, pl.ds(pl.multiple_of(z * depth, depth), depth)]
 
 
+def pack_kernel(w_ref, t_ref, g_ref, out, sems):
+    half, width = out.shape[0], w_ref.shape[1]
+    quarter = t_ref.shape[1] // 4
+    y = lax.axis_index("groups")
+    f = lax.axis_index("fsdp")
+    copies = [
+        pltpu.make_async_copy(
+            w_ref.at[pl.ds(pl.multiple_of(y * half, half), half), :],
+            out.at[:, pl.ds(0, width)],
+            sems.at[0],
+        ),
+        pltpu.make_async_copy(
+            t_ref.at[:, pl.ds(pl.multiple_of(f * quarter, quarter), quarter)],
+            out.at[:, pl.ds(width, quarter)],
+            sems.at[1],
+        ),
+        pltpu.make_async_copy(
+            g_ref, out.at[:, pl.ds(width + quarter, g_ref.shape[1])], sems.at[2]
+        ),
+    ]
+    for copy in copies:
+        copy.start()
+    for copy in copies:
+        copy.wait()
+
+
+def pack(tokens, qkv_weight, grad_out):
+    rows, features = tokens.shape
+    columns = qkv_weight.shape[1] + features // 4 + grad_out.shape[1]
+    return pl.pallas_call(
+        pack_kernel,
+        out_shape=pltpu.VMEM((rows, columns), BF),
+        in_specs=[pl.BlockSpec(memory_space=pl.ANY)] * 3,
+        out_specs=pl.BlockSpec(memory_space=pltpu.VMEM),
+        scratch_shapes=[pltpu.SemaphoreType.DMA((3,))],
+        name="pack",
+    )(qkv_weight, tokens, grad_out)
+
+
 def short(tokens, qkv_weight, covisible, block_drive, grad_out):
     rows, features = tokens.shape
     slots = lax.axis_size("seq")
@@ -276,31 +316,30 @@
         n = lax.axis_size(axis)
         return lax.ppermute(x, axis, [(i, i ^ bit) for i in range(n)])
 
-    packed = jnp.concatenate(
-        [
-            lax.dynamic_slice_in_dim(qkv_weight, y * half, half, 0),
-            lax.dynamic_slice_in_dim(tokens, f * quarter, quarter, 1),
-            grad_out,
-        ],
-        axis=1,
-    )
-    got = {}
-    got[2] = swap(packed, "seq", 2)
-    got[1] = swap(packed, "seq", 1)
-    got[3] = swap(got[2], "seq", 1)
-    names, values = ["covis", "drive", "t0", "w0", "g0"], []
-    values = [covisible, block_drive, tokens, qkv_weight, grad_out]
-    for k in (2, 1, 3):
-        piece = got[k][:, width : width + quarter]
-        far = swap(piece, "fsdp", 2)
-        names += ["r%d" % k, "v%d" % k, "t%d_1" % k, "t%d_2" % k, "t%d_3" % k]
-        values += [
-            got[k],
-            swap(got[k][:, :width], "groups", 1),
-            swap(piece, "fsdp", 1),
-            far,
-            swap(far, "fsdp", 1),
-        ]
+    packed = pack(tokens, qkv_weight, grad_out)
+    got2 = swap(packed, "seq", 2)
+    got1 = swap(packed, "seq", 1)
+    got3 = swap(got2, "seq", 1)
+    near = jnp.concatenate([got1, got2], axis=0)
+    piece12 = near[:, width : width + quarter]
+    piece3 = got3[:, width : width + quarter]
+    x3 = swap(piece3, "fsdp", 2)
+    v12 = swap(near[:, :width], "groups", 1)
+    c3 = swap(piece3, "fsdp", 1)
+    v3 = swap(got3[:, :width], "groups", 1)
+    x12 = swap(piece12, "fsdp", 2)
+    d3 = swap(piece3, "fsdp", 3)
+    c12 = swap(piece12, "fsdp", 1)
+    d12 = swap(piece12, "fsdp", 3)
+    moved = dict(d12=d12, near=near, c3=c3, x3=x3, d3=d3, c12=c12, v3=v3, x12=x12, v12=v12, got3=got3)
+    where = {}
+    for k, at in ((1, 0), (2, rows)):
+        where.update({(k, "r"): ("near", at), (k, "v"): ("v12", at)})
+        where.update({(k, 1): ("c12", at), (k, 2): ("x12", at), (k, 3): ("d12", at)})
+    where.update({(3, "r"): ("got3", 0), (3, "v"): ("v3", 0)})
+    where.update({(3, 1): ("c3", 0), (3, 2): ("x3", 0), (3, 3): ("d3", 0)})
+    names = ["covis", "drive", "t0", "w0", "g0"] + list(moved)
+    values = [covisible, block_drive, tokens, qkv_weight, grad_out] + list(moved.values())
     outs = [
         ("attention", (rows, grad_out.shape[1]), BF),
         ("gq", (rows * slots, width), BF),
@@ -318,8 +357,8 @@
     smem = pl.BlockSpec(memory_space=pltpu.SMEM)
     refs_of = names + [n for n, _, _ in outs] + [n for n, _ in scratch]
     attention, gq, t_d, *parts = pl.pallas_call(
-        functools.partial(heads_kernel, slots, refs_of),
-        out_shape=[jax.ShapeDtypeStruct(s, d) for _, s, d in outs],
+        functools.partial(heads_kernel, slots, refs_of, where),
+        out_shape=[pltpu.VMEM(s, d) for _, s, d in outs],
         in_specs=[smem, smem] + [vmem] * (len(names) - 2),
         out_specs=[vmem] * len(outs),
         scratch_shapes=[s for _, s in scratch],

time: 42.4 us -> 38.9 us (0.917)
  starting transfers between devices: 16.9 us -> 15.1 us
  local copies, waits for them, and re-layouts: 1.83 us -> 0.72 us
  Pallas kernels: 5.97 us -> 5.27 us
    ppermute x18 -> x14, starting transfers between devices: 16.9 us -> 15.1 us  [swap(): return lax.ppermute(x, axis, [(i, i ^ bit) for i in range(n)])]
    dynamic_slice x2 -> x0, local copies, waits for them, and re-layouts: 1.76 us -> none  [the longest x1 0.91 us: short(): lax.dynamic_slice_in_dim(qkv_weight, y * half, half, 0)]
    pallas_call x1 -> x2, Pallas kernels: 5.97 us -> 5.27 us  [the longest x1 4.33 us: short(): pl.pallas_call(functools.partial(heads_kernel, slots, refs_of, where), ou...]
    unnamed x10 -> x12, local copies, waits for them, and re-layouts: 0.02 us -> 0.66 us
    ppermute x18 -> x14, waiting for transfers between devices: 15 us -> 15.1 us  [swap(): return lax.ppermute(x, axis, [(i, i ^ bit) for i in range(n)])]
  transfers between devices with their start and end apart: 18 -> 14, of which waited for: 9 -> 8; matrix products, arithmetic and copies ran while one was open for 3% -> 5% of each run, Pallas kernels for 0% -> 0%
where the time goes in v2:
time: 38.9 us; the launch traced here: 38.7 us
  starting transfers between devices  15.1 us (39%)
  waiting for transfers between devices  15.1 us (39%)
  Pallas kernels  5.27 us (14%)
  matrix products  1.07 us (3%)
  between operations  0.77 us (2%)
  local copies, waits for them, and re-layouts  0.72 us (2%)
  other arithmetic  0.66 us (2%)
    ppermute x14, waiting for transfers between devices, swap(): return lax.ppermute(x, axis, [(i, i ^ bit) for i in range(n)])  15.1 us
    ppermute x14, starting transfers between devices, swap(): return lax.ppermute(x, axis, [(i, i ^ bit) for i in range(n)])  15.1 us
    pallas_call x1, Pallas kernels, short(): pl.pallas_call(functools.partial(heads_kernel, slots, refs_of, where), ou...  4.33 us
    dot_general x1, matrix products, short(): lax.dot_general(t_d, gq, (((0,), (0,)), ((), ())), preferred_element_type...  1.07 us
    pallas_call x1, Pallas kernels, pack(): pl.pallas_call(pack_kernel, out_shape=pltpu.VMEM((rows, columns), BF), in...  0.94 us
  transfers between devices with their start and end apart: 14, of which 8 were waited for; matrix products, arithmetic and copies ran while one was open for 5% of the time, Pallas kernels for 0%

profile of v2, /device:TPU:0, one launch (start us, length us, event | category | flops | bytes accessed | tf_op | source)
XLA Modules:
  0.0 38.7 jit_solution(7531748387801141045)
XLA Ops:
  0.6 0.9 %pack.1 = bf16[128,768]{1,0:T(8,128)(2,1)S(1)} custom-call(bf16[256,384]{1,0:T(8,128)(2,1)} %refs_3_.1, bf16[128,1024]{1,0:T(8,128)(2,1)} %refs_2_.1, bf16[128,128]{1,0:T(8,128)(2,1)} %refs_4_.1), custom_call_target="tpu_custom_call" | custom-call | tf_op jit(solution)/shard_map/pack/pallas_call | solution.py:295
  1.6 4.1 %collective-permute-start.1 = (bf16[128,768]{1,0:T(8,128)(2,1)S(1)}, bf16[128,768]{1,0:T(8,128)(2,1)S(1)}, u32[]{:S(2)}, u32[]{:S(2)}) collective-permute-start(bf16[128,768]{1,0:T(8,128)(2,1)S(1)} %pack.1), channel_id=1, source_target_pairs={{0,8},{4,12},{8,0},{12,4},{1,9},{5,13},{9,1},{13,5},{2,10},{6,14},... | collective-permute-start | bytes 589832 | tf_op jit(solution)/shard_map/ppermute | solution.py:317
  5.7 1.6 %collective-permute-start = (bf16[128,768]{1,0:T(8,128)(2,1)S(1)}, bf16[128,768]{1,0:T(8,128)(2,1)S(1)}, u32[]{:S(2)}, u32[]{:S(2)}) collective-permute-start(bf16[128,768]{1,0:T(8,128)(2,1)S(1)} %pack.1), channel_id=1, source_target_pairs={{0,4},{4,0},{8,12},{12,8},{1,5},{5,1},{9,13},{13,9},{2,6},{6,2},{1... | collective-permute-start | bytes 589832 | tf_op jit(solution)/shard_map/ppermute | solution.py:317
  7.3 7.6 %collective-permute-done.1 = bf16[128,768]{1,0:T(8,128)(2,1)S(1)} collective-permute-done((bf16[128,768]{1,0:T(8,128)(2,1)S(1)}, bf16[128,768]{1,0:T(8,128)(2,1)S(1)}, u32[]{:S(2)}, u32[]{:S(2)}) %collective-permute-start.1) | collective-permute-done | bytes 196640 | tf_op jit(solution)/shard_map/ppermute | solution.py:317
  14.9 0.6 %collective-permute-start.3 = (bf16[128,768]{1,0:T(8,128)(2,1)S(1)}, bf16[128,768]{1,0:T(8,128)(2,1)S(1)}, u32[]{:S(2)}, u32[]{:S(2)}) collective-permute-start(bf16[128,768]{1,0:T(8,128)(2,1)S(1)} %collective-permute-done.1), channel_id=1, source_target_pairs={{0,4},{4,0},{8,12},{12,8},{1,5},{5,1},{9,13},{13,9},{2,6},{6,2},{1... | collective-permute-start | bytes 589832 | tf_op jit(solution)/shard_map/ppermute | solution.py:317
  15.5 0.0 collective-permute-done
  15.6 1.6 %collective-permute-start.9 = (bf16[256,256]{1,0:T(8,128)(2,1)S(1)}, bf16[256,256]{1,0:T(8,128)(2,1)S(1)}, u32[]{:S(2)}, u32[]{:S(2)}) collective-permute-start(bf16[256,256]{1,0:T(8,128)(2,1)S(1)} %slice.16), channel_id=1, source_target_pairs={{0,2},{1,3},{2,0},{3,1},{4,6},{5,7},{6,4},{7,5},{8,10},{9,11},{10,... | collective-permute-start | bytes 393224 | tf_op jit(solution)/shard_map/ppermute | solution.py:317
  17.1 0.0 collective-permute-start.7
  17.1 0.0 copy-start.1
  17.2 0.0 copy-start
  17.2 1.6 %collective-permute-start.10 = (bf16[256,384]{1,0:T(8,128)(2,1)S(1)}, bf16[256,384]{1,0:T(8,128)(2,1)S(1)}, u32[]{:S(2)}, u32[]{:S(2)}) collective-permute-start(bf16[256,384]{1,0:T(8,128)(2,1)S(1)} %slice.19), channel_id=1, source_target_pairs={{0,16},{16,0},{1,17},{17,1},{2,18},{18,2},{3,19},{19,3},{4,20},{20... | collective-permute-start | bytes 589832 | tf_op jit(solution)/shard_map/ppermute | solution.py:317
  18.8 0.4 collective-permute-start.2
  19.1 1.8 %collective-permute-done.3.refs_14_ = bf16[128,768]{1,0:T(8,128)(2,1)S(1)} collective-permute-done((bf16[128,768]{1,0:T(8,128)(2,1)S(1)}, bf16[128,768]{1,0:T(8,128)(2,1)S(1)}, u32[]{:S(2)}, u32[]{:S(2)}) %collective-permute-start.3) | collective-permute-done | bytes 196640 | tf_op jit(solution)/shard_map/ppermute | solution.py:317
  20.9 0.0 copy-start.2
  20.9 0.0 copy-start.3
  21.0 0.0 copy-start.4
  21.0 1.3 %collective-permute-start.8 = (bf16[128,384]{1,0:T(8,128)(2,1)S(1)}, bf16[128,384]{1,0:T(8,128)(2,1)S(1)}, u32[]{:S(2)}, u32[]{:S(2)}) collective-permute-start(bf16[128,384]{1,0:T(8,128)(2,1)S(1)} %slice.18), channel_id=1, source_target_pairs={{0,16},{16,0},{1,17},{17,1},{2,18},{18,2},{3,19},{19,3},{4,20},{20... | collective-permute-start | bytes 294920 | tf_op jit(solution)/shard_map/ppermute | solution.py:317
  22.3 0.0 collective-permute-done.9.refs_12_
  22.3 0.1 collective-permute-start.6
  22.4 0.0 collective-permute-done.7.refs_10_
  22.4 1.6 %collective-permute-start.5 = (bf16[128,256]{1,0:T(8,128)(2,1)S(1)}, bf16[128,256]{1,0:T(8,128)(2,1)S(1)}, u32[]{:S(2)}, u32[]{:S(2)}) collective-permute-start(bf16[128,256]{1,0:T(8,128)(2,1)S(1)} %slice.17), channel_id=1, source_target_pairs={{0,2},{1,3},{2,0},{3,1},{4,6},{5,7},{6,4},{7,5},{8,10},{9,11},{10,... | collective-permute-start | bytes 196616 | tf_op jit(solution)/shard_map/ppermute | solution.py:317
  23.9 0.3 collective-permute-done.2.refs_5_
  24.2 0.4 %collective-permute-start.4 = (bf16[128,256]{1,0:T(8,128)(2,1)S(1)}, bf16[128,256]{1,0:T(8,128)(2,1)S(1)}, u32[]{:S(2)}, u32[]{:S(2)}) collective-permute-start(bf16[128,256]{1,0:T(8,128)(2,1)S(1)} %slice.17), channel_id=1, source_target_pairs={{0,1},{1,0},{2,3},{3,2},{4,5},{5,4},{6,7},{7,6},{8,9},{9,8},{10,11... | collective-permute-start | bytes 196616 | tf_op jit(solution)/shard_map/ppermute | solution.py:317
  24.7 0.3 collective-permute-done.10.refs_13_
  24.9 1.8 %collective-permute-done.6.refs_9_ = bf16[128,256]{1,0:T(8,128)(2,1)S(1)} collective-permute-done((bf16[128,256]{1,0:T(8,128)(2,1)S(1)}, bf16[128,256]{1,0:T(8,128)(2,1)S(1)}, u32[]{:S(2)}, u32[]{:S(2)}) %collective-permute-start.6) | collective-permute-done | bytes 65568 | tf_op jit(solution)/shard_map/ppermute | solution.py:317
  26.7 1.5 %collective-permute-done.5.refs_8_ = bf16[128,256]{1,0:T(8,128)(2,1)S(1)} collective-permute-done((bf16[128,256]{1,0:T(8,128)(2,1)S(1)}, bf16[128,256]{1,0:T(8,128)(2,1)S(1)}, u32[]{:S(2)}, u32[]{:S(2)}) %collective-permute-start.5) | collective-permute-done | bytes 65568 | tf_op jit(solution)/shard_map/ppermute | solution.py:317
  28.1 0.0 collective-permute-done.4.refs_7_
  28.1 0.0 collective-permute-done.8.refs_11_
  28.1 0.0 copy-done.1
  28.2 0.0 copy-done
  28.2 0.0 copy-done.2
  28.2 0.0 copy-done.3
  28.2 0.0 copy-done.4
  28.2 4.3 %heads.1 = (bf16[128,128]{1,0:T(8,128)(2,1)S(1)}, bf16[512,384]{1,0:T(8,128)(2,1)S(1)}, bf16[512,256]{1,0:T(8,128)(2,1)S(1)}, f32[128,256]{1,0:T(8,128)S(1)}, bf...) custom-call(s32[4,4]{1,0:T(4,128)S(1)} %copy-done.3, s32[4]{0:T(128)S(1)} %copy-done.4, ...), custom_call_target="tpu_custom_call" | custom-call | tf_op jit(solution)/shard_map/heads/pallas_call | solution.py:359
  32.5 0.1 collective-permute-start.11
  32.7 0.8 %collective-permute-start.12 = (bf16[128,256]{1,0:T(8,128)(2,1)S(1)}, bf16[128,256]{1,0:T(8,128)(2,1)S(1)}, u32[]{:S(2)}, u32[]{:S(2)}) collective-permute-start(bf16[128,256]{1,0:T(8,128)(2,1)S(1)} %get-tuple-element.13), channel_id=1, source_target_pairs={{0,2},{1,3},{2,0},{3,1},{4,6},{5,7},{6,4},{7,5},{8,10},{9,11},{10,... | collective-permute-start | bytes 196616 | tf_op jit(solution)/shard_map/ppermute | solution.py:317
  33.4 1.0 %collective-permute-start.13 = (bf16[128,256]{1,0:T(8,128)(2,1)S(1)}, bf16[128,256]{1,0:T(8,128)(2,1)S(1)}, u32[]{:S(2)}, u32[]{:S(2)}) collective-permute-start(bf16[128,256]{1,0:T(8,128)(2,1)S(1)} %get-tuple-element.14), channel_id=1, source_target_pairs={{0,3},{1,2},{2,1},{3,0},{4,7},{5,6},{6,5},{7,4},{8,11},{9,10},{10,... | collective-permute-start | bytes 196616 | tf_op jit(solution)/shard_map/ppermute | solution.py:317
  34.5 1.1 %convolution_multiply_fusion = f32[256,384]{1,0:T(8,128)} fusion(bf16[512,256]{1,0:T(8,128)(2,1)S(1)} %get-tuple-element.15, bf16[512,384]{1,0:T(8,128)(2,1)S(1)} %get-tuple-element.16), kind=kOutput, calls=%fused_computation | convolution fusion | flops 100761600 | bytes 1048576 | tf_op jit(solution)/shard_map/dot_general | solution.py:372
  35.5 0.6 %copy.9 = bf16[128,128]{1,0:T(8,128)(2,1)} copy(bf16[128,128]{1,0:T(8,128)(2,1)S(1)} %get-tuple-element.17) | data formatting | bytes 65536
  36.2 0.0 collective-permute-done.11
  36.2 1.4 %collective-permute-done.12 = bf16[128,256]{1,0:T(8,128)(2,1)S(1)} collective-permute-done((bf16[128,256]{1,0:T(8,128)(2,1)S(1)}, bf16[128,256]{1,0:T(8,128)(2,1)S(1)}, u32[]{:S(2)}, u32[]{:S(2)}) %collective-permute-start.12) | collective-permute-done | bytes 65568 | tf_op jit(solution)/shard_map/ppermute | solution.py:317
  37.6 0.5 %collective-permute-done.13 = bf16[128,256]{1,0:T(8,128)(2,1)S(1)} collective-permute-done((bf16[128,256]{1,0:T(8,128)(2,1)S(1)}, bf16[128,256]{1,0:T(8,128)(2,1)S(1)}, u32[]{:S(2)}, u32[]{:S(2)}) %collective-permute-start.13) | collective-permute-done | bytes 65568 | tf_op jit(solution)/shard_map/ppermute | solution.py:317
  38.1 0.7 %add_convert_fusion = bf16[128,256]{1,0:T(8,128)(2,1)} fusion(bf16[128,256]{1,0:T(8,128)(2,1)S(1)} %collective-permute-done.13, bf16[128,256]{1,0:T(8,128)(2,1)S(1)} %collective-permute-done.12, f32[128,256]{1,0:T(8,128)S(1)} %get-tuple-element.11, bf16[128,256]{1,0:T(8,128)(2,1)S(1)} %collective-permute-done.11), kind=kLoop, calls=%fused_computation.1 | loop fusion | flops 229376 | bytes 393216 | tf_op jit(solution)/shard_map/convert_element_type | solution.py:371
  (6 shorter events, 0.1 us)
Async XLA Ops:
  1.6 13.3 %collective-permute-start.1 = (bf16[128,768]{1,0:T(8,128)(2,1)S(1)}, bf16[128,768]{1,0:T(8,128)(2,1)S(1)}, u32[]{:S(2)}, u32[]{:S(2)}) collective-permute-start(bf16[128,768]{1,0:T(8,128)(2,1)S(1)} %pack.1), channel_id=1, source_target_pairs={{0,8},{4,12},{8,0},{12,4},{1,9},{5,13},{9,1},{13,5},{2,10},{6,14},... | collective-permute-start | bytes 589832 | tf_op jit(solution)/shard_map/ppermute | solution.py:317
  5.7 9.8 %collective-permute-start = (bf16[128,768]{1,0:T(8,128)(2,1)S(1)}, bf16[128,768]{1,0:T(8,128)(2,1)S(1)}, u32[]{:S(2)}, u32[]{:S(2)}) collective-permute-start(bf16[128,768]{1,0:T(8,128)(2,1)S(1)} %pack.1), channel_id=1, source_target_pairs={{0,4},{4,0},{8,12},{12,8},{1,5},{5,1},{9,13},{13,9},{2,6},{6,2},{1... | collective-permute-start | bytes 589832 | tf_op jit(solution)/shard_map/ppermute | solution.py:317
  14.9 6.0 %collective-permute-start.3 = (bf16[128,768]{1,0:T(8,128)(2,1)S(1)}, bf16[128,768]{1,0:T(8,128)(2,1)S(1)}, u32[]{:S(2)}, u32[]{:S(2)}) collective-permute-start(bf16[128,768]{1,0:T(8,128)(2,1)S(1)} %collective-permute-done.1), channel_id=1, source_target_pairs={{0,4},{4,0},{8,12},{12,8},{1,5},{5,1},{9,13},{13,9},{2,6},{6,2},{1... | collective-permute-start | bytes 589832 | tf_op jit(solution)/shard_map/ppermute | solution.py:317
  15.6 6.7 %collective-permute-start.9 = (bf16[256,256]{1,0:T(8,128)(2,1)S(1)}, bf16[256,256]{1,0:T(8,128)(2,1)S(1)}, u32[]{:S(2)}, u32[]{:S(2)}) collective-permute-start(bf16[256,256]{1,0:T(8,128)(2,1)S(1)} %slice.16), channel_id=1, source_target_pairs={{0,2},{1,3},{2,0},{3,1},{4,6},{5,7},{6,4},{7,5},{8,10},{9,11},{10,... | collective-permute-start | bytes 393224 | tf_op jit(solution)/shard_map/ppermute | solution.py:317
  17.1 5.2 %collective-permute-start.7 = (bf16[256,256]{1,0:T(8,128)(2,1)S(1)}, bf16[256,256]{1,0:T(8,128)(2,1)S(1)}, u32[]{:S(2)}, u32[]{:S(2)}) collective-permute-start(bf16[256,256]{1,0:T(8,128)(2,1)S(1)} %slice.16), channel_id=1, source_target_pairs={{0,1},{1,0},{2,3},{3,2},{4,5},{5,4},{6,7},{7,6},{8,9},{9,8},{10,11... | collective-permute-start | bytes 393224 | tf_op jit(solution)/shard_map/ppermute | solution.py:317
  17.1 11.0 %copy-start.1 = (bf16[256,384]{1,0:T(8,128)(2,1)S(1)}, bf16[256,384]{1,0:T(8,128)(2,1)}, u32[]{:S(2)}) copy-start(bf16[256,384]{1,0:T(8,128)(2,1)} %refs_3_.1) | copy-start | bytes 589828
  17.2 11.0 %copy-start = (bf16[128,1024]{1,0:T(8,128)(2,1)S(1)}, bf16[128,1024]{1,0:T(8,128)(2,1)}, u32[]{:S(2)}) copy-start(bf16[128,1024]{1,0:T(8,128)(2,1)} %refs_2_.1) | copy-start | bytes 786436
  17.2 7.8 %collective-permute-start.10 = (bf16[256,384]{1,0:T(8,128)(2,1)S(1)}, bf16[256,384]{1,0:T(8,128)(2,1)S(1)}, u32[]{:S(2)}, u32[]{:S(2)}) collective-permute-start(bf16[256,384]{1,0:T(8,128)(2,1)S(1)} %slice.19), channel_id=1, source_target_pairs={{0,16},{16,0},{1,17},{17,1},{2,18},{18,2},{3,19},{19,3},{4,20},{20... | collective-permute-start | bytes 589832 | tf_op jit(solution)/shard_map/ppermute | solution.py:317
  18.8 5.5 %collective-permute-start.2 = (bf16[256,256]{1,0:T(8,128)(2,1)S(1)}, bf16[256,256]{1,0:T(8,128)(2,1)S(1)}, u32[]{:S(2)}, u32[]{:S(2)}) collective-permute-start(bf16[256,256]{1,0:T(8,128)(2,1)S(1)} %slice.16), channel_id=1, source_target_pairs={{0,3},{1,2},{2,1},{3,0},{4,7},{5,6},{6,5},{7,4},{8,11},{9,10},{10,... | collective-permute-start | bytes 393224 | tf_op jit(solution)/shard_map/ppermute | solution.py:317
  20.9 7.2 %copy-start.2 = (bf16[128,128]{1,0:T(8,128)(2,1)S(1)}, bf16[128,128]{1,0:T(8,128)(2,1)}, u32[]{:S(2)}) copy-start(bf16[128,128]{1,0:T(8,128)(2,1)} %refs_4_.1) | copy-start | bytes 98308
  20.9 7.2 %copy-start.3 = (s32[4,4]{1,0:T(4,128)S(1)}, s32[4,4]{1,0:T(4,128)}, u32[]{:S(2)}) copy-start(s32[4,4]{1,0:T(4,128)} %refs_0_.1) | copy-start | bytes 196
  21.0 7.2 %copy-start.4 = (s32[4]{0:T(128)S(1)}, s32[4]{0:T(128)}, u32[]{:S(2)}) copy-start(s32[4]{0:T(128)} %refs_1_.1) | copy-start | bytes 52
  21.0 7.2 %collective-permute-start.8 = (bf16[128,384]{1,0:T(8,128)(2,1)S(1)}, bf16[128,384]{1,0:T(8,128)(2,1)S(1)}, u32[]{:S(2)}, u32[]{:S(2)}) collective-permute-start(bf16[128,384]{1,0:T(8,128)(2,1)S(1)} %slice.18), channel_id=1, source_target_pairs={{0,16},{16,0},{1,17},{17,1},{2,18},{18,2},{3,19},{19,3},{4,20},{20... | collective-permute-start | bytes 294920 | tf_op jit(solution)/shard_map/ppermute | solution.py:317
  22.3 4.4 %collective-permute-start.6 = (bf16[128,256]{1,0:T(8,128)(2,1)S(1)}, bf16[128,256]{1,0:T(8,128)(2,1)S(1)}, u32[]{:S(2)}, u32[]{:S(2)}) collective-permute-start(bf16[128,256]{1,0:T(8,128)(2,1)S(1)} %slice.17), channel_id=1, source_target_pairs={{0,3},{1,2},{2,1},{3,0},{4,7},{5,6},{6,5},{7,4},{8,11},{9,10},{10,... | collective-permute-start | bytes 196616 | tf_op jit(solution)/shard_map/ppermute | solution.py:317
  22.4 5.8 %collective-permute-start.5 = (bf16[128,256]{1,0:T(8,128)(2,1)S(1)}, bf16[128,256]{1,0:T(8,128)(2,1)S(1)}, u32[]{:S(2)}, u32[]{:S(2)}) collective-permute-start(bf16[128,256]{1,0:T(8,128)(2,1)S(1)} %slice.17), channel_id=1, source_target_pairs={{0,2},{1,3},{2,0},{3,1},{4,6},{5,7},{6,4},{7,5},{8,10},{9,11},{10,... | collective-permute-start | bytes 196616 | tf_op jit(solution)/shard_map/ppermute | solution.py:317
  24.2 3.9 %collective-permute-start.4 = (bf16[128,256]{1,0:T(8,128)(2,1)S(1)}, bf16[128,256]{1,0:T(8,128)(2,1)S(1)}, u32[]{:S(2)}, u32[]{:S(2)}) collective-permute-start(bf16[128,256]{1,0:T(8,128)(2,1)S(1)} %slice.17), channel_id=1, source_target_pairs={{0,1},{1,0},{2,3},{3,2},{4,5},{5,4},{6,7},{7,6},{8,9},{9,8},{10,11... | collective-permute-start | bytes 196616 | tf_op jit(solution)/shard_map/ppermute | solution.py:317
  32.5 3.6 %collective-permute-start.11 = (bf16[128,256]{1,0:T(8,128)(2,1)S(1)}, bf16[128,256]{1,0:T(8,128)(2,1)S(1)}, u32[]{:S(2)}, u32[]{:S(2)}) collective-permute-start(bf16[128,256]{1,0:T(8,128)(2,1)S(1)} %get-tuple-element.12), channel_id=1, source_target_pairs={{0,1},{1,0},{2,3},{3,2},{4,5},{5,4},{6,7},{7,6},{8,9},{9,8},{10,11... | collective-permute-start | bytes 196616 | tf_op jit(solution)/shard_map/ppermute | solution.py:317
  32.7 4.9 %collective-permute-start.12 = (bf16[128,256]{1,0:T(8,128)(2,1)S(1)}, bf16[128,256]{1,0:T(8,128)(2,1)S(1)}, u32[]{:S(2)}, u32[]{:S(2)}) collective-permute-start(bf16[128,256]{1,0:T(8,128)(2,1)S(1)} %get-tuple-element.13), channel_id=1, source_target_pairs={{0,2},{1,3},{2,0},{3,1},{4,6},{5,7},{6,4},{7,5},{8,10},{9,11},{10,... | collective-permute-start | bytes 196616 | tf_op jit(solution)/shard_map/ppermute | solution.py:317
  33.4 4.6 %collective-permute-start.13 = (bf16[128,256]{1,0:T(8,128)(2,1)S(1)}, bf16[128,256]{1,0:T(8,128)(2,1)S(1)}, u32[]{:S(2)}, u32[]{:S(2)}) collective-permute-start(bf16[128,256]{1,0:T(8,128)(2,1)S(1)} %get-tuple-element.14), channel_id=1, source_target_pairs={{0,3},{1,2},{2,1},{3,0},{4,7},{5,6},{6,5},{7,4},{8,11},{9,10},{10,... | collective-permute-start | bytes 196616 | tf_op jit(solution)/shard_map/ppermute | solution.py:317

commit v3 on v2

--- a/solution.py
+++ b/solution.py
@@ -160,36 +160,28 @@
 def heads_kernel(slots, refs_of, where, *refs):
     named = dict(zip(refs_of, refs))
     covis, drive = named["covis"], named["drive"]
-    t_all, w_all, gq = named["t_all"], named["w_all"], named["gq"]
+    t_all, w_all = named["t_all"], named["w_all"]
     rows = BLOCK
     length = slots * rows
     z = lax.axis_index("seq")
     f = lax.axis_index("fsdp")
-    y = lax.axis_index("groups")
     depth = w_all.shape[0] // slots
-    half = depth // 2
     quarter = t_all.shape[1] // 4
 
     t_all[0:rows, :] = named["t0"][...]
-    w_all[pl.ds(pl.multiple_of(z * depth, depth), depth), :] = named["w0"][...]
     width = w_all.shape[1]
     grads = [named["g0"][...]]
     for k in range(1, slots):
-        name, at = where[k, "r"]
-        r = named[name].at[pl.ds(at, rows), :]
-        name, at = where[k, "v"]
-        v = named[name].at[pl.ds(at, rows), :]
-        first = (z ^ k) * depth
-        w_all[pl.ds(pl.multiple_of(first + y * half, half), half), :] = r[:, 0:width]
-        w_all[pl.ds(pl.multiple_of(first + (1 - y) * half, half), half), :] = v[...]
-        pieces = [r[:, width : width + quarter]]
+        name, at, off = where[k, "t"]
+        tg = named[name].at[pl.ds(at, rows), :]
+        pieces = [tg[:, off : off + quarter]]
         for m in range(1, 4):
             name, at = where[k, m]
             pieces.append(named[name][pl.ds(at, rows), :])
         for m, piece in enumerate(pieces):
             columns = pl.ds(pl.multiple_of((f ^ m) * quarter, quarter), quarter)
             t_all[pl.ds(k * rows, rows), columns] = piece
-        grads.append(r[:, width + quarter :])
+        grads.append(tg[:, off + quarter :])
     grads = jnp.concatenate(grads, axis=0)
     projected = dot(t_all[...], w_all[...]).astype(BF)
     grads_t = jnp.transpose(grads)
@@ -202,65 +194,83 @@
             bias[a, b] = jnp.where(seen, 0.0, MASKED_SCORE).astype(F32)
 
     heads = width // (3 * HD)
-    span = 4 * rows
-    out_columns = []
-    attention_t = []
+    scale = HD ** (-0.5)
+    bias_rows = [
+        jnp.concatenate([jnp.full((1, rows), bias[a, b], F32) for a in range(slots)], axis=1)
+        for b in range(slots)
+    ]
+    own = []
     for h in range(heads):
-        base = 3 * HD * h
-        q8 = projected[:, base : base + HD] * jnp.asarray(HD ** (-0.5), BF)
-        k_h = projected[:, base + HD : base + 2 * HD]
-        v_h = projected[:, base + 2 * HD : base + 3 * HD]
-        k_t = jnp.transpose(k_h)
-        v_t = jnp.transpose(v_h)
+        q8, k_h, v_h = split_heads(projected, h)
         g_h = grads[:, HD * h : HD * (h + 1)]
         g_t = grads_t[HD * h : HD * (h + 1), :]
-        d_k = jnp.zeros((length, HD), F32)
-        d_v = jnp.zeros((length, HD), F32)
-        d_q_t = []
-        for part in range(length // span):
-            at = slice(part * span, (part + 1) * span)
-            s_t = dot_nt(k_h, q8[at])
-            masked = []
-            for b in range(slots):
-                masked.append(
-                    jnp.concatenate(
-                        [
-                            s_t[b * rows : (b + 1) * rows, e * rows : (e + 1) * rows]
-                            + bias[part * (span // rows) + e, b]
-                            for e in range(span // rows)
-                        ],
-                        axis=1,
-                    )
-                )
-            s_t = jnp.concatenate(masked, axis=0)
-            top = jnp.max(s_t, axis=0, keepdims=True)
-            e_t = jnp.exp(s_t - top)
-            total = jnp.sum(e_t, axis=0, keepdims=True)
-            p_t = e_t * (1.0 / total)
-            p_b = p_t.astype(BF)
-            p_rest = (p_t - p_b.astype(F32)).astype(BF)
-            o_t = (dot(v_t, p_b) + dot(v_t, p_rest)).astype(BF)
-            if part == 0:
-                attention_t.append(o_t[:, 0:rows])
-            grad_dot = jnp.sum(
-                g_t[:, at].astype(F32) * o_t.astype(F32), axis=0, keepdims=True
-            )
-            dp_t = dot_nt(v_h, g_h[at])
-            ds_t = (p_t * (dp_t - grad_dot)).astype(BF)
-            d_v = d_v + dot(p_b, g_h[at])
-            d_k = d_k + dot(ds_t, q8[at])
-            d_q_t.append(dot(k_t, ds_t))
-        d_q = jnp.transpose(jnp.concatenate(d_q_t, axis=1)) * (HD ** (-0.5))
-        out_columns += [d_q, d_k, d_v]
-    grad_qkv = jnp.concatenate(out_columns, axis=1).astype(BF)
-    gq[...] = grad_qkv
-    named["attention"][...] = jnp.transpose(jnp.concatenate(attention_t, axis=0))
-    own = grad_qkv[0:rows]
+        s_t = dot_nt(k_h, q8)
+        s_t = jnp.concatenate(
+            [s_t[b * rows : (b + 1) * rows] + bias_rows[b] for b in range(slots)], axis=0
+        )
+        top = jnp.max(s_t, axis=0, keepdims=True)
+        e_t = jnp.exp(s_t - top)
+        total = jnp.sum(e_t, axis=0, keepdims=True)
+        p_t = e_t * (1.0 / total)
+        p_b = p_t.astype(BF)
+        p_rest = (p_t - p_b.astype(F32)).astype(BF)
+        v_t = jnp.transpose(v_h)
+        o_t = (dot(v_t, p_b) + dot(v_t, p_rest)).astype(BF)
+        grad_dot = jnp.sum(g_t.astype(F32) * o_t.astype(F32), axis=0, keepdims=True)
+        named["p_b"][h] = p_b
+        named["p_rest"][h] = p_rest
+        named["grad_dot"][h] = grad_dot
+        named["attention_t"][HD * h : HD * (h + 1), :] = o_t[:, 0:rows]
+        ds_q = (p_t[:, 0:rows] * (dot_nt(v_h, g_h[0:rows]) - grad_dot[:, 0:rows])).astype(BF)
+        ds_k = (p_t[0:rows] * (dot_nt(v_h[0:rows], g_h) - grad_dot)).astype(BF)
+        d_q = jnp.transpose(dot(jnp.transpose(k_h), ds_q)) * scale
+        own += [d_q, dot(ds_k, q8), dot(p_b[0:rows], g_h)]
+    own = jnp.concatenate(own, axis=1).astype(BF)
     for m in range(4):
         out = named["part%d" % m]
         w_rows = w_all[pl.ds(pl.multiple_of((f ^ m) * depth, depth), depth), :]
         out[...] = dot_nt(own, w_rows).astype(out.dtype)
+    named["projected"][...] = projected
+    named["grads"][...] = grads
     named["t_d"][...] = t_all[:, pl.ds(pl.multiple_of(z * depth, depth), depth)]
+
+
+def split_heads(projected, h):
+    base = 3 * HD * h
+    q8 = projected[:, base : base + HD] * jnp.asarray(HD ** (-0.5), BF)
+    return q8, projected[:, base + HD : base + 2 * HD], projected[:, base + 2 * HD : base + 3 * HD]
+
+
+def rest_kernel(
+    p_b_ref, p_rest_ref, grad_dot_ref, attention_t, projected_ref, grads_ref, t_d, attention, weight
+):
+    projected, grads = projected_ref[...], grads_ref[...]
+    columns = []
+    for h in range(p_b_ref.shape[0]):
+        q8, k_h, v_h = split_heads(projected, h)
+        g_h = grads[:, HD * h : HD * (h + 1)]
+        p_b = p_b_ref[h]
+        p_t = p_b.astype(F32) + p_rest_ref[h].astype(F32)
+        ds_t = (p_t * (dot_nt(v_h, g_h) - grad_dot_ref[h])).astype(BF)
+        d_q = jnp.transpose(dot(jnp.transpose(k_h), ds_t)) * (HD ** (-0.5))
+        columns += [d_q, dot(ds_t, q8), dot(p_b, g_h)]
+    grad_qkv = jnp.concatenate(columns, axis=1).astype(BF)
+    token_scale = grads.shape[0] ** (-0.5)
+    weight[...] = dot(jnp.transpose(t_d[...]), grad_qkv) * token_scale
+    attention[...] = jnp.transpose(attention_t[...])
+
+
+def weight_kernel(slots, w0, near, far, near_half, far_half, out):
+    z = lax.axis_index("seq")
+    y = lax.axis_index("groups")
+    depth, width = w0.shape
+    half = depth // 2
+    out[pl.ds(pl.multiple_of(z * depth, depth), depth), :] = w0[...]
+    for k in range(1, slots):
+        a, b, at = (far, far_half, 0) if k == 3 else (near, near_half, (k - 1) * half)
+        first = (z ^ k) * depth
+        out[pl.ds(pl.multiple_of(first + y * half, half), half), :] = a[at : at + half, 0:width]
+        out[pl.ds(pl.multiple_of(first + (1 - y) * half, half), half), :] = b[at : at + half, :]
 
 
 def pack_kernel(w_ref, t_ref, g_ref, out, sems):
@@ -319,31 +329,47 @@
     packed = pack(tokens, qkv_weight, grad_out)
     got2 = swap(packed, "seq", 2)
     got1 = swap(packed, "seq", 1)
-    got3 = swap(got2, "seq", 1)
+    tg3 = swap(got2[:, width:], "seq", 1)
+    got3 = swap(got2[:, :width], "seq", 1)
     near = jnp.concatenate([got1, got2], axis=0)
     piece12 = near[:, width : width + quarter]
-    piece3 = got3[:, width : width + quarter]
+    w12 = near[:, :width]
+    piece3 = tg3[:, :quarter]
+    w3 = got3
+    v12 = swap(w12, "groups", 1)
+    x12 = swap(piece12, "fsdp", 2)
     x3 = swap(piece3, "fsdp", 2)
-    v12 = swap(near[:, :width], "groups", 1)
-    c3 = swap(piece3, "fsdp", 1)
-    v3 = swap(got3[:, :width], "groups", 1)
-    x12 = swap(piece12, "fsdp", 2)
-    d3 = swap(piece3, "fsdp", 3)
-    c12 = swap(piece12, "fsdp", 1)
-    d12 = swap(piece12, "fsdp", 3)
-    moved = dict(d12=d12, near=near, c3=c3, x3=x3, d3=d3, c12=c12, v3=v3, x12=x12, v12=v12, got3=got3)
+    v3 = swap(w3, "groups", 1)
+    call = swap(jnp.concatenate([piece12, x12, piece3, x3], axis=0), "fsdp", 1)
+    vmem = pl.BlockSpec(memory_space=pltpu.VMEM)
+    w_all = pl.pallas_call(
+        functools.partial(weight_kernel, slots),
+        out_shape=pltpu.VMEM((depth * slots, width), BF),
+        in_specs=[vmem] * 5,
+        out_specs=vmem,
+        cost_estimate=pl.CostEstimate(flops=8000000000, transcendentals=0, bytes_accessed=2000000),
+        compiler_params=pltpu.CompilerParams(vmem_limit_bytes=16 << 20),
+        name="weight",
+    )(qkv_weight, near, got3, v12, v3)
+    moved = dict(near=near, tg3=tg3, x12=x12, x3=x3, call=call)
     where = {}
     for k, at in ((1, 0), (2, rows)):
-        where.update({(k, "r"): ("near", at), (k, "v"): ("v12", at)})
-        where.update({(k, 1): ("c12", at), (k, 2): ("x12", at), (k, 3): ("d12", at)})
-    where.update({(3, "r"): ("got3", 0), (3, "v"): ("v3", 0)})
-    where.update({(3, 1): ("c3", 0), (3, 2): ("x3", 0), (3, 3): ("d3", 0)})
-    names = ["covis", "drive", "t0", "w0", "g0"] + list(moved)
-    values = [covisible, block_drive, tokens, qkv_weight, grad_out] + list(moved.values())
+        where.update({(k, "r"): ("near", at), (k, "t"): ("near", at, width), (k, "v"): ("v12", at)})
+        where.update({(k, 1): ("call", at), (k, 2): ("x12", at), (k, 3): ("call", 2 * rows + at)})
+    where.update({(3, "r"): ("got3", 0), (3, "t"): ("tg3", 0, 0), (3, "v"): ("v3", 0)})
+    where.update({(3, 1): ("call", 4 * rows), (3, 2): ("x3", 0), (3, 3): ("call", 5 * rows)})
+    names = ["covis", "drive", "t0", "g0", "w_all"] + list(moved)
+    values = [covisible, block_drive, tokens, grad_out, w_all] + list(moved.values())
+    heads = width // (3 * HD)
+    length = rows * slots
     outs = [
-        ("attention", (rows, grad_out.shape[1]), BF),
-        ("gq", (rows * slots, width), BF),
-        ("t_d", (rows * slots, depth), BF),
+        ("p_b", (heads, length, length), BF),
+        ("p_rest", (heads, length, length), BF),
+        ("grad_dot", (heads, 1, length), F32),
+        ("attention_t", (heads * HD, rows), BF),
+        ("projected", (length, width), BF),
+        ("grads", (length, heads * HD), BF),
+        ("t_d", (length, depth), BF),
         ("part0", (rows, depth), F32),
         ("part1", (rows, depth), BF),
         ("part2", (rows, depth), BF),
@@ -351,12 +377,11 @@
     ]
     scratch = [
         ("t_all", pltpu.VMEM((rows * slots, features), BF)),
-        ("w_all", pltpu.VMEM((depth * slots, width), BF)),
     ]
     vmem = pl.BlockSpec(memory_space=pltpu.VMEM)
     smem = pl.BlockSpec(memory_space=pltpu.SMEM)
     refs_of = names + [n for n, _, _ in outs] + [n for n, _ in scratch]
-    attention, gq, t_d, *parts = pl.pallas_call(
+    *kept, part0, part1, part2, part3 = pl.pallas_call(
         functools.partial(heads_kernel, slots, refs_of, where),
         out_shape=[pltpu.VMEM(s, d) for _, s, d in outs],
         in_specs=[smem, smem] + [vmem] * (len(names) - 2),
@@ -365,13 +390,21 @@
         compiler_params=pltpu.CompilerParams(vmem_limit_bytes=48 << 20),
         name="heads",
     )(*values)
-    total = parts[0]
-    for m in (1, 2, 3):
-        total = total + swap(parts[m], "fsdp", m).astype(F32)
+    total = part0
+    for m, part in ((1, part1), (2, part2), (3, part3)):
+        total = total + swap(part, "fsdp", m).astype(F32)
     grad_input = total.astype(BF)
-    grad_weight = lax.dot_general(
-        t_d, gq, (((0,), (0,)), ((), ())), preferred_element_type=F32
-    ) * ((rows * slots) ** (-0.5))
+    attention, grad_weight = pl.pallas_call(
+        rest_kernel,
+        out_shape=[
+            jax.ShapeDtypeStruct(grad_out.shape, BF),
+            jax.ShapeDtypeStruct((depth, width), F32),
+        ],
+        in_specs=[vmem] * len(kept),
+        out_specs=[vmem] * 2,
+        compiler_params=pltpu.CompilerParams(vmem_limit_bytes=48 << 20),
+        name="rest",
+    )(*kept)
     return attention, grad_input, grad_weight
 
 

time: 38.9 us -> 37.2 us (0.956)
  waiting for transfers between devices: 15.1 us -> 11.9 us
  Pallas kernels: 5.27 us -> 7.41 us
  starting transfers between devices: 15.1 us -> 16.2 us
  matrix products: 1.07 us -> 0 us
  local copies, waits for them, and re-layouts: 0.72 us -> 0.12 us
    ppermute x14 -> x12, waiting for transfers between devices: 15.1 us -> 11.9 us  [swap(): return lax.ppermute(x, axis, [(i, i ^ bit) for i in range(n)])]
    pallas_call x0 -> x2, Pallas kernels: none -> 2.57 us  [the longest x1 2.48 us: short(): pl.pallas_call(rest_kernel, out_shape=[jax.ShapeDtypeStruct(grad_out.shap...]
    dot_general x1 -> x0, matrix products: 1.07 us -> none  [short(): lax.dot_general(t_d, gq, (((0,), (0,)), ((), ())), preferred_element_type...]
    ppermute x14 -> x12, starting transfers between devices: 15.1 us -> 16.2 us  [swap(): return lax.ppermute(x, axis, [(i, i ^ bit) for i in range(n)])]
    unnamed x12 -> x11, local copies, waits for them, and re-layouts: 0.66 us -> 0.05 us
    pallas_call x1, Pallas kernels: 4.33 us -> 3.91 us  [short(): pl.pallas_call(functools.partial(heads_kernel, slots, refs_of, where), ou...]
  transfers between devices with their start and end apart: 14 -> 12, of which waited for: 8 -> 5; matrix products, arithmetic and copies ran while one was open for 5% -> 0% of each run, Pallas kernels for 0% -> 7%
where the time goes in v3:
time: 37.2 us; the launch traced here: 37.1 us
  starting transfers between devices  16.2 us (44%)
  waiting for transfers between devices  11.9 us (32%)
  Pallas kernels  7.41 us (20%)
  between operations  0.79 us (2%)
  other arithmetic  0.69 us (2%)
    ppermute x12, starting transfers between devices, swap(): return lax.ppermute(x, axis, [(i, i ^ bit) for i in range(n)])  16.2 us
    ppermute x12, waiting for transfers between devices, swap(): return lax.ppermute(x, axis, [(i, i ^ bit) for i in range(n)])  11.9 us
    pallas_call x1, Pallas kernels, short(): pl.pallas_call(functools.partial(heads_kernel, slots, refs_of, where), ou...  3.91 us
    pallas_call x1, Pallas kernels, short(): pl.pallas_call(rest_kernel, out_shape=[jax.ShapeDtypeStruct(grad_out.shap...  2.48 us
    pallas_call x1, Pallas kernels, pack(): pl.pallas_call(pack_kernel, out_shape=pltpu.VMEM((rows, columns), BF), in...  0.94 us
  transfers between devices with their start and end apart: 12, of which 5 were waited for; matrix products, arithmetic and copies ran while one was open for 0% of the time, Pallas kernels for 7%

profile of v3, /device:TPU:0, one launch (start us, length us, event | category | flops | bytes accessed | tf_op | source)
XLA Modules:
  0.0 37.1 jit_solution(8954995687799902662)
XLA Ops:
  0.6 0.9 %pack.1 = bf16[128,768]{1,0:T(8,128)(2,1)S(1)} custom-call(bf16[256,384]{1,0:T(8,128)(2,1)} %w0.1, bf16[128,1024]{1,0:T(8,128)(2,1)} %refs_2_.1, bf16[128,128]{1,0:T(8,128)(2,1)} %refs_3_.1), custom_call_target="tpu_custom_call" | custom-call | tf_op jit(solution)/shard_map/pack/pallas_call | solution.py:305
  1.6 4.1 %collective-permute-start.1 = (bf16[128,768]{1,0:T(8,128)(2,1)S(1)}, bf16[128,768]{1,0:T(8,128)(2,1)S(1)}, u32[]{:S(2)}, u32[]{:S(2)}) collective-permute-start(bf16[128,768]{1,0:T(8,128)(2,1)S(1)} %pack.1), channel_id=1, source_target_pairs={{0,8},{4,12},{8,0},{12,4},{1,9},{5,13},{9,1},{13,5},{2,10},{6,14},... | collective-permute-start | bytes 589832 | tf_op jit(solution)/shard_map/ppermute | solution.py:327
  5.7 1.6 %collective-permute-start = (bf16[128,768]{1,0:T(8,128)(2,1)S(1)}, bf16[128,768]{1,0:T(8,128)(2,1)S(1)}, u32[]{:S(2)}, u32[]{:S(2)}) collective-permute-start(bf16[128,768]{1,0:T(8,128)(2,1)S(1)} %pack.1), channel_id=1, source_target_pairs={{0,4},{4,0},{8,12},{12,8},{1,5},{5,1},{9,13},{13,9},{2,6},{6,2},{1... | collective-permute-start | bytes 589832 | tf_op jit(solution)/shard_map/ppermute | solution.py:327
  7.3 7.6 %collective-permute-done.1 = bf16[128,768]{1,0:T(8,128)(2,1)S(1)} collective-permute-done((bf16[128,768]{1,0:T(8,128)(2,1)S(1)}, bf16[128,768]{1,0:T(8,128)(2,1)S(1)}, u32[]{:S(2)}, u32[]{:S(2)}) %collective-permute-start.1) | collective-permute-done | bytes 196640 | tf_op jit(solution)/shard_map/ppermute | solution.py:327
  14.9 0.7 %collective-permute-start.5 = (bf16[128,384]{1,0:T(8,128)(2,1)S(1)}, bf16[128,384]{1,0:T(8,128)(2,1)S(1)}, u32[]{:S(2)}, u32[]{:S(2)}) collective-permute-start(bf16[128,384]{1,0:T(8,128)(2,1)S(1)} %get-tuple-element.29), channel_id=1, source_target_pairs={{0,4},{4,0},{8,12},{12,8},{1,5},{5,1},{9,13},{13,9},{2,6},{6,2},{1... | collective-permute-start | bytes 294920 | tf_op jit(solution)/shard_map/ppermute | solution.py:327
  15.6 0.0 collective-permute-done
  15.7 1.6 %collective-permute-start.6 = (bf16[256,256]{1,0:T(8,128)(2,1)S(1)}, bf16[256,256]{1,0:T(8,128)(2,1)S(1)}, u32[]{:S(2)}, u32[]{:S(2)}) collective-permute-start(bf16[256,256]{1,0:T(8,128)(2,1)S(1)} %slice.23), channel_id=1, source_target_pairs={{0,2},{1,3},{2,0},{3,1},{4,6},{5,7},{6,4},{7,5},{8,10},{9,11},{10,... | collective-permute-start | bytes 393224 | tf_op jit(solution)/shard_map/ppermute | solution.py:327
  17.2 1.5 %collective-permute-start.2 = (bf16[128,384]{1,0:T(8,128)(2,1)S(1)}, bf16[128,384]{1,0:T(8,128)(2,1)S(1)}, u32[]{:S(2)}, u32[]{:S(2)}) collective-permute-start(bf16[128,384]{1,0:T(8,128)(2,1)S(1)} %get-tuple-element.30), channel_id=1, source_target_pairs={{0,4},{4,0},{8,12},{12,8},{1,5},{5,1},{9,13},{13,9},{2,6},{6,2},{1... | collective-permute-start | bytes 294920 | tf_op jit(solution)/shard_map/ppermute | solution.py:327
  18.7 1.6 %collective-permute-start.3 = (bf16[256,384]{1,0:T(8,128)(2,1)S(1)}, bf16[256,384]{1,0:T(8,128)(2,1)S(1)}, u32[]{:S(2)}, u32[]{:S(2)}) collective-permute-start(bf16[256,384]{1,0:T(8,128)(2,1)S(1)} %slice.21), channel_id=1, source_target_pairs={{0,16},{16,0},{1,17},{17,1},{2,18},{18,2},{3,19},{19,3},{4,20},{20... | collective-permute-start | bytes 589832 | tf_op jit(solution)/shard_map/ppermute | solution.py:327
  20.3 0.0 collective-permute-done.5.refs_6_
  20.3 0.0 copy-start.1
  20.3 1.7 %collective-permute-start.7 = (bf16[128,256]{1,0:T(8,128)(2,1)S(1)}, bf16[128,256]{1,0:T(8,128)(2,1)S(1)}, u32[]{:S(2)}, u32[]{:S(2)}) collective-permute-start(bf16[128,256]{1,0:T(8,128)(2,1)S(1)} %slice.24), channel_id=1, source_target_pairs={{0,2},{1,3},{2,0},{3,1},{4,6},{5,7},{6,4},{7,5},{8,10},{9,11},{10,... | collective-permute-start | bytes 196616 | tf_op jit(solution)/shard_map/ppermute | solution.py:327
  22.0 0.0 collective-permute-done.2.far
  22.0 1.5 %collective-permute-start.4 = (bf16[128,384]{1,0:T(8,128)(2,1)S(1)}, bf16[128,384]{1,0:T(8,128)(2,1)S(1)}, u32[]{:S(2)}, u32[]{:S(2)}) collective-permute-start(bf16[128,384]{1,0:T(8,128)(2,1)S(1)} %collective-permute-done.2.far), channel_id=1, source_target_pairs={{0,16},{16,0},{1,17},{17,1},{2,18},{18,2},{3,19},{19,3},{4,20},{20... | collective-permute-start | bytes 294920 | tf_op jit(solution)/shard_map/ppermute | solution.py:327
  23.5 0.0 collective-permute-done.6.refs_7_
  23.5 1.1 %collective-permute-done.7.refs_8_ = bf16[128,256]{1,0:T(8,128)(2,1)S(1)} collective-permute-done((bf16[128,256]{1,0:T(8,128)(2,1)S(1)}, bf16[128,256]{1,0:T(8,128)(2,1)S(1)}, u32[]{:S(2)}, u32[]{:S(2)}) %collective-permute-start.7) | collective-permute-done | bytes 65568 | tf_op jit(solution)/shard_map/ppermute | solution.py:327
  24.7 0.0 copy-start
  24.7 0.0 copy-start.2
  24.7 0.0 copy-start.3
  24.7 0.0 copy-start.4
  24.7 0.1 collective-permute-start.8
  24.8 1.8 %collective-permute-done.4.far_half = bf16[128,384]{1,0:T(8,128)(2,1)S(1)} collective-permute-done((bf16[128,384]{1,0:T(8,128)(2,1)S(1)}, bf16[128,384]{1,0:T(8,128)(2,1)S(1)}, u32[]{:S(2)}, u32[]{:S(2)}) %collective-permute-start.4) | collective-permute-done | bytes 98336 | tf_op jit(solution)/shard_map/ppermute | solution.py:327
  26.6 0.0 collective-permute-done.3.near_half
  26.6 0.0 copy-done.1
  26.6 0.1 weight.1.refs_4_
  26.7 0.0 collective-permute-done.8.refs_9_
  26.7 0.0 copy-done
  26.7 0.0 copy-done.2
  26.7 0.0 copy-done.3
  26.7 0.0 copy-done.4
  26.8 3.9 %heads.1 = (bf16[2,512,512]{2,1,0:T(8,128)(2,1)S(1)}, bf16[2,512,512]{2,1,0:T(8,128)(2,1)S(1)}, f32[2,1,512]{2,1,0:T(1,128)S(1)}, bf16[128,128]{1,0:T(8,128)(2,1...) custom-call(s32[4,4]{1,0:T(4,128)S(1)} %copy-done.3, ...), custom_call_target="tpu_custom_call" | custom-call | tf_op jit(solution)/shard_map/heads/pallas_call | solution.py:384
  30.7 0.1 collective-permute-start.9
  30.7 1.5 %collective-permute-start.10 = (bf16[128,256]{1,0:T(8,128)(2,1)S(1)}, bf16[128,256]{1,0:T(8,128)(2,1)S(1)}, u32[]{:S(2)}, u32[]{:S(2)}) collective-permute-start(bf16[128,256]{1,0:T(8,128)(2,1)S(1)} %get-tuple-element.26), channel_id=1, source_target_pairs={{0,2},{1,3},{2,0},{3,1},{4,6},{5,7},{6,4},{7,5},{8,10},{9,11},{10,... | collective-permute-start | bytes 196616 | tf_op jit(solution)/shard_map/ppermute | solution.py:327
  32.3 0.3 collective-permute-start.11
  32.6 2.5 %rest.1 = (bf16[128,128]{1,0:T(8,128)(2,1)}, f32[256,384]{1,0:T(8,128)}) custom-call(bf16[2,512,512]{2,1,0:T(8,128)(2,1)S(1)} %get-tuple-element.16.p_b_ref, bf16[2,512,512]{2,1,0:T(8,128)(2,1)S(1)} %get-tuple-element.17.p_rest_ref, f32[2,1,512]{2,1,0:T(1,128)S(1)} %get-tuple-element.18.grad_dot_ref, bf16[128,128]{1,0:T(8,128)(2,1)S(1)} %get-tuple-element.19.attention_t, ...), custom_call_target="tpu_custom_call" | custom-call | tf_op jit(solution)/shard_map/rest/pallas_call | solution.py:397
  35.1 0.0 collective-permute-done.9
  35.1 0.2 collective-permute-done.10
  35.3 1.2 %collective-permute-done.11 = bf16[128,256]{1,0:T(8,128)(2,1)S(1)} collective-permute-done((bf16[128,256]{1,0:T(8,128)(2,1)S(1)}, bf16[128,256]{1,0:T(8,128)(2,1)S(1)}, u32[]{:S(2)}, u32[]{:S(2)}) %collective-permute-start.11) | collective-permute-done | bytes 65568 | tf_op jit(solution)/shard_map/ppermute | solution.py:327
  36.4 0.7 %add_convert_fusion = bf16[128,256]{1,0:T(8,128)(2,1)} fusion(bf16[128,256]{1,0:T(8,128)(2,1)S(1)} %collective-permute-done.11, bf16[128,256]{1,0:T(8,128)(2,1)S(1)} %collective-permute-done.10, f32[128,256]{1,0:T(8,128)S(1)} %get-tuple-element.24, bf16[128,256]{1,0:T(8,128)(2,1)S(1)} %collective-permute-done.9), kind=kLoop, calls=%fused_computation.1 | loop fusion | flops 229376 | bytes 393216 | tf_op jit(solution)/shard_map/convert_element_type | solution.py:396
  (7 shorter events, 0.1 us)
Async XLA Ops:
  1.6 13.3 %collective-permute-start.1 = (bf16[128,768]{1,0:T(8,128)(2,1)S(1)}, bf16[128,768]{1,0:T(8,128)(2,1)S(1)}, u32[]{:S(2)}, u32[]{:S(2)}) collective-permute-start(bf16[128,768]{1,0:T(8,128)(2,1)S(1)} %pack.1), channel_id=1, source_target_pairs={{0,8},{4,12},{8,0},{12,4},{1,9},{5,13},{9,1},{13,5},{2,10},{6,14},... | collective-permute-start | bytes 589832 | tf_op jit(solution)/shard_map/ppermute | solution.py:327
  5.7 9.9 %collective-permute-start = (bf16[128,768]{1,0:T(8,128)(2,1)S(1)}, bf16[128,768]{1,0:T(8,128)(2,1)S(1)}, u32[]{:S(2)}, u32[]{:S(2)}) collective-permute-start(bf16[128,768]{1,0:T(8,128)(2,1)S(1)} %pack.1), channel_id=1, source_target_pairs={{0,4},{4,0},{8,12},{12,8},{1,5},{5,1},{9,13},{13,9},{2,6},{6,2},{1... | collective-permute-start | bytes 589832 | tf_op jit(solution)/shard_map/ppermute | solution.py:327
  14.9 5.4 %collective-permute-start.5 = (bf16[128,384]{1,0:T(8,128)(2,1)S(1)}, bf16[128,384]{1,0:T(8,128)(2,1)S(1)}, u32[]{:S(2)}, u32[]{:S(2)}) collective-permute-start(bf16[128,384]{1,0:T(8,128)(2,1)S(1)} %get-tuple-element.29), channel_id=1, source_target_pairs={{0,4},{4,0},{8,12},{12,8},{1,5},{5,1},{9,13},{13,9},{2,6},{6,2},{1... | collective-permute-start | bytes 294920 | tf_op jit(solution)/shard_map/ppermute | solution.py:327
  15.7 7.9 %collective-permute-start.6 = (bf16[256,256]{1,0:T(8,128)(2,1)S(1)}, bf16[256,256]{1,0:T(8,128)(2,1)S(1)}, u32[]{:S(2)}, u32[]{:S(2)}) collective-permute-start(bf16[256,256]{1,0:T(8,128)(2,1)S(1)} %slice.23), channel_id=1, source_target_pairs={{0,2},{1,3},{2,0},{3,1},{4,6},{5,7},{6,4},{7,5},{8,10},{9,11},{10,... | collective-permute-start | bytes 393224 | tf_op jit(solution)/shard_map/ppermute | solution.py:327
  17.2 4.8 %collective-permute-start.2 = (bf16[128,384]{1,0:T(8,128)(2,1)S(1)}, bf16[128,384]{1,0:T(8,128)(2,1)S(1)}, u32[]{:S(2)}, u32[]{:S(2)}) collective-permute-start(bf16[128,384]{1,0:T(8,128)(2,1)S(1)} %get-tuple-element.30), channel_id=1, source_target_pairs={{0,4},{4,0},{8,12},{12,8},{1,5},{5,1},{9,13},{13,9},{2,6},{6,2},{1... | collective-permute-start | bytes 294920 | tf_op jit(solution)/shard_map/ppermute | solution.py:327
  18.7 7.9 %collective-permute-start.3 = (bf16[256,384]{1,0:T(8,128)(2,1)S(1)}, bf16[256,384]{1,0:T(8,128)(2,1)S(1)}, u32[]{:S(2)}, u32[]{:S(2)}) collective-permute-start(bf16[256,384]{1,0:T(8,128)(2,1)S(1)} %slice.21), channel_id=1, source_target_pairs={{0,16},{16,0},{1,17},{17,1},{2,18},{18,2},{3,19},{19,3},{4,20},{20... | collective-permute-start | bytes 589832 | tf_op jit(solution)/shard_map/ppermute | solution.py:327
  20.3 6.3 %copy-start.1 = (bf16[256,384]{1,0:T(8,128)(2,1)S(1)}, bf16[256,384]{1,0:T(8,128)(2,1)}, u32[]{:S(2)}) copy-start(bf16[256,384]{1,0:T(8,128)(2,1)} %w0.1) | copy-start | bytes 589828
  20.3 4.3 %collective-permute-start.7 = (bf16[128,256]{1,0:T(8,128)(2,1)S(1)}, bf16[128,256]{1,0:T(8,128)(2,1)S(1)}, u32[]{:S(2)}, u32[]{:S(2)}) collective-permute-start(bf16[128,256]{1,0:T(8,128)(2,1)S(1)} %slice.24), channel_id=1, source_target_pairs={{0,2},{1,3},{2,0},{3,1},{4,6},{5,7},{6,4},{7,5},{8,10},{9,11},{10,... | collective-permute-start | bytes 196616 | tf_op jit(solution)/shard_map/ppermute | solution.py:327
  22.0 4.6 %collective-permute-start.4 = (bf16[128,384]{1,0:T(8,128)(2,1)S(1)}, bf16[128,384]{1,0:T(8,128)(2,1)S(1)}, u32[]{:S(2)}, u32[]{:S(2)}) collective-permute-start(bf16[128,384]{1,0:T(8,128)(2,1)S(1)} %collective-permute-done.2.far), channel_id=1, source_target_pairs={{0,16},{16,0},{1,17},{17,1},{2,18},{18,2},{3,19},{19,3},{4,20},{20... | collective-permute-start | bytes 294920 | tf_op jit(solution)/shard_map/ppermute | solution.py:327
  24.7 2.0 %copy-start = (bf16[128,1024]{1,0:T(8,128)(2,1)S(1)}, bf16[128,1024]{1,0:T(8,128)(2,1)}, u32[]{:S(2)}) copy-start(bf16[128,1024]{1,0:T(8,128)(2,1)} %refs_2_.1) | copy-start | bytes 786436
  24.7 2.0 %copy-start.2 = (bf16[128,128]{1,0:T(8,128)(2,1)S(1)}, bf16[128,128]{1,0:T(8,128)(2,1)}, u32[]{:S(2)}) copy-start(bf16[128,128]{1,0:T(8,128)(2,1)} %refs_3_.1) | copy-start | bytes 98308
  24.7 2.0 %copy-start.3 = (s32[4,4]{1,0:T(4,128)S(1)}, s32[4,4]{1,0:T(4,128)}, u32[]{:S(2)}) copy-start(s32[4,4]{1,0:T(4,128)} %refs_0_.1) | copy-start | bytes 196
  24.7 2.0 %copy-start.4 = (s32[4]{0:T(128)S(1)}, s32[4]{0:T(128)}, u32[]{:S(2)}) copy-start(s32[4]{0:T(128)} %refs_1_.1) | copy-start | bytes 52
  24.7 2.0 %collective-permute-start.8 = (bf16[768,256]{1,0:T(8,128)(2,1)S(1)}, bf16[768,256]{1,0:T(8,128)(2,1)S(1)}, u32[]{:S(2)}, u32[]{:S(2)}) collective-permute-start(bf16[768,256]{1,0:T(8,128)(2,1)S(1)} %pad_maximum_fusion), channel_id=1, source_target_pairs={{0,1},{1,0},{2,3},{3,2},{4,5},{5,4},{6,7},{7,6},{8,9},{9,8},{10,11... | collective-permute-start | bytes 1179656 | tf_op jit(solution)/shard_map/ppermute | solution.py:327
  30.7 4.4 %collective-permute-start.9 = (bf16[128,256]{1,0:T(8,128)(2,1)S(1)}, bf16[128,256]{1,0:T(8,128)(2,1)S(1)}, u32[]{:S(2)}, u32[]{:S(2)}) collective-permute-start(bf16[128,256]{1,0:T(8,128)(2,1)S(1)} %get-tuple-element.25), channel_id=1, source_target_pairs={{0,1},{1,0},{2,3},{3,2},{4,5},{5,4},{6,7},{7,6},{8,9},{9,8},{10,11... | collective-permute-start | bytes 196616 | tf_op jit(solution)/shard_map/ppermute | solution.py:327
  30.7 4.5 %collective-permute-start.10 = (bf16[128,256]{1,0:T(8,128)(2,1)S(1)}, bf16[128,256]{1,0:T(8,128)(2,1)S(1)}, u32[]{:S(2)}, u32[]{:S(2)}) collective-permute-start(bf16[128,256]{1,0:T(8,128)(2,1)S(1)} %get-tuple-element.26), channel_id=1, source_target_pairs={{0,2},{1,3},{2,0},{3,1},{4,6},{5,7},{6,4},{7,5},{8,10},{9,11},{10,... | collective-permute-start | bytes 196616 | tf_op jit(solution)/shard_map/ppermute | solution.py:327
  32.3 4.1 %collective-permute-start.11 = (bf16[128,256]{1,0:T(8,128)(2,1)S(1)}, bf16[128,256]{1,0:T(8,128)(2,1)S(1)}, u32[]{:S(2)}, u32[]{:S(2)}) collective-permute-start(bf16[128,256]{1,0:T(8,128)(2,1)S(1)} %get-tuple-element.27), channel_id=1, source_target_pairs={{0,3},{1,2},{2,1},{3,0},{4,7},{5,6},{6,5},{7,4},{8,11},{9,10},{10,... | collective-permute-start | bytes 196616 | tf_op jit(solution)/shard_map/ppermute | solution.py:327

commit v4 on v3

--- a/solution.py
+++ b/solution.py
@@ -160,30 +160,36 @@
 def heads_kernel(slots, refs_of, where, *refs):
     named = dict(zip(refs_of, refs))
     covis, drive = named["covis"], named["drive"]
-    t_all, w_all = named["t_all"], named["w_all"]
+    w_all = named["w_all"]
     rows = BLOCK
     length = slots * rows
     z = lax.axis_index("seq")
     f = lax.axis_index("fsdp")
     depth = w_all.shape[0] // slots
-    quarter = t_all.shape[1] // 4
-
-    t_all[0:rows, :] = named["t0"][...]
+    quarter = depth
+
     width = w_all.shape[1]
     grads = [named["g0"][...]]
+    pieces = [
+        [named["t0"][:, pl.ds(pl.multiple_of((f ^ m) * quarter, quarter), quarter)]]
+        for m in range(4)
+    ]
     for k in range(1, slots):
         name, at, off = where[k, "t"]
         tg = named[name].at[pl.ds(at, rows), :]
-        pieces = [tg[:, off : off + quarter]]
+        pieces[0].append(tg[:, off : off + quarter])
         for m in range(1, 4):
             name, at = where[k, m]
-            pieces.append(named[name][pl.ds(at, rows), :])
-        for m, piece in enumerate(pieces):
-            columns = pl.ds(pl.multiple_of((f ^ m) * quarter, quarter), quarter)
-            t_all[pl.ds(k * rows, rows), columns] = piece
+            pieces[m].append(named[name][pl.ds(at, rows), :])
         grads.append(tg[:, off + quarter :])
     grads = jnp.concatenate(grads, axis=0)
-    projected = dot(t_all[...], w_all[...]).astype(BF)
+    projected = None
+    for m in range(4):
+        piece = jnp.concatenate(pieces[m], axis=0)
+        named["pieces"][m] = piece
+        term = dot(piece, w_all[pl.ds(pl.multiple_of((f ^ m) * quarter, quarter), quarter), :])
+        projected = term if projected is None else projected + term
+    projected = projected.astype(BF)
     grads_t = jnp.transpose(grads)
 
     bias = {}
@@ -195,36 +201,50 @@
 
     heads = width // (3 * HD)
     scale = HD ** (-0.5)
-    bias_rows = [
-        jnp.concatenate([jnp.full((1, rows), bias[a, b], F32) for a in range(slots)], axis=1)
-        for b in range(slots)
-    ]
+    lane = lax.broadcasted_iota(jnp.int32, (rows, HD), 1)
+    mark = [jnp.where(lane == b, 1.0, 0.0).astype(BF) for b in range(slots)]
+    mark = jnp.concatenate(mark, axis=0)
+    cost = []
+    for a in range(slots):
+        block = jnp.zeros((rows, HD), F32)
+        for b in range(slots):
+            block = jnp.where(lane == b, bias[a, b], block)
+        cost.append(block.astype(BF))
+    cost = jnp.concatenate(cost, axis=0)
     own = []
+    state = []
     for h in range(heads):
         q8, k_h, v_h = split_heads(projected, h)
         g_h = grads[:, HD * h : HD * (h + 1)]
         g_t = grads_t[HD * h : HD * (h + 1), :]
-        s_t = dot_nt(k_h, q8)
-        s_t = jnp.concatenate(
-            [s_t[b * rows : (b + 1) * rows] + bias_rows[b] for b in range(slots)], axis=0
+        s_t = dot_nt(
+            jnp.concatenate([k_h, mark], axis=1), jnp.concatenate([q8, cost], axis=1)
         )
+        state.append((q8, k_h, v_h, g_h, g_t, s_t))
+    more = []
+    for h in range(heads):
+        s_t = state[h][-1]
         top = jnp.max(s_t, axis=0, keepdims=True)
         e_t = jnp.exp(s_t - top)
         total = jnp.sum(e_t, axis=0, keepdims=True)
         p_t = e_t * (1.0 / total)
         p_b = p_t.astype(BF)
         p_rest = (p_t - p_b.astype(F32)).astype(BF)
-        v_t = jnp.transpose(v_h)
-        o_t = (dot(v_t, p_b) + dot(v_t, p_rest)).astype(BF)
-        grad_dot = jnp.sum(g_t.astype(F32) * o_t.astype(F32), axis=0, keepdims=True)
         named["p_b"][h] = p_b
         named["p_rest"][h] = p_rest
+        v_t = jnp.transpose(state[h][2])
+        o_t = (dot(v_t, p_b) + dot(v_t, p_rest)).astype(BF)
+        more.append((p_t[:, 0:rows], p_t[0:rows], p_b[0:rows], o_t))
+    for h in range(heads):
+        q8, k_h, v_h, g_h, g_t, _ = state[h]
+        p_q, p_k, p_bk, o_t = more[h]
+        grad_dot = jnp.sum(g_t.astype(F32) * o_t.astype(F32), axis=0, keepdims=True)
         named["grad_dot"][h] = grad_dot
         named["attention_t"][HD * h : HD * (h + 1), :] = o_t[:, 0:rows]
-        ds_q = (p_t[:, 0:rows] * (dot_nt(v_h, g_h[0:rows]) - grad_dot[:, 0:rows])).astype(BF)
-        ds_k = (p_t[0:rows] * (dot_nt(v_h[0:rows], g_h) - grad_dot)).astype(BF)
+        ds_q = (p_q * (dot_nt(v_h, g_h[0:rows]) - grad_dot[:, 0:rows])).astype(BF)
+        ds_k = (p_k * (dot_nt(v_h[0:rows], g_h) - grad_dot)).astype(BF)
         d_q = jnp.transpose(dot(jnp.transpose(k_h), ds_q)) * scale
-        own += [d_q, dot(ds_k, q8), dot(p_b[0:rows], g_h)]
+        own += [d_q, dot(ds_k, q8), dot(p_bk, g_h)]
     own = jnp.concatenate(own, axis=1).astype(BF)
     for m in range(4):
         out = named["part%d" % m]
@@ -232,7 +252,6 @@
         out[...] = dot_nt(own, w_rows).astype(out.dtype)
     named["projected"][...] = projected
     named["grads"][...] = grads
-    named["t_d"][...] = t_all[:, pl.ds(pl.multiple_of(z * depth, depth), depth)]
 
 
 def split_heads(projected, h):
@@ -256,7 +275,7 @@
         columns += [d_q, dot(ds_t, q8), dot(p_b, g_h)]
     grad_qkv = jnp.concatenate(columns, axis=1).astype(BF)
     token_scale = grads.shape[0] ** (-0.5)
-    weight[...] = dot(jnp.transpose(t_d[...]), grad_qkv) * token_scale
+    weight[...] = dot(jnp.transpose(t_d[lax.axis_index("fsdp") ^ lax.axis_index("seq")]), grad_qkv) * token_scale
     attention[...] = jnp.transpose(attention_t[...])
 
 
@@ -369,15 +388,13 @@
         ("attention_t", (heads * HD, rows), BF),
         ("projected", (length, width), BF),
         ("grads", (length, heads * HD), BF),
-        ("t_d", (length, depth), BF),
+        ("pieces", (4, length, depth), BF),
         ("part0", (rows, depth), F32),
         ("part1", (rows, depth), BF),
         ("part2", (rows, depth), BF),
         ("part3", (rows, depth), BF),
     ]
-    scratch = [
-        ("t_all", pltpu.VMEM((rows * slots, features), BF)),
-    ]
+    scratch = []
     vmem = pl.BlockSpec(memory_space=pltpu.VMEM)
     smem = pl.BlockSpec(memory_space=pltpu.SMEM)
     refs_of = names + [n for n, _, _ in outs] + [n for n, _ in scratch]

time: 37.2 us -> 36.9 us (level)
  Pallas kernels: 7.41 us -> 7.03 us
where the time goes in v4:
time: 36.9 us; the launch traced here: 36.7 us
  starting transfers between devices  16.2 us (44%)
  waiting for transfers between devices  11.9 us (32%)
  Pallas kernels  7.03 us (19%)
  between operations  0.79 us (2%)
  other arithmetic  0.69 us (2%)
    ppermute x12, starting transfers between devices, swap(): return lax.ppermute(x, axis, [(i, i ^ bit) for i in range(n)])  16.2 us
    ppermute x12, waiting for transfers between devices, swap(): return lax.ppermute(x, axis, [(i, i ^ bit) for i in range(n)])  11.9 us
    pallas_call x1, Pallas kernels, short(): pl.pallas_call(functools.partial(heads_kernel, slots, refs_of, where), ou...  3.55 us
    pallas_call x1, Pallas kernels, short(): pl.pallas_call(rest_kernel, out_shape=[jax.ShapeDtypeStruct(grad_out.shap...  2.46 us
    pallas_call x1, Pallas kernels, pack(): pl.pallas_call(pack_kernel, out_shape=pltpu.VMEM((rows, columns), BF), in...  0.94 us
  transfers between devices with their start and end apart: 12, of which 5 were waited for; matrix products, arithmetic and copies ran while one was open for 0% of the time, Pallas kernels for 7%

profile of v4, /device:TPU:0, one launch (start us, length us, event | category | flops | bytes accessed | tf_op | source)
XLA Modules:
  0.0 36.7 jit_solution(179845911311882187)
XLA Ops:
  0.6 0.9 %pack.1 = bf16[128,768]{1,0:T(8,128)(2,1)S(1)} custom-call(bf16[256,384]{1,0:T(8,128)(2,1)} %w0.1, bf16[128,1024]{1,0:T(8,128)(2,1)} %refs_2_.1, bf16[128,128]{1,0:T(8,128)(2,1)} %refs_3_.1), custom_call_target="tpu_custom_call" | custom-call | tf_op jit(solution)/shard_map/pack/pallas_call | solution.py:324
  1.6 4.1 %collective-permute-start.1 = (bf16[128,768]{1,0:T(8,128)(2,1)S(1)}, bf16[128,768]{1,0:T(8,128)(2,1)S(1)}, u32[]{:S(2)}, u32[]{:S(2)}) collective-permute-start(bf16[128,768]{1,0:T(8,128)(2,1)S(1)} %pack.1), channel_id=1, source_target_pairs={{0,8},{4,12},{8,0},{12,4},{1,9},{5,13},{9,1},{13,5},{2,10},{6,14},... | collective-permute-start | bytes 589832 | tf_op jit(solution)/shard_map/ppermute | solution.py:346
  5.7 1.6 %collective-permute-start = (bf16[128,768]{1,0:T(8,128)(2,1)S(1)}, bf16[128,768]{1,0:T(8,128)(2,1)S(1)}, u32[]{:S(2)}, u32[]{:S(2)}) collective-permute-start(bf16[128,768]{1,0:T(8,128)(2,1)S(1)} %pack.1), channel_id=1, source_target_pairs={{0,4},{4,0},{8,12},{12,8},{1,5},{5,1},{9,13},{13,9},{2,6},{6,2},{1... | collective-permute-start | bytes 589832 | tf_op jit(solution)/shard_map/ppermute | solution.py:346
  7.3 7.6 %collective-permute-done.1 = bf16[128,768]{1,0:T(8,128)(2,1)S(1)} collective-permute-done((bf16[128,768]{1,0:T(8,128)(2,1)S(1)}, bf16[128,768]{1,0:T(8,128)(2,1)S(1)}, u32[]{:S(2)}, u32[]{:S(2)}) %collective-permute-start.1) | collective-permute-done | bytes 196640 | tf_op jit(solution)/shard_map/ppermute | solution.py:346
  14.9 0.7 %collective-permute-start.5 = (bf16[128,384]{1,0:T(8,128)(2,1)S(1)}, bf16[128,384]{1,0:T(8,128)(2,1)S(1)}, u32[]{:S(2)}, u32[]{:S(2)}) collective-permute-start(bf16[128,384]{1,0:T(8,128)(2,1)S(1)} %get-tuple-element.29), channel_id=1, source_target_pairs={{0,4},{4,0},{8,12},{12,8},{1,5},{5,1},{9,13},{13,9},{2,6},{6,2},{1... | collective-permute-start | bytes 294920 | tf_op jit(solution)/shard_map/ppermute | solution.py:346
  15.6 0.0 collective-permute-done
  15.7 1.6 %collective-permute-start.6 = (bf16[256,256]{1,0:T(8,128)(2,1)S(1)}, bf16[256,256]{1,0:T(8,128)(2,1)S(1)}, u32[]{:S(2)}, u32[]{:S(2)}) collective-permute-start(bf16[256,256]{1,0:T(8,128)(2,1)S(1)} %slice.23), channel_id=1, source_target_pairs={{0,2},{1,3},{2,0},{3,1},{4,6},{5,7},{6,4},{7,5},{8,10},{9,11},{10,... | collective-permute-start | bytes 393224 | tf_op jit(solution)/shard_map/ppermute | solution.py:346
  17.2 1.5 %collective-permute-start.2 = (bf16[128,384]{1,0:T(8,128)(2,1)S(1)}, bf16[128,384]{1,0:T(8,128)(2,1)S(1)}, u32[]{:S(2)}, u32[]{:S(2)}) collective-permute-start(bf16[128,384]{1,0:T(8,128)(2,1)S(1)} %get-tuple-element.30), channel_id=1, source_target_pairs={{0,4},{4,0},{8,12},{12,8},{1,5},{5,1},{9,13},{13,9},{2,6},{6,2},{1... | collective-permute-start | bytes 294920 | tf_op jit(solution)/shard_map/ppermute | solution.py:346
  18.7 1.6 %collective-permute-start.3 = (bf16[256,384]{1,0:T(8,128)(2,1)S(1)}, bf16[256,384]{1,0:T(8,128)(2,1)S(1)}, u32[]{:S(2)}, u32[]{:S(2)}) collective-permute-start(bf16[256,384]{1,0:T(8,128)(2,1)S(1)} %slice.21), channel_id=1, source_target_pairs={{0,16},{16,0},{1,17},{17,1},{2,18},{18,2},{3,19},{19,3},{4,20},{20... | collective-permute-start | bytes 589832 | tf_op jit(solution)/shard_map/ppermute | solution.py:346
  20.3 0.0 collective-permute-done.5.refs_6_
  20.3 0.0 copy-start.1
  20.3 1.7 %collective-permute-start.7 = (bf16[128,256]{1,0:T(8,128)(2,1)S(1)}, bf16[128,256]{1,0:T(8,128)(2,1)S(1)}, u32[]{:S(2)}, u32[]{:S(2)}) collective-permute-start(bf16[128,256]{1,0:T(8,128)(2,1)S(1)} %slice.24), channel_id=1, source_target_pairs={{0,2},{1,3},{2,0},{3,1},{4,6},{5,7},{6,4},{7,5},{8,10},{9,11},{10,... | collective-permute-start | bytes 196616 | tf_op jit(solution)/shard_map/ppermute | solution.py:346
  22.0 0.0 collective-permute-done.2.far
  22.0 1.5 %collective-permute-start.4 = (bf16[128,384]{1,0:T(8,128)(2,1)S(1)}, bf16[128,384]{1,0:T(8,128)(2,1)S(1)}, u32[]{:S(2)}, u32[]{:S(2)}) collective-permute-start(bf16[128,384]{1,0:T(8,128)(2,1)S(1)} %collective-permute-done.2.far), channel_id=1, source_target_pairs={{0,16},{16,0},{1,17},{17,1},{2,18},{18,2},{3,19},{19,3},{4,20},{20... | collective-permute-start | bytes 294920 | tf_op jit(solution)/shard_map/ppermute | solution.py:346
  23.5 0.0 collective-permute-done.6.refs_7_
  23.5 1.1 %collective-permute-done.7.refs_8_ = bf16[128,256]{1,0:T(8,128)(2,1)S(1)} collective-permute-done((bf16[128,256]{1,0:T(8,128)(2,1)S(1)}, bf16[128,256]{1,0:T(8,128)(2,1)S(1)}, u32[]{:S(2)}, u32[]{:S(2)}) %collective-permute-start.7) | collective-permute-done | bytes 65568 | tf_op jit(solution)/shard_map/ppermute | solution.py:346
  24.7 0.0 copy-start
  24.7 0.0 copy-start.2
  24.7 0.0 copy-start.3
  24.7 0.0 copy-start.4
  24.7 0.1 collective-permute-start.8
  24.8 1.8 %collective-permute-done.4.far_half = bf16[128,384]{1,0:T(8,128)(2,1)S(1)} collective-permute-done((bf16[128,384]{1,0:T(8,128)(2,1)S(1)}, bf16[128,384]{1,0:T(8,128)(2,1)S(1)}, u32[]{:S(2)}, u32[]{:S(2)}) %collective-permute-start.4) | collective-permute-done | bytes 98336 | tf_op jit(solution)/shard_map/ppermute | solution.py:346
  26.6 0.0 collective-permute-done.3.near_half
  26.6 0.0 copy-done.1
  26.6 0.1 weight.1.refs_4_
  26.7 0.0 collective-permute-done.8.refs_9_
  26.7 0.0 copy-done
  26.7 0.0 copy-done.2
  26.7 0.0 copy-done.3
  26.7 0.0 copy-done.4
  26.8 3.5 %heads.1 = (bf16[2,512,512]{2,1,0:T(8,128)(2,1)S(1)}, bf16[2,512,512]{2,1,0:T(8,128)(2,1)S(1)}, f32[2,1,512]{2,1,0:T(1,128)S(1)}, bf16[128,128]{1,0:T(8,128)(2,1...) custom-call(s32[4,4]{1,0:T(4,128)S(1)} %copy-done.3, ...), custom_call_target="tpu_custom_call" | custom-call | tf_op jit(solution)/shard_map/heads/pallas_call | solution.py:401
  30.3 0.1 collective-permute-start.9
  30.4 1.5 %collective-permute-start.10 = (bf16[128,256]{1,0:T(8,128)(2,1)S(1)}, bf16[128,256]{1,0:T(8,128)(2,1)S(1)}, u32[]{:S(2)}, u32[]{:S(2)}) collective-permute-start(bf16[128,256]{1,0:T(8,128)(2,1)S(1)} %get-tuple-element.26), channel_id=1, source_target_pairs={{0,2},{1,3},{2,0},{3,1},{4,6},{5,7},{6,4},{7,5},{8,10},{9,11},{10,... | collective-permute-start | bytes 196616 | tf_op jit(solution)/shard_map/ppermute | solution.py:346
  31.9 0.3 collective-permute-start.11
  32.2 2.5 %rest.1 = (bf16[128,128]{1,0:T(8,128)(2,1)}, f32[256,384]{1,0:T(8,128)}) custom-call(bf16[2,512,512]{2,1,0:T(8,128)(2,1)S(1)} %get-tuple-element.16.p_b_ref, bf16[2,512,512]{2,1,0:T(8,128)(2,1)S(1)} %get-tuple-element.17.p_rest_ref, f32[2,1,512]{2,1,0:T(1,128)S(1)} %get-tuple-element.18.grad_dot_ref, bf16[128,128]{1,0:T(8,128)(2,1)S(1)} %get-tuple-element.19.attention_t, ...), custom_call_target="tpu_custom_call" | custom-call | tf_op jit(solution)/shard_map/rest/pallas_call | solution.py:414
  34.7 0.0 collective-permute-done.9
  34.7 0.2 collective-permute-done.10
  34.9 1.1 %collective-permute-done.11 = bf16[128,256]{1,0:T(8,128)(2,1)S(1)} collective-permute-done((bf16[128,256]{1,0:T(8,128)(2,1)S(1)}, bf16[128,256]{1,0:T(8,128)(2,1)S(1)}, u32[]{:S(2)}, u32[]{:S(2)}) %collective-permute-start.11) | collective-permute-done | bytes 65568 | tf_op jit(solution)/shard_map/ppermute | solution.py:346
  36.0 0.7 %add_convert_fusion = bf16[128,256]{1,0:T(8,128)(2,1)} fusion(bf16[128,256]{1,0:T(8,128)(2,1)S(1)} %collective-permute-done.11, bf16[128,256]{1,0:T(8,128)(2,1)S(1)} %collective-permute-done.10, f32[128,256]{1,0:T(8,128)S(1)} %get-tuple-element.24, bf16[128,256]{1,0:T(8,128)(2,1)S(1)} %collective-permute-done.9), kind=kLoop, calls=%fused_computation.1 | loop fusion | flops 229376 | bytes 393216 | tf_op jit(solution)/shard_map/convert_element_type | solution.py:413
  (7 shorter events, 0.1 us)
Async XLA Ops:
  1.6 13.3 %collective-permute-start.1 = (bf16[128,768]{1,0:T(8,128)(2,1)S(1)}, bf16[128,768]{1,0:T(8,128)(2,1)S(1)}, u32[]{:S(2)}, u32[]{:S(2)}) collective-permute-start(bf16[128,768]{1,0:T(8,128)(2,1)S(1)} %pack.1), channel_id=1, source_target_pairs={{0,8},{4,12},{8,0},{12,4},{1,9},{5,13},{9,1},{13,5},{2,10},{6,14},... | collective-permute-start | bytes 589832 | tf_op jit(solution)/shard_map/ppermute | solution.py:346
  5.7 9.9 %collective-permute-start = (bf16[128,768]{1,0:T(8,128)(2,1)S(1)}, bf16[128,768]{1,0:T(8,128)(2,1)S(1)}, u32[]{:S(2)}, u32[]{:S(2)}) collective-permute-start(bf16[128,768]{1,0:T(8,128)(2,1)S(1)} %pack.1), channel_id=1, source_target_pairs={{0,4},{4,0},{8,12},{12,8},{1,5},{5,1},{9,13},{13,9},{2,6},{6,2},{1... | collective-permute-start | bytes 589832 | tf_op jit(solution)/shard_map/ppermute | solution.py:346
  14.9 5.4 %collective-permute-start.5 = (bf16[128,384]{1,0:T(8,128)(2,1)S(1)}, bf16[128,384]{1,0:T(8,128)(2,1)S(1)}, u32[]{:S(2)}, u32[]{:S(2)}) collective-permute-start(bf16[128,384]{1,0:T(8,128)(2,1)S(1)} %get-tuple-element.29), channel_id=1, source_target_pairs={{0,4},{4,0},{8,12},{12,8},{1,5},{5,1},{9,13},{13,9},{2,6},{6,2},{1... | collective-permute-start | bytes 294920 | tf_op jit(solution)/shard_map/ppermute | solution.py:346
  15.7 7.9 %collective-permute-start.6 = (bf16[256,256]{1,0:T(8,128)(2,1)S(1)}, bf16[256,256]{1,0:T(8,128)(2,1)S(1)}, u32[]{:S(2)}, u32[]{:S(2)}) collective-permute-start(bf16[256,256]{1,0:T(8,128)(2,1)S(1)} %slice.23), channel_id=1, source_target_pairs={{0,2},{1,3},{2,0},{3,1},{4,6},{5,7},{6,4},{7,5},{8,10},{9,11},{10,... | collective-permute-start | bytes 393224 | tf_op jit(solution)/shard_map/ppermute | solution.py:346
  17.2 4.8 %collective-permute-start.2 = (bf16[128,384]{1,0:T(8,128)(2,1)S(1)}, bf16[128,384]{1,0:T(8,128)(2,1)S(1)}, u32[]{:S(2)}, u32[]{:S(2)}) collective-permute-start(bf16[128,384]{1,0:T(8,128)(2,1)S(1)} %get-tuple-element.30), channel_id=1, source_target_pairs={{0,4},{4,0},{8,12},{12,8},{1,5},{5,1},{9,13},{13,9},{2,6},{6,2},{1... | collective-permute-start | bytes 294920 | tf_op jit(solution)/shard_map/ppermute | solution.py:346
  18.7 7.9 %collective-permute-start.3 = (bf16[256,384]{1,0:T(8,128)(2,1)S(1)}, bf16[256,384]{1,0:T(8,128)(2,1)S(1)}, u32[]{:S(2)}, u32[]{:S(2)}) collective-permute-start(bf16[256,384]{1,0:T(8,128)(2,1)S(1)} %slice.21), channel_id=1, source_target_pairs={{0,16},{16,0},{1,17},{17,1},{2,18},{18,2},{3,19},{19,3},{4,20},{20... | collective-permute-start | bytes 589832 | tf_op jit(solution)/shard_map/ppermute | solution.py:346
  20.3 6.3 %copy-start.1 = (bf16[256,384]{1,0:T(8,128)(2,1)S(1)}, bf16[256,384]{1,0:T(8,128)(2,1)}, u32[]{:S(2)}) copy-start(bf16[256,384]{1,0:T(8,128)(2,1)} %w0.1) | copy-start | bytes 589828
  20.3 4.3 %collective-permute-start.7 = (bf16[128,256]{1,0:T(8,128)(2,1)S(1)}, bf16[128,256]{1,0:T(8,128)(2,1)S(1)}, u32[]{:S(2)}, u32[]{:S(2)}) collective-permute-start(bf16[128,256]{1,0:T(8,128)(2,1)S(1)} %slice.24), channel_id=1, source_target_pairs={{0,2},{1,3},{2,0},{3,1},{4,6},{5,7},{6,4},{7,5},{8,10},{9,11},{10,... | collective-permute-start | bytes 196616 | tf_op jit(solution)/shard_map/ppermute | solution.py:346
  22.0 4.6 %collective-permute-start.4 = (bf16[128,384]{1,0:T(8,128)(2,1)S(1)}, bf16[128,384]{1,0:T(8,128)(2,1)S(1)}, u32[]{:S(2)}, u32[]{:S(2)}) collective-permute-start(bf16[128,384]{1,0:T(8,128)(2,1)S(1)} %collective-permute-done.2.far), channel_id=1, source_target_pairs={{0,16},{16,0},{1,17},{17,1},{2,18},{18,2},{3,19},{19,3},{4,20},{20... | collective-permute-start | bytes 294920 | tf_op jit(solution)/shard_map/ppermute | solution.py:346
  24.7 2.0 %copy-start = (bf16[128,1024]{1,0:T(8,128)(2,1)S(1)}, bf16[128,1024]{1,0:T(8,128)(2,1)}, u32[]{:S(2)}) copy-start(bf16[128,1024]{1,0:T(8,128)(2,1)} %refs_2_.1) | copy-start | bytes 786436
  24.7 2.0 %copy-start.2 = (bf16[128,128]{1,0:T(8,128)(2,1)S(1)}, bf16[128,128]{1,0:T(8,128)(2,1)}, u32[]{:S(2)}) copy-start(bf16[128,128]{1,0:T(8,128)(2,1)} %refs_3_.1) | copy-start | bytes 98308
  24.7 2.0 %copy-start.3 = (s32[4,4]{1,0:T(4,128)S(1)}, s32[4,4]{1,0:T(4,128)}, u32[]{:S(2)}) copy-start(s32[4,4]{1,0:T(4,128)} %refs_0_.1) | copy-start | bytes 196
  24.7 2.0 %copy-start.4 = (s32[4]{0:T(128)S(1)}, s32[4]{0:T(128)}, u32[]{:S(2)}) copy-start(s32[4]{0:T(128)} %refs_1_.1) | copy-start | bytes 52
  24.7 2.0 %collective-permute-start.8 = (bf16[768,256]{1,0:T(8,128)(2,1)S(1)}, bf16[768,256]{1,0:T(8,128)(2,1)S(1)}, u32[]{:S(2)}, u32[]{:S(2)}) collective-permute-start(bf16[768,256]{1,0:T(8,128)(2,1)S(1)} %pad_maximum_fusion), channel_id=1, source_target_pairs={{0,1},{1,0},{2,3},{3,2},{4,5},{5,4},{6,7},{7,6},{8,9},{9,8},{10,11... | collective-permute-start | bytes 1179656 | tf_op jit(solution)/shard_map/ppermute | solution.py:346
  30.3 4.4 %collective-permute-start.9 = (bf16[128,256]{1,0:T(8,128)(2,1)S(1)}, bf16[128,256]{1,0:T(8,128)(2,1)S(1)}, u32[]{:S(2)}, u32[]{:S(2)}) collective-permute-start(bf16[128,256]{1,0:T(8,128)(2,1)S(1)} %get-tuple-element.25), channel_id=1, source_target_pairs={{0,1},{1,0},{2,3},{3,2},{4,5},{5,4},{6,7},{7,6},{8,9},{9,8},{10,11... | collective-permute-start | bytes 196616 | tf_op jit(solution)/shard_map/ppermute | solution.py:346
  30.4 4.5 %collective-permute-start.10 = (bf16[128,256]{1,0:T(8,128)(2,1)S(1)}, bf16[128,256]{1,0:T(8,128)(2,1)S(1)}, u32[]{:S(2)}, u32[]{:S(2)}) collective-permute-start(bf16[128,256]{1,0:T(8,128)(2,1)S(1)} %get-tuple-element.26), channel_id=1, source_target_pairs={{0,2},{1,3},{2,0},{3,1},{4,6},{5,7},{6,4},{7,5},{8,10},{9,11},{10,... | collective-permute-start | bytes 196616 | tf_op jit(solution)/shard_map/ppermute | solution.py:346
  31.9 4.1 %collective-permute-start.11 = (bf16[128,256]{1,0:T(8,128)(2,1)S(1)}, bf16[128,256]{1,0:T(8,128)(2,1)S(1)}, u32[]{:S(2)}, u32[]{:S(2)}) collective-permute-start(bf16[128,256]{1,0:T(8,128)(2,1)S(1)} %get-tuple-element.27), channel_id=1, source_target_pairs={{0,3},{1,2},{2,1},{3,0},{4,7},{5,6},{6,5},{7,4},{8,11},{9,10},{10,... | collective-permute-start | bytes 196616 | tf_op jit(solution)/shard_map/ppermute | solution.py:346

commit v5 on v4

--- a/solution.py
+++ b/solution.py
@@ -265,14 +265,18 @@
 ):
     projected, grads = projected_ref[...], grads_ref[...]
     columns = []
-    for h in range(p_b_ref.shape[0]):
-        q8, k_h, v_h = split_heads(projected, h)
-        g_h = grads[:, HD * h : HD * (h + 1)]
-        p_b = p_b_ref[h]
-        p_t = p_b.astype(F32) + p_rest_ref[h].astype(F32)
-        ds_t = (p_t * (dot_nt(v_h, g_h) - grad_dot_ref[h])).astype(BF)
-        d_q = jnp.transpose(dot(jnp.transpose(k_h), ds_t)) * (HD ** (-0.5))
-        columns += [d_q, dot(ds_t, q8), dot(p_b, g_h)]
+    heads = range(p_b_ref.shape[0])
+    parts = [split_heads(projected, h) for h in heads]
+    cotangents = [grads[:, HD * h : HD * (h + 1)] for h in heads]
+    products = [dot_nt(parts[h][2], cotangents[h]) for h in heads]
+    slopes = []
+    for h in heads:
+        p_t = p_b_ref[h].astype(F32) + p_rest_ref[h].astype(F32)
+        slopes.append((p_t * (products[h] - grad_dot_ref[h])).astype(BF))
+    for h in heads:
+        q8, k_h, _ = parts[h]
+        d_q = jnp.transpose(dot(jnp.transpose(k_h), slopes[h])) * (HD ** (-0.5))
+        columns += [d_q, dot(slopes[h], q8), dot(p_b_ref[h], cotangents[h])]
     grad_qkv = jnp.concatenate(columns, axis=1).astype(BF)
     token_scale = grads.shape[0] ** (-0.5)
     weight[...] = dot(jnp.transpose(t_d[lax.axis_index("fsdp") ^ lax.axis_index("seq")]), grad_qkv) * token_scale
@@ -391,7 +395,7 @@
         ("pieces", (4, length, depth), BF),
         ("part0", (rows, depth), F32),
         ("part1", (rows, depth), BF),
-        ("part2", (rows, depth), BF),
+        ("part2", (rows, depth), F32),
         ("part3", (rows, depth), BF),
     ]
     scratch = []
@@ -404,13 +408,12 @@
         in_specs=[smem, smem] + [vmem] * (len(names) - 2),
         out_specs=[vmem] * len(outs),
         scratch_shapes=[s for _, s in scratch],
-        compiler_params=pltpu.CompilerParams(vmem_limit_bytes=48 << 20),
+        compiler_params=pltpu.CompilerParams(vmem_limit_bytes=16 << 20),
         name="heads",
     )(*values)
-    total = part0
-    for m, part in ((1, part1), (2, part2), (3, part3)):
-        total = total + swap(part, "fsdp", m).astype(F32)
-    grad_input = total.astype(BF)
+    pair = (part2 + swap(part3, "fsdp", 1).astype(F32)).astype(BF)
+    far = swap(pair, "fsdp", 2).astype(F32)
+    grad_input = (part0 + swap(part1, "fsdp", 1).astype(F32) + far).astype(BF)
     attention, grad_weight = pl.pallas_call(
         rest_kernel,
         out_shape=[
@@ -419,7 +422,7 @@
         ],
         in_specs=[vmem] * len(kept),
         out_specs=[vmem] * 2,
-        compiler_params=pltpu.CompilerParams(vmem_limit_bytes=48 << 20),
+        compiler_params=pltpu.CompilerParams(vmem_limit_bytes=16 << 20),
         name="rest",
     )(*kept)
     return attention, grad_input, grad_weight

time: 36.9 us -> 36.8 us (level)
  no operation moved by 1% of the time
where the time goes in v5:
time: 36.8 us; the launch traced here: 36.6 us
  starting transfers between devices  16.2 us (44%)
  waiting for transfers between devices  11.7 us (32%)
  Pallas kernels  7.03 us (19%)
  between operations  0.79 us (2%)
  other arithmetic  0.69 us (2%)
    ppermute x12, starting transfers between devices, swap(): return lax.ppermute(x, axis, [(i, i ^ bit) for i in range(n)])  16.2 us
    ppermute x12, waiting for transfers between devices, swap(): return lax.ppermute(x, axis, [(i, i ^ bit) for i in range(n)])  11.7 us
    pallas_call x1, Pallas kernels, short(): pl.pallas_call(functools.partial(heads_kernel, slots, refs_of, where), ou...  3.55 us
    pallas_call x1, Pallas kernels, short(): pl.pallas_call(rest_kernel, out_shape=[jax.ShapeDtypeStruct(grad_out.shap...  2.47 us
    pallas_call x1, Pallas kernels, pack(): pl.pallas_call(pack_kernel, out_shape=pltpu.VMEM((rows, columns), BF), in...  0.94 us
  transfers between devices with their start and end apart: 12, of which 5 were waited for; matrix products, arithmetic and copies ran while one was open for 0% of the time, Pallas kernels for 7%

profile of v5, /device:TPU:0, one launch (start us, length us, event | category | flops | bytes accessed | tf_op | source)
XLA Modules:
  0.0 36.6 jit_solution(2613530914317968323)
XLA Ops:
  0.6 0.9 %pack.1 = bf16[128,768]{1,0:T(8,128)(2,1)S(1)} custom-call(bf16[256,384]{1,0:T(8,128)(2,1)} %w0.1, bf16[128,1024]{1,0:T(8,128)(2,1)} %refs_2_.1, bf16[128,128]{1,0:T(8,128)(2,1)} %refs_3_.1), custom_call_target="tpu_custom_call" | custom-call | tf_op jit(solution)/shard_map/pack/pallas_call | solution.py:328
  1.6 4.1 %collective-permute-start.1 = (bf16[128,768]{1,0:T(8,128)(2,1)S(1)}, bf16[128,768]{1,0:T(8,128)(2,1)S(1)}, u32[]{:S(2)}, u32[]{:S(2)}) collective-permute-start(bf16[128,768]{1,0:T(8,128)(2,1)S(1)} %pack.1), channel_id=1, source_target_pairs={{0,8},{4,12},{8,0},{12,4},{1,9},{5,13},{9,1},{13,5},{2,10},{6,14},... | collective-permute-start | bytes 589832 | tf_op jit(solution)/shard_map/ppermute | solution.py:350
  5.7 1.6 %collective-permute-start = (bf16[128,768]{1,0:T(8,128)(2,1)S(1)}, bf16[128,768]{1,0:T(8,128)(2,1)S(1)}, u32[]{:S(2)}, u32[]{:S(2)}) collective-permute-start(bf16[128,768]{1,0:T(8,128)(2,1)S(1)} %pack.1), channel_id=1, source_target_pairs={{0,4},{4,0},{8,12},{12,8},{1,5},{5,1},{9,13},{13,9},{2,6},{6,2},{1... | collective-permute-start | bytes 589832 | tf_op jit(solution)/shard_map/ppermute | solution.py:350
  7.3 7.6 %collective-permute-done.1 = bf16[128,768]{1,0:T(8,128)(2,1)S(1)} collective-permute-done((bf16[128,768]{1,0:T(8,128)(2,1)S(1)}, bf16[128,768]{1,0:T(8,128)(2,1)S(1)}, u32[]{:S(2)}, u32[]{:S(2)}) %collective-permute-start.1) | collective-permute-done | bytes 196640 | tf_op jit(solution)/shard_map/ppermute | solution.py:350
  14.9 0.7 %collective-permute-start.5 = (bf16[128,384]{1,0:T(8,128)(2,1)S(1)}, bf16[128,384]{1,0:T(8,128)(2,1)S(1)}, u32[]{:S(2)}, u32[]{:S(2)}) collective-permute-start(bf16[128,384]{1,0:T(8,128)(2,1)S(1)} %get-tuple-element.29), channel_id=1, source_target_pairs={{0,4},{4,0},{8,12},{12,8},{1,5},{5,1},{9,13},{13,9},{2,6},{6,2},{1... | collective-permute-start | bytes 294920 | tf_op jit(solution)/shard_map/ppermute | solution.py:350
  15.6 0.0 collective-permute-done
  15.7 1.6 %collective-permute-start.6 = (bf16[256,256]{1,0:T(8,128)(2,1)S(1)}, bf16[256,256]{1,0:T(8,128)(2,1)S(1)}, u32[]{:S(2)}, u32[]{:S(2)}) collective-permute-start(bf16[256,256]{1,0:T(8,128)(2,1)S(1)} %slice.23), channel_id=1, source_target_pairs={{0,2},{1,3},{2,0},{3,1},{4,6},{5,7},{6,4},{7,5},{8,10},{9,11},{10,... | collective-permute-start | bytes 393224 | tf_op jit(solution)/shard_map/ppermute | solution.py:350
  17.2 1.5 %collective-permute-start.2 = (bf16[128,384]{1,0:T(8,128)(2,1)S(1)}, bf16[128,384]{1,0:T(8,128)(2,1)S(1)}, u32[]{:S(2)}, u32[]{:S(2)}) collective-permute-start(bf16[128,384]{1,0:T(8,128)(2,1)S(1)} %get-tuple-element.30), channel_id=1, source_target_pairs={{0,4},{4,0},{8,12},{12,8},{1,5},{5,1},{9,13},{13,9},{2,6},{6,2},{1... | collective-permute-start | bytes 294920 | tf_op jit(solution)/shard_map/ppermute | solution.py:350
  18.7 1.6 %collective-permute-start.3 = (bf16[256,384]{1,0:T(8,128)(2,1)S(1)}, bf16[256,384]{1,0:T(8,128)(2,1)S(1)}, u32[]{:S(2)}, u32[]{:S(2)}) collective-permute-start(bf16[256,384]{1,0:T(8,128)(2,1)S(1)} %slice.21), channel_id=1, source_target_pairs={{0,16},{16,0},{1,17},{17,1},{2,18},{18,2},{3,19},{19,3},{4,20},{20... | collective-permute-start | bytes 589832 | tf_op jit(solution)/shard_map/ppermute | solution.py:350
  20.3 0.0 collective-permute-done.5.refs_6_
  20.3 0.0 copy-start.1
  20.3 1.7 %collective-permute-start.7 = (bf16[128,256]{1,0:T(8,128)(2,1)S(1)}, bf16[128,256]{1,0:T(8,128)(2,1)S(1)}, u32[]{:S(2)}, u32[]{:S(2)}) collective-permute-start(bf16[128,256]{1,0:T(8,128)(2,1)S(1)} %slice.24), channel_id=1, source_target_pairs={{0,2},{1,3},{2,0},{3,1},{4,6},{5,7},{6,4},{7,5},{8,10},{9,11},{10,... | collective-permute-start | bytes 196616 | tf_op jit(solution)/shard_map/ppermute | solution.py:350
  22.0 0.0 collective-permute-done.2.far
  22.0 1.5 %collective-permute-start.4 = (bf16[128,384]{1,0:T(8,128)(2,1)S(1)}, bf16[128,384]{1,0:T(8,128)(2,1)S(1)}, u32[]{:S(2)}, u32[]{:S(2)}) collective-permute-start(bf16[128,384]{1,0:T(8,128)(2,1)S(1)} %collective-permute-done.2.far), channel_id=1, source_target_pairs={{0,16},{16,0},{1,17},{17,1},{2,18},{18,2},{3,19},{19,3},{4,20},{20... | collective-permute-start | bytes 294920 | tf_op jit(solution)/shard_map/ppermute | solution.py:350
  23.5 0.0 collective-permute-done.6.refs_7_
  23.5 1.1 %collective-permute-done.7.refs_8_ = bf16[128,256]{1,0:T(8,128)(2,1)S(1)} collective-permute-done((bf16[128,256]{1,0:T(8,128)(2,1)S(1)}, bf16[128,256]{1,0:T(8,128)(2,1)S(1)}, u32[]{:S(2)}, u32[]{:S(2)}) %collective-permute-start.7) | collective-permute-done | bytes 65568 | tf_op jit(solution)/shard_map/ppermute | solution.py:350
  24.7 0.0 copy-start
  24.7 0.0 copy-start.2
  24.7 0.0 copy-start.3
  24.7 0.0 copy-start.4
  24.7 0.1 collective-permute-start.8
  24.8 1.8 %collective-permute-done.4.far_half = bf16[128,384]{1,0:T(8,128)(2,1)S(1)} collective-permute-done((bf16[128,384]{1,0:T(8,128)(2,1)S(1)}, bf16[128,384]{1,0:T(8,128)(2,1)S(1)}, u32[]{:S(2)}, u32[]{:S(2)}) %collective-permute-start.4) | collective-permute-done | bytes 98336 | tf_op jit(solution)/shard_map/ppermute | solution.py:350
  26.6 0.0 collective-permute-done.3.near_half
  26.6 0.0 copy-done.1
  26.6 0.1 weight.1.refs_4_
  26.7 0.0 collective-permute-done.8.refs_9_
  26.7 0.0 copy-done
  26.7 0.0 copy-done.2
  26.7 0.0 copy-done.3
  26.7 0.0 copy-done.4
  26.8 3.5 %heads.1 = (bf16[2,512,512]{2,1,0:T(8,128)(2,1)S(1)}, bf16[2,512,512]{2,1,0:T(8,128)(2,1)S(1)}, f32[2,1,512]{2,1,0:T(1,128)S(1)}, bf16[128,128]{1,0:T(8,128)(2,1...) custom-call(s32[4,4]{1,0:T(4,128)S(1)} %copy-done.3, ...), custom_call_target="tpu_custom_call" | custom-call | tf_op jit(solution)/shard_map/heads/pallas_call | solution.py:405
  30.3 0.1 collective-permute-start.10
  30.4 0.5 %collective-permute-start.9 = (bf16[128,256]{1,0:T(8,128)(2,1)S(1)}, bf16[128,256]{1,0:T(8,128)(2,1)S(1)}, u32[]{:S(2)}, u32[]{:S(2)}) collective-permute-start(bf16[128,256]{1,0:T(8,128)(2,1)S(1)} %get-tuple-element.25), channel_id=1, source_target_pairs={{0,1},{1,0},{2,3},{3,2},{4,5},{5,4},{6,7},{7,6},{8,9},{9,8},{10,11... | collective-permute-start | bytes 196616 | tf_op jit(solution)/shard_map/ppermute | solution.py:350
  30.9 0.7 %collective-permute-done.10 = bf16[128,256]{1,0:T(8,128)(2,1)S(1)} collective-permute-done((bf16[128,256]{1,0:T(8,128)(2,1)S(1)}, bf16[128,256]{1,0:T(8,128)(2,1)S(1)}, u32[]{:S(2)}, u32[]{:S(2)}) %collective-permute-start.10) | collective-permute-done | bytes 65568 | tf_op jit(solution)/shard_map/ppermute | solution.py:350
  31.6 1.5 %collective-permute-start.11 = (bf16[128,256]{1,0:T(8,128)(2,1)S(1)}, bf16[128,256]{1,0:T(8,128)(2,1)S(1)}, u32[]{:S(2)}, u32[]{:S(2)}) collective-permute-start(bf16[128,256]{1,0:T(8,128)(2,1)S(1)} %add_convert_fusion.1), channel_id=1, source_target_pairs={{0,2},{1,3},{2,0},{3,1},{4,6},{5,7},{6,4},{7,5},{8,10},{9,11},{10,... | collective-permute-start | bytes 196616 | tf_op jit(solution)/shard_map/ppermute | solution.py:350
  33.1 2.5 %rest.1 = (bf16[128,128]{1,0:T(8,128)(2,1)}, f32[256,384]{1,0:T(8,128)}) custom-call(bf16[2,512,512]{2,1,0:T(8,128)(2,1)S(1)} %get-tuple-element.16.p_b_ref, bf16[2,512,512]{2,1,0:T(8,128)(2,1)S(1)} %get-tuple-element.17.p_rest_ref, f32[2,1,512]{2,1,0:T(1,128)S(1)} %get-tuple-element.18.grad_dot_ref, bf16[128,128]{1,0:T(8,128)(2,1)S(1)} %get-tuple-element.19.attention_t, ...), custom_call_target="tpu_custom_call" | custom-call | tf_op jit(solution)/shard_map/rest/pallas_call | solution.py:417
  35.6 0.0 collective-permute-done.9
  35.6 0.4 %collective-permute-done.11 = bf16[128,256]{1,0:T(8,128)(2,1)S(1)} collective-permute-done((bf16[128,256]{1,0:T(8,128)(2,1)S(1)}, bf16[128,256]{1,0:T(8,128)(2,1)S(1)}, u32[]{:S(2)}, u32[]{:S(2)}) %collective-permute-start.11) | collective-permute-done | bytes 65568 | tf_op jit(solution)/shard_map/ppermute | solution.py:350
  36.0 0.7 %add_convert_fusion = bf16[128,256]{1,0:T(8,128)(2,1)} fusion(bf16[128,256]{1,0:T(8,128)(2,1)S(1)} %collective-permute-done.11, f32[128,256]{1,0:T(8,128)S(1)} %get-tuple-element.24, bf16[128,256]{1,0:T(8,128)(2,1)S(1)} %collective-permute-done.9), kind=kLoop, calls=%fused_computation.1 | loop fusion | flops 163840 | bytes 327680 | tf_op jit(solution)/shard_map/convert_element_type | solution.py:416
  (8 shorter events, 0.1 us)
Async XLA Ops:
  1.6 13.3 %collective-permute-start.1 = (bf16[128,768]{1,0:T(8,128)(2,1)S(1)}, bf16[128,768]{1,0:T(8,128)(2,1)S(1)}, u32[]{:S(2)}, u32[]{:S(2)}) collective-permute-start(bf16[128,768]{1,0:T(8,128)(2,1)S(1)} %pack.1), channel_id=1, source_target_pairs={{0,8},{4,12},{8,0},{12,4},{1,9},{5,13},{9,1},{13,5},{2,10},{6,14},... | collective-permute-start | bytes 589832 | tf_op jit(solution)/shard_map/ppermute | solution.py:350
  5.7 9.9 %collective-permute-start = (bf16[128,768]{1,0:T(8,128)(2,1)S(1)}, bf16[128,768]{1,0:T(8,128)(2,1)S(1)}, u32[]{:S(2)}, u32[]{:S(2)}) collective-permute-start(bf16[128,768]{1,0:T(8,128)(2,1)S(1)} %pack.1), channel_id=1, source_target_pairs={{0,4},{4,0},{8,12},{12,8},{1,5},{5,1},{9,13},{13,9},{2,6},{6,2},{1... | collective-permute-start | bytes 589832 | tf_op jit(solution)/shard_map/ppermute | solution.py:350
  14.9 5.4 %collective-permute-start.5 = (bf16[128,384]{1,0:T(8,128)(2,1)S(1)}, bf16[128,384]{1,0:T(8,128)(2,1)S(1)}, u32[]{:S(2)}, u32[]{:S(2)}) collective-permute-start(bf16[128,384]{1,0:T(8,128)(2,1)S(1)} %get-tuple-element.29), channel_id=1, source_target_pairs={{0,4},{4,0},{8,12},{12,8},{1,5},{5,1},{9,13},{13,9},{2,6},{6,2},{1... | collective-permute-start | bytes 294920 | tf_op jit(solution)/shard_map/ppermute | solution.py:350
  15.7 7.9 %collective-permute-start.6 = (bf16[256,256]{1,0:T(8,128)(2,1)S(1)}, bf16[256,256]{1,0:T(8,128)(2,1)S(1)}, u32[]{:S(2)}, u32[]{:S(2)}) collective-permute-start(bf16[256,256]{1,0:T(8,128)(2,1)S(1)} %slice.23), channel_id=1, source_target_pairs={{0,2},{1,3},{2,0},{3,1},{4,6},{5,7},{6,4},{7,5},{8,10},{9,11},{10,... | collective-permute-start | bytes 393224 | tf_op jit(solution)/shard_map/ppermute | solution.py:350
  17.2 4.8 %collective-permute-start.2 = (bf16[128,384]{1,0:T(8,128)(2,1)S(1)}, bf16[128,384]{1,0:T(8,128)(2,1)S(1)}, u32[]{:S(2)}, u32[]{:S(2)}) collective-permute-start(bf16[128,384]{1,0:T(8,128)(2,1)S(1)} %get-tuple-element.30), channel_id=1, source_target_pairs={{0,4},{4,0},{8,12},{12,8},{1,5},{5,1},{9,13},{13,9},{2,6},{6,2},{1... | collective-permute-start | bytes 294920 | tf_op jit(solution)/shard_map/ppermute | solution.py:350
  18.7 7.9 %collective-permute-start.3 = (bf16[256,384]{1,0:T(8,128)(2,1)S(1)}, bf16[256,384]{1,0:T(8,128)(2,1)S(1)}, u32[]{:S(2)}, u32[]{:S(2)}) collective-permute-start(bf16[256,384]{1,0:T(8,128)(2,1)S(1)} %slice.21), channel_id=1, source_target_pairs={{0,16},{16,0},{1,17},{17,1},{2,18},{18,2},{3,19},{19,3},{4,20},{20... | collective-permute-start | bytes 589832 | tf_op jit(solution)/shard_map/ppermute | solution.py:350
  20.3 6.3 %copy-start.1 = (bf16[256,384]{1,0:T(8,128)(2,1)S(1)}, bf16[256,384]{1,0:T(8,128)(2,1)}, u32[]{:S(2)}) copy-start(bf16[256,384]{1,0:T(8,128)(2,1)} %w0.1) | copy-start | bytes 589828
  20.3 4.3 %collective-permute-start.7 = (bf16[128,256]{1,0:T(8,128)(2,1)S(1)}, bf16[128,256]{1,0:T(8,128)(2,1)S(1)}, u32[]{:S(2)}, u32[]{:S(2)}) collective-permute-start(bf16[128,256]{1,0:T(8,128)(2,1)S(1)} %slice.24), channel_id=1, source_target_pairs={{0,2},{1,3},{2,0},{3,1},{4,6},{5,7},{6,4},{7,5},{8,10},{9,11},{10,... | collective-permute-start | bytes 196616 | tf_op jit(solution)/shard_map/ppermute | solution.py:350
  22.0 4.6 %collective-permute-start.4 = (bf16[128,384]{1,0:T(8,128)(2,1)S(1)}, bf16[128,384]{1,0:T(8,128)(2,1)S(1)}, u32[]{:S(2)}, u32[]{:S(2)}) collective-permute-start(bf16[128,384]{1,0:T(8,128)(2,1)S(1)} %collective-permute-done.2.far), channel_id=1, source_target_pairs={{0,16},{16,0},{1,17},{17,1},{2,18},{18,2},{3,19},{19,3},{4,20},{20... | collective-permute-start | bytes 294920 | tf_op jit(solution)/shard_map/ppermute | solution.py:350
  24.7 2.0 %copy-start = (bf16[128,1024]{1,0:T(8,128)(2,1)S(1)}, bf16[128,1024]{1,0:T(8,128)(2,1)}, u32[]{:S(2)}) copy-start(bf16[128,1024]{1,0:T(8,128)(2,1)} %refs_2_.1) | copy-start | bytes 786436
  24.7 2.0 %copy-start.2 = (bf16[128,128]{1,0:T(8,128)(2,1)S(1)}, bf16[128,128]{1,0:T(8,128)(2,1)}, u32[]{:S(2)}) copy-start(bf16[128,128]{1,0:T(8,128)(2,1)} %refs_3_.1) | copy-start | bytes 98308
  24.7 2.0 %copy-start.3 = (s32[4,4]{1,0:T(4,128)S(1)}, s32[4,4]{1,0:T(4,128)}, u32[]{:S(2)}) copy-start(s32[4,4]{1,0:T(4,128)} %refs_0_.1) | copy-start | bytes 196
  24.7 2.0 %copy-start.4 = (s32[4]{0:T(128)S(1)}, s32[4]{0:T(128)}, u32[]{:S(2)}) copy-start(s32[4]{0:T(128)} %refs_1_.1) | copy-start | bytes 52
  24.7 2.0 %collective-permute-start.8 = (bf16[768,256]{1,0:T(8,128)(2,1)S(1)}, bf16[768,256]{1,0:T(8,128)(2,1)S(1)}, u32[]{:S(2)}, u32[]{:S(2)}) collective-permute-start(bf16[768,256]{1,0:T(8,128)(2,1)S(1)} %pad_maximum_fusion), channel_id=1, source_target_pairs={{0,1},{1,0},{2,3},{3,2},{4,5},{5,4},{6,7},{7,6},{8,9},{9,8},{10,11... | collective-permute-start | bytes 1179656 | tf_op jit(solution)/shard_map/ppermute | solution.py:350
  30.3 1.3 %collective-permute-start.10 = (bf16[128,256]{1,0:T(8,128)(2,1)S(1)}, bf16[128,256]{1,0:T(8,128)(2,1)S(1)}, u32[]{:S(2)}, u32[]{:S(2)}) collective-permute-start(bf16[128,256]{1,0:T(8,128)(2,1)S(1)} %get-tuple-element.27), channel_id=1, source_target_pairs={{0,1},{1,0},{2,3},{3,2},{4,5},{5,4},{6,7},{7,6},{8,9},{9,8},{10,11... | collective-permute-start | bytes 196616 | tf_op jit(solution)/shard_map/ppermute | solution.py:350
  30.4 5.2 %collective-permute-start.9 = (bf16[128,256]{1,0:T(8,128)(2,1)S(1)}, bf16[128,256]{1,0:T(8,128)(2,1)S(1)}, u32[]{:S(2)}, u32[]{:S(2)}) collective-permute-start(bf16[128,256]{1,0:T(8,128)(2,1)S(1)} %get-tuple-element.25), channel_id=1, source_target_pairs={{0,1},{1,0},{2,3},{3,2},{4,5},{5,4},{6,7},{7,6},{8,9},{9,8},{10,11... | collective-permute-start | bytes 196616 | tf_op jit(solution)/shard_map/ppermute | solution.py:350
  31.6 4.3 %collective-permute-start.11 = (bf16[128,256]{1,0:T(8,128)(2,1)S(1)}, bf16[128,256]{1,0:T(8,128)(2,1)S(1)}, u32[]{:S(2)}, u32[]{:S(2)}) collective-permute-start(bf16[128,256]{1,0:T(8,128)(2,1)S(1)} %add_convert_fusion.1), channel_id=1, source_target_pairs={{0,2},{1,3},{2,0},{3,1},{4,6},{5,7},{6,4},{7,5},{8,10},{9,11},{10,... | collective-permute-start | bytes 196616 | tf_op jit(solution)/shard_map/ppermute | solution.py:350

commit v6 on v5

--- a/solution.py
+++ b/solution.py
@@ -220,7 +220,10 @@
         s_t = dot_nt(
             jnp.concatenate([k_h, mark], axis=1), jnp.concatenate([q8, cost], axis=1)
         )
-        state.append((q8, k_h, v_h, g_h, g_t, s_t))
+        d_pq = dot_nt(v_h, g_h[0:rows])
+        d_pk = dot_nt(v_h[0:rows], g_h)
+        k_t, v_t = jnp.transpose(k_h), jnp.transpose(v_h)
+        state.append((q8, k_t, d_pq, d_pk, v_t, g_h, g_t, s_t))
     more = []
     for h in range(heads):
         s_t = state[h][-1]
@@ -232,18 +235,18 @@
         p_rest = (p_t - p_b.astype(F32)).astype(BF)
         named["p_b"][h] = p_b
         named["p_rest"][h] = p_rest
-        v_t = jnp.transpose(state[h][2])
+        v_t = state[h][4]
         o_t = (dot(v_t, p_b) + dot(v_t, p_rest)).astype(BF)
         more.append((p_t[:, 0:rows], p_t[0:rows], p_b[0:rows], o_t))
     for h in range(heads):
-        q8, k_h, v_h, g_h, g_t, _ = state[h]
+        q8, k_t, d_pq, d_pk, _, g_h, g_t, _ = state[h]
         p_q, p_k, p_bk, o_t = more[h]
         grad_dot = jnp.sum(g_t.astype(F32) * o_t.astype(F32), axis=0, keepdims=True)
         named["grad_dot"][h] = grad_dot
         named["attention_t"][HD * h : HD * (h + 1), :] = o_t[:, 0:rows]
-        ds_q = (p_q * (dot_nt(v_h, g_h[0:rows]) - grad_dot[:, 0:rows])).astype(BF)
-        ds_k = (p_k * (dot_nt(v_h[0:rows], g_h) - grad_dot)).astype(BF)
-        d_q = jnp.transpose(dot(jnp.transpose(k_h), ds_q)) * scale
+        ds_q = (p_q * (d_pq - grad_dot[:, 0:rows])).astype(BF)
+        ds_k = (p_k * (d_pk - grad_dot)).astype(BF)
+        d_q = jnp.transpose(dot(k_t, ds_q)) * scale
         own += [d_q, dot(ds_k, q8), dot(p_bk, g_h)]
     own = jnp.concatenate(own, axis=1).astype(BF)
     for m in range(4):

time: 36.8 us -> 36.5 us (level)
  no operation moved by 1% of the time
where the time goes in v6:
time: 36.5 us; the launch traced here: 36.3 us
  starting transfers between devices  16.3 us (45%)
  waiting for transfers between devices  11.7 us (32%)
  Pallas kernels  6.75 us (18%)
  between operations  0.79 us (2%)
  other arithmetic  0.69 us (2%)
    ppermute x12, starting transfers between devices, swap(): return lax.ppermute(x, axis, [(i, i ^ bit) for i in range(n)])  16.3 us
    ppermute x12, waiting for transfers between devices, swap(): return lax.ppermute(x, axis, [(i, i ^ bit) for i in range(n)])  11.7 us
    pallas_call x1, Pallas kernels, short(): pl.pallas_call(functools.partial(heads_kernel, slots, refs_of, where), ou...  3.27 us
    pallas_call x1, Pallas kernels, short(): pl.pallas_call(rest_kernel, out_shape=[jax.ShapeDtypeStruct(grad_out.shap...  2.47 us
    pallas_call x1, Pallas kernels, pack(): pl.pallas_call(pack_kernel, out_shape=pltpu.VMEM((rows, columns), BF), in...  0.94 us
  transfers between devices with their start and end apart: 12, of which 5 were waited for; matrix products, arithmetic and copies ran while one was open for 0% of the time, Pallas kernels for 7%

profile of v6, /device:TPU:0, one launch (start us, length us, event | category | flops | bytes accessed | tf_op | source)
XLA Modules:
  0.0 36.3 jit_solution(14716538192333254158)
XLA Ops:
  0.6 0.9 %pack.1 = bf16[128,768]{1,0:T(8,128)(2,1)S(1)} custom-call(bf16[256,384]{1,0:T(8,128)(2,1)} %w0.1, bf16[128,1024]{1,0:T(8,128)(2,1)} %refs_2_.1, bf16[128,128]{1,0:T(8,128)(2,1)} %refs_3_.1), custom_call_target="tpu_custom_call" | custom-call | tf_op jit(solution)/shard_map/pack/pallas_call | solution.py:331
  1.6 4.1 %collective-permute-start.1 = (bf16[128,768]{1,0:T(8,128)(2,1)S(1)}, bf16[128,768]{1,0:T(8,128)(2,1)S(1)}, u32[]{:S(2)}, u32[]{:S(2)}) collective-permute-start(bf16[128,768]{1,0:T(8,128)(2,1)S(1)} %pack.1), channel_id=1, source_target_pairs={{0,8},{4,12},{8,0},{12,4},{1,9},{5,13},{9,1},{13,5},{2,10},{6,14},... | collective-permute-start | bytes 589832 | tf_op jit(solution)/shard_map/ppermute | solution.py:353
  5.7 1.6 %collective-permute-start = (bf16[128,768]{1,0:T(8,128)(2,1)S(1)}, bf16[128,768]{1,0:T(8,128)(2,1)S(1)}, u32[]{:S(2)}, u32[]{:S(2)}) collective-permute-start(bf16[128,768]{1,0:T(8,128)(2,1)S(1)} %pack.1), channel_id=1, source_target_pairs={{0,4},{4,0},{8,12},{12,8},{1,5},{5,1},{9,13},{13,9},{2,6},{6,2},{1... | collective-permute-start | bytes 589832 | tf_op jit(solution)/shard_map/ppermute | solution.py:353
  7.3 7.6 %collective-permute-done.1 = bf16[128,768]{1,0:T(8,128)(2,1)S(1)} collective-permute-done((bf16[128,768]{1,0:T(8,128)(2,1)S(1)}, bf16[128,768]{1,0:T(8,128)(2,1)S(1)}, u32[]{:S(2)}, u32[]{:S(2)}) %collective-permute-start.1) | collective-permute-done | bytes 196640 | tf_op jit(solution)/shard_map/ppermute | solution.py:353
  14.9 0.7 %collective-permute-start.5 = (bf16[128,384]{1,0:T(8,128)(2,1)S(1)}, bf16[128,384]{1,0:T(8,128)(2,1)S(1)}, u32[]{:S(2)}, u32[]{:S(2)}) collective-permute-start(bf16[128,384]{1,0:T(8,128)(2,1)S(1)} %get-tuple-element.29), channel_id=1, source_target_pairs={{0,4},{4,0},{8,12},{12,8},{1,5},{5,1},{9,13},{13,9},{2,6},{6,2},{1... | collective-permute-start | bytes 294920 | tf_op jit(solution)/shard_map/ppermute | solution.py:353
  15.6 0.0 collective-permute-done
  15.7 1.6 %collective-permute-start.6 = (bf16[256,256]{1,0:T(8,128)(2,1)S(1)}, bf16[256,256]{1,0:T(8,128)(2,1)S(1)}, u32[]{:S(2)}, u32[]{:S(2)}) collective-permute-start(bf16[256,256]{1,0:T(8,128)(2,1)S(1)} %slice.23), channel_id=1, source_target_pairs={{0,2},{1,3},{2,0},{3,1},{4,6},{5,7},{6,4},{7,5},{8,10},{9,11},{10,... | collective-permute-start | bytes 393224 | tf_op jit(solution)/shard_map/ppermute | solution.py:353
  17.2 1.5 %collective-permute-start.2 = (bf16[128,384]{1,0:T(8,128)(2,1)S(1)}, bf16[128,384]{1,0:T(8,128)(2,1)S(1)}, u32[]{:S(2)}, u32[]{:S(2)}) collective-permute-start(bf16[128,384]{1,0:T(8,128)(2,1)S(1)} %get-tuple-element.30), channel_id=1, source_target_pairs={{0,4},{4,0},{8,12},{12,8},{1,5},{5,1},{9,13},{13,9},{2,6},{6,2},{1... | collective-permute-start | bytes 294920 | tf_op jit(solution)/shard_map/ppermute | solution.py:353
  18.7 1.6 %collective-permute-start.3 = (bf16[256,384]{1,0:T(8,128)(2,1)S(1)}, bf16[256,384]{1,0:T(8,128)(2,1)S(1)}, u32[]{:S(2)}, u32[]{:S(2)}) collective-permute-start(bf16[256,384]{1,0:T(8,128)(2,1)S(1)} %slice.21), channel_id=1, source_target_pairs={{0,16},{16,0},{1,17},{17,1},{2,18},{18,2},{3,19},{19,3},{4,20},{20... | collective-permute-start | bytes 589832 | tf_op jit(solution)/shard_map/ppermute | solution.py:353
  20.3 0.0 collective-permute-done.5.refs_6_
  20.3 0.0 copy-start.1
  20.3 1.7 %collective-permute-start.7 = (bf16[128,256]{1,0:T(8,128)(2,1)S(1)}, bf16[128,256]{1,0:T(8,128)(2,1)S(1)}, u32[]{:S(2)}, u32[]{:S(2)}) collective-permute-start(bf16[128,256]{1,0:T(8,128)(2,1)S(1)} %slice.24), channel_id=1, source_target_pairs={{0,2},{1,3},{2,0},{3,1},{4,6},{5,7},{6,4},{7,5},{8,10},{9,11},{10,... | collective-permute-start | bytes 196616 | tf_op jit(solution)/shard_map/ppermute | solution.py:353
  22.0 0.0 collective-permute-done.2.far
  22.0 1.5 %collective-permute-start.4 = (bf16[128,384]{1,0:T(8,128)(2,1)S(1)}, bf16[128,384]{1,0:T(8,128)(2,1)S(1)}, u32[]{:S(2)}, u32[]{:S(2)}) collective-permute-start(bf16[128,384]{1,0:T(8,128)(2,1)S(1)} %collective-permute-done.2.far), channel_id=1, source_target_pairs={{0,16},{16,0},{1,17},{17,1},{2,18},{18,2},{3,19},{19,3},{4,20},{20... | collective-permute-start | bytes 294920 | tf_op jit(solution)/shard_map/ppermute | solution.py:353
  23.5 0.0 collective-permute-done.6.refs_7_
  23.5 1.1 %collective-permute-done.7.refs_8_ = bf16[128,256]{1,0:T(8,128)(2,1)S(1)} collective-permute-done((bf16[128,256]{1,0:T(8,128)(2,1)S(1)}, bf16[128,256]{1,0:T(8,128)(2,1)S(1)}, u32[]{:S(2)}, u32[]{:S(2)}) %collective-permute-start.7) | collective-permute-done | bytes 65568 | tf_op jit(solution)/shard_map/ppermute | solution.py:353
  24.7 0.0 copy-start
  24.7 0.0 copy-start.2
  24.7 0.0 copy-start.3
  24.7 0.0 copy-start.4
  24.7 0.1 collective-permute-start.8
  24.8 1.8 %collective-permute-done.4.far_half = bf16[128,384]{1,0:T(8,128)(2,1)S(1)} collective-permute-done((bf16[128,384]{1,0:T(8,128)(2,1)S(1)}, bf16[128,384]{1,0:T(8,128)(2,1)S(1)}, u32[]{:S(2)}, u32[]{:S(2)}) %collective-permute-start.4) | collective-permute-done | bytes 98336 | tf_op jit(solution)/shard_map/ppermute | solution.py:353
  26.6 0.0 collective-permute-done.3.near_half
  26.6 0.0 copy-done.1
  26.6 0.1 weight.1.refs_4_
  26.7 0.0 collective-permute-done.8.refs_9_
  26.7 0.0 copy-done
  26.7 0.0 copy-done.2
  26.7 0.0 copy-done.3
  26.7 0.0 copy-done.4
  26.8 3.3 %heads.1 = (bf16[2,512,512]{2,1,0:T(8,128)(2,1)S(1)}, bf16[2,512,512]{2,1,0:T(8,128)(2,1)S(1)}, f32[2,1,512]{2,1,0:T(1,128)S(1)}, bf16[128,128]{1,0:T(8,128)(2,1...) custom-call(s32[4,4]{1,0:T(4,128)S(1)} %copy-done.3, ...), custom_call_target="tpu_custom_call" | custom-call | tf_op jit(solution)/shard_map/heads/pallas_call | solution.py:408
  30.0 0.1 collective-permute-start.10
  30.1 0.5 %collective-permute-start.9 = (bf16[128,256]{1,0:T(8,128)(2,1)S(1)}, bf16[128,256]{1,0:T(8,128)(2,1)S(1)}, u32[]{:S(2)}, u32[]{:S(2)}) collective-permute-start(bf16[128,256]{1,0:T(8,128)(2,1)S(1)} %get-tuple-element.25), channel_id=1, source_target_pairs={{0,1},{1,0},{2,3},{3,2},{4,5},{5,4},{6,7},{7,6},{8,9},{9,8},{10,11... | collective-permute-start | bytes 196616 | tf_op jit(solution)/shard_map/ppermute | solution.py:353
  30.6 0.7 %collective-permute-done.10 = bf16[128,256]{1,0:T(8,128)(2,1)S(1)} collective-permute-done((bf16[128,256]{1,0:T(8,128)(2,1)S(1)}, bf16[128,256]{1,0:T(8,128)(2,1)S(1)}, u32[]{:S(2)}, u32[]{:S(2)}) %collective-permute-start.10) | collective-permute-done | bytes 65568 | tf_op jit(solution)/shard_map/ppermute | solution.py:353
  31.4 1.5 %collective-permute-start.11 = (bf16[128,256]{1,0:T(8,128)(2,1)S(1)}, bf16[128,256]{1,0:T(8,128)(2,1)S(1)}, u32[]{:S(2)}, u32[]{:S(2)}) collective-permute-start(bf16[128,256]{1,0:T(8,128)(2,1)S(1)} %add_convert_fusion.1), channel_id=1, source_target_pairs={{0,2},{1,3},{2,0},{3,1},{4,6},{5,7},{6,4},{7,5},{8,10},{9,11},{10,... | collective-permute-start | bytes 196616 | tf_op jit(solution)/shard_map/ppermute | solution.py:353
  32.8 2.5 %rest.1 = (bf16[128,128]{1,0:T(8,128)(2,1)}, f32[256,384]{1,0:T(8,128)}) custom-call(bf16[2,512,512]{2,1,0:T(8,128)(2,1)S(1)} %get-tuple-element.16.p_b_ref, bf16[2,512,512]{2,1,0:T(8,128)(2,1)S(1)} %get-tuple-element.17.p_rest_ref, f32[2,1,512]{2,1,0:T(1,128)S(1)} %get-tuple-element.18.grad_dot_ref, bf16[128,128]{1,0:T(8,128)(2,1)S(1)} %get-tuple-element.19.attention_t, ...), custom_call_target="tpu_custom_call" | custom-call | tf_op jit(solution)/shard_map/rest/pallas_call | solution.py:420
  35.3 0.0 collective-permute-done.9
  35.3 0.4 %collective-permute-done.11 = bf16[128,256]{1,0:T(8,128)(2,1)S(1)} collective-permute-done((bf16[128,256]{1,0:T(8,128)(2,1)S(1)}, bf16[128,256]{1,0:T(8,128)(2,1)S(1)}, u32[]{:S(2)}, u32[]{:S(2)}) %collective-permute-start.11) | collective-permute-done | bytes 65568 | tf_op jit(solution)/shard_map/ppermute | solution.py:353
  35.7 0.7 %add_convert_fusion = bf16[128,256]{1,0:T(8,128)(2,1)} fusion(bf16[128,256]{1,0:T(8,128)(2,1)S(1)} %collective-permute-done.11, f32[128,256]{1,0:T(8,128)S(1)} %get-tuple-element.24, bf16[128,256]{1,0:T(8,128)(2,1)S(1)} %collective-permute-done.9), kind=kLoop, calls=%fused_computation.1 | loop fusion | flops 163840 | bytes 327680 | tf_op jit(solution)/shard_map/convert_element_type | solution.py:419
  (8 shorter events, 0.1 us)
Async XLA Ops:
  1.6 13.3 %collective-permute-start.1 = (bf16[128,768]{1,0:T(8,128)(2,1)S(1)}, bf16[128,768]{1,0:T(8,128)(2,1)S(1)}, u32[]{:S(2)}, u32[]{:S(2)}) collective-permute-start(bf16[128,768]{1,0:T(8,128)(2,1)S(1)} %pack.1), channel_id=1, source_target_pairs={{0,8},{4,12},{8,0},{12,4},{1,9},{5,13},{9,1},{13,5},{2,10},{6,14},... | collective-permute-start | bytes 589832 | tf_op jit(solution)/shard_map/ppermute | solution.py:353
  5.7 9.9 %collective-permute-start = (bf16[128,768]{1,0:T(8,128)(2,1)S(1)}, bf16[128,768]{1,0:T(8,128)(2,1)S(1)}, u32[]{:S(2)}, u32[]{:S(2)}) collective-permute-start(bf16[128,768]{1,0:T(8,128)(2,1)S(1)} %pack.1), channel_id=1, source_target_pairs={{0,4},{4,0},{8,12},{12,8},{1,5},{5,1},{9,13},{13,9},{2,6},{6,2},{1... | collective-permute-start | bytes 589832 | tf_op jit(solution)/shard_map/ppermute | solution.py:353
  14.9 5.4 %collective-permute-start.5 = (bf16[128,384]{1,0:T(8,128)(2,1)S(1)}, bf16[128,384]{1,0:T(8,128)(2,1)S(1)}, u32[]{:S(2)}, u32[]{:S(2)}) collective-permute-start(bf16[128,384]{1,0:T(8,128)(2,1)S(1)} %get-tuple-element.29), channel_id=1, source_target_pairs={{0,4},{4,0},{8,12},{12,8},{1,5},{5,1},{9,13},{13,9},{2,6},{6,2},{1... | collective-permute-start | bytes 294920 | tf_op jit(solution)/shard_map/ppermute | solution.py:353
  15.7 7.9 %collective-permute-start.6 = (bf16[256,256]{1,0:T(8,128)(2,1)S(1)}, bf16[256,256]{1,0:T(8,128)(2,1)S(1)}, u32[]{:S(2)}, u32[]{:S(2)}) collective-permute-start(bf16[256,256]{1,0:T(8,128)(2,1)S(1)} %slice.23), channel_id=1, source_target_pairs={{0,2},{1,3},{2,0},{3,1},{4,6},{5,7},{6,4},{7,5},{8,10},{9,11},{10,... | collective-permute-start | bytes 393224 | tf_op jit(solution)/shard_map/ppermute | solution.py:353
  17.2 4.8 %collective-permute-start.2 = (bf16[128,384]{1,0:T(8,128)(2,1)S(1)}, bf16[128,384]{1,0:T(8,128)(2,1)S(1)}, u32[]{:S(2)}, u32[]{:S(2)}) collective-permute-start(bf16[128,384]{1,0:T(8,128)(2,1)S(1)} %get-tuple-element.30), channel_id=1, source_target_pairs={{0,4},{4,0},{8,12},{12,8},{1,5},{5,1},{9,13},{13,9},{2,6},{6,2},{1... | collective-permute-start | bytes 294920 | tf_op jit(solution)/shard_map/ppermute | solution.py:353
  18.7 7.9 %collective-permute-start.3 = (bf16[256,384]{1,0:T(8,128)(2,1)S(1)}, bf16[256,384]{1,0:T(8,128)(2,1)S(1)}, u32[]{:S(2)}, u32[]{:S(2)}) collective-permute-start(bf16[256,384]{1,0:T(8,128)(2,1)S(1)} %slice.21), channel_id=1, source_target_pairs={{0,16},{16,0},{1,17},{17,1},{2,18},{18,2},{3,19},{19,3},{4,20},{20... | collective-permute-start | bytes 589832 | tf_op jit(solution)/shard_map/ppermute | solution.py:353
  20.3 6.3 %copy-start.1 = (bf16[256,384]{1,0:T(8,128)(2,1)S(1)}, bf16[256,384]{1,0:T(8,128)(2,1)}, u32[]{:S(2)}) copy-start(bf16[256,384]{1,0:T(8,128)(2,1)} %w0.1) | copy-start | bytes 589828
  20.3 4.3 %collective-permute-start.7 = (bf16[128,256]{1,0:T(8,128)(2,1)S(1)}, bf16[128,256]{1,0:T(8,128)(2,1)S(1)}, u32[]{:S(2)}, u32[]{:S(2)}) collective-permute-start(bf16[128,256]{1,0:T(8,128)(2,1)S(1)} %slice.24), channel_id=1, source_target_pairs={{0,2},{1,3},{2,0},{3,1},{4,6},{5,7},{6,4},{7,5},{8,10},{9,11},{10,... | collective-permute-start | bytes 196616 | tf_op jit(solution)/shard_map/ppermute | solution.py:353
  22.0 4.6 %collective-permute-start.4 = (bf16[128,384]{1,0:T(8,128)(2,1)S(1)}, bf16[128,384]{1,0:T(8,128)(2,1)S(1)}, u32[]{:S(2)}, u32[]{:S(2)}) collective-permute-start(bf16[128,384]{1,0:T(8,128)(2,1)S(1)} %collective-permute-done.2.far), channel_id=1, source_target_pairs={{0,16},{16,0},{1,17},{17,1},{2,18},{18,2},{3,19},{19,3},{4,20},{20... | collective-permute-start | bytes 294920 | tf_op jit(solution)/shard_map/ppermute | solution.py:353
  24.7 2.0 %copy-start = (bf16[128,1024]{1,0:T(8,128)(2,1)S(1)}, bf16[128,1024]{1,0:T(8,128)(2,1)}, u32[]{:S(2)}) copy-start(bf16[128,1024]{1,0:T(8,128)(2,1)} %refs_2_.1) | copy-start | bytes 786436
  24.7 2.0 %copy-start.2 = (bf16[128,128]{1,0:T(8,128)(2,1)S(1)}, bf16[128,128]{1,0:T(8,128)(2,1)}, u32[]{:S(2)}) copy-start(bf16[128,128]{1,0:T(8,128)(2,1)} %refs_3_.1) | copy-start | bytes 98308
  24.7 2.0 %copy-start.3 = (s32[4,4]{1,0:T(4,128)S(1)}, s32[4,4]{1,0:T(4,128)}, u32[]{:S(2)}) copy-start(s32[4,4]{1,0:T(4,128)} %refs_0_.1) | copy-start | bytes 196
  24.7 2.0 %copy-start.4 = (s32[4]{0:T(128)S(1)}, s32[4]{0:T(128)}, u32[]{:S(2)}) copy-start(s32[4]{0:T(128)} %refs_1_.1) | copy-start | bytes 52
  24.7 2.0 %collective-permute-start.8 = (bf16[768,256]{1,0:T(8,128)(2,1)S(1)}, bf16[768,256]{1,0:T(8,128)(2,1)S(1)}, u32[]{:S(2)}, u32[]{:S(2)}) collective-permute-start(bf16[768,256]{1,0:T(8,128)(2,1)S(1)} %pad_maximum_fusion), channel_id=1, source_target_pairs={{0,1},{1,0},{2,3},{3,2},{4,5},{5,4},{6,7},{7,6},{8,9},{9,8},{10,11... | collective-permute-start | bytes 1179656 | tf_op jit(solution)/shard_map/ppermute | solution.py:353
  30.0 1.3 %collective-permute-start.10 = (bf16[128,256]{1,0:T(8,128)(2,1)S(1)}, bf16[128,256]{1,0:T(8,128)(2,1)S(1)}, u32[]{:S(2)}, u32[]{:S(2)}) collective-permute-start(bf16[128,256]{1,0:T(8,128)(2,1)S(1)} %get-tuple-element.27), channel_id=1, source_target_pairs={{0,1},{1,0},{2,3},{3,2},{4,5},{5,4},{6,7},{7,6},{8,9},{9,8},{10,11... | collective-permute-start | bytes 196616 | tf_op jit(solution)/shard_map/ppermute | solution.py:353
  30.1 5.2 %collective-permute-start.9 = (bf16[128,256]{1,0:T(8,128)(2,1)S(1)}, bf16[128,256]{1,0:T(8,128)(2,1)S(1)}, u32[]{:S(2)}, u32[]{:S(2)}) collective-permute-start(bf16[128,256]{1,0:T(8,128)(2,1)S(1)} %get-tuple-element.25), channel_id=1, source_target_pairs={{0,1},{1,0},{2,3},{3,2},{4,5},{5,4},{6,7},{7,6},{8,9},{9,8},{10,11... | collective-permute-start | bytes 196616 | tf_op jit(solution)/shard_map/ppermute | solution.py:353
  31.4 4.3 %collective-permute-start.11 = (bf16[128,256]{1,0:T(8,128)(2,1)S(1)}, bf16[128,256]{1,0:T(8,128)(2,1)S(1)}, u32[]{:S(2)}, u32[]{:S(2)}) collective-permute-start(bf16[128,256]{1,0:T(8,128)(2,1)S(1)} %add_convert_fusion.1), channel_id=1, source_target_pairs={{0,2},{1,3},{2,0},{3,1},{4,6},{5,7},{6,4},{7,5},{8,10},{9,11},{10,... | collective-permute-start | bytes 196616 | tf_op jit(solution)/shard_map/ppermute | solution.py:353

commit v7 on v6

--- a/solution.py
+++ b/solution.py
@@ -237,7 +237,7 @@
         named["p_rest"][h] = p_rest
         v_t = state[h][4]
         o_t = (dot(v_t, p_b) + dot(v_t, p_rest)).astype(BF)
-        more.append((p_t[:, 0:rows], p_t[0:rows], p_b[0:rows], o_t))
+        more.append((p_t[:, 0:rows], p_t[0:rows], dot(p_b[0:rows], state[h][5]), o_t))
     for h in range(heads):
         q8, k_t, d_pq, d_pk, _, g_h, g_t, _ = state[h]
         p_q, p_k, p_bk, o_t = more[h]
@@ -247,9 +247,9 @@
         ds_q = (p_q * (d_pq - grad_dot[:, 0:rows])).astype(BF)
         ds_k = (p_k * (d_pk - grad_dot)).astype(BF)
         d_q = jnp.transpose(dot(k_t, ds_q)) * scale
-        own += [d_q, dot(ds_k, q8), dot(p_bk, g_h)]
+        own += [d_q, dot(ds_k, q8), p_bk]
     own = jnp.concatenate(own, axis=1).astype(BF)
-    for m in range(4):
+    for m in (3, 2, 1, 0):
         out = named["part%d" % m]
         w_rows = w_all[pl.ds(pl.multiple_of((f ^ m) * depth, depth), depth), :]
         out[...] = dot_nt(own, w_rows).astype(out.dtype)

time: 36.5 us -> 36.5 us (level)
  no operation moved by 1% of the time
where the time goes in v7:
time: 36.5 us; the launch traced here: 36.4 us
  starting transfers between devices  16.2 us (44%)
  waiting for transfers between devices  11.7 us (32%)
  Pallas kernels  6.77 us (19%)
  between operations  0.79 us (2%)
  other arithmetic  0.69 us (2%)
    ppermute x12, starting transfers between devices, swap(): return lax.ppermute(x, axis, [(i, i ^ bit) for i in range(n)])  16.2 us
    ppermute x12, waiting for transfers between devices, swap(): return lax.ppermute(x, axis, [(i, i ^ bit) for i in range(n)])  11.7 us
    pallas_call x1, Pallas kernels, short(): pl.pallas_call(functools.partial(heads_kernel, slots, refs_of, where), ou...  3.28 us
    pallas_call x1, Pallas kernels, short(): pl.pallas_call(rest_kernel, out_shape=[jax.ShapeDtypeStruct(grad_out.shap...  2.47 us
    pallas_call x1, Pallas kernels, pack(): pl.pallas_call(pack_kernel, out_shape=pltpu.VMEM((rows, columns), BF), in...  0.94 us
  transfers between devices with their start and end apart: 12, of which 5 were waited for; matrix products, arithmetic and copies ran while one was open for 0% of the time, Pallas kernels for 7%

profile of v7, /device:TPU:0, one launch (start us, length us, event | category | flops | bytes accessed | tf_op | source)
XLA Modules:
  0.0 36.4 jit_solution(7041117015440824999)
XLA Ops:
  0.6 0.9 %pack.1 = bf16[128,768]{1,0:T(8,128)(2,1)S(1)} custom-call(bf16[256,384]{1,0:T(8,128)(2,1)} %w0.1, bf16[128,1024]{1,0:T(8,128)(2,1)} %refs_2_.1, bf16[128,128]{1,0:T(8,128)(2,1)} %refs_3_.1), custom_call_target="tpu_custom_call" | custom-call | tf_op jit(solution)/shard_map/pack/pallas_call | solution.py:331
  1.6 4.1 %collective-permute-start.1 = (bf16[128,768]{1,0:T(8,128)(2,1)S(1)}, bf16[128,768]{1,0:T(8,128)(2,1)S(1)}, u32[]{:S(2)}, u32[]{:S(2)}) collective-permute-start(bf16[128,768]{1,0:T(8,128)(2,1)S(1)} %pack.1), channel_id=1, source_target_pairs={{0,8},{4,12},{8,0},{12,4},{1,9},{5,13},{9,1},{13,5},{2,10},{6,14},... | collective-permute-start | bytes 589832 | tf_op jit(solution)/shard_map/ppermute | solution.py:353
  5.7 1.6 %collective-permute-start = (bf16[128,768]{1,0:T(8,128)(2,1)S(1)}, bf16[128,768]{1,0:T(8,128)(2,1)S(1)}, u32[]{:S(2)}, u32[]{:S(2)}) collective-permute-start(bf16[128,768]{1,0:T(8,128)(2,1)S(1)} %pack.1), channel_id=1, source_target_pairs={{0,4},{4,0},{8,12},{12,8},{1,5},{5,1},{9,13},{13,9},{2,6},{6,2},{1... | collective-permute-start | bytes 589832 | tf_op jit(solution)/shard_map/ppermute | solution.py:353
  7.3 7.6 %collective-permute-done.1 = bf16[128,768]{1,0:T(8,128)(2,1)S(1)} collective-permute-done((bf16[128,768]{1,0:T(8,128)(2,1)S(1)}, bf16[128,768]{1,0:T(8,128)(2,1)S(1)}, u32[]{:S(2)}, u32[]{:S(2)}) %collective-permute-start.1) | collective-permute-done | bytes 196640 | tf_op jit(solution)/shard_map/ppermute | solution.py:353
  14.9 0.7 %collective-permute-start.5 = (bf16[128,384]{1,0:T(8,128)(2,1)S(1)}, bf16[128,384]{1,0:T(8,128)(2,1)S(1)}, u32[]{:S(2)}, u32[]{:S(2)}) collective-permute-start(bf16[128,384]{1,0:T(8,128)(2,1)S(1)} %get-tuple-element.29), channel_id=1, source_target_pairs={{0,4},{4,0},{8,12},{12,8},{1,5},{5,1},{9,13},{13,9},{2,6},{6,2},{1... | collective-permute-start | bytes 294920 | tf_op jit(solution)/shard_map/ppermute | solution.py:353
  15.6 0.0 collective-permute-done
  15.7 1.6 %collective-permute-start.6 = (bf16[256,256]{1,0:T(8,128)(2,1)S(1)}, bf16[256,256]{1,0:T(8,128)(2,1)S(1)}, u32[]{:S(2)}, u32[]{:S(2)}) collective-permute-start(bf16[256,256]{1,0:T(8,128)(2,1)S(1)} %slice.23), channel_id=1, source_target_pairs={{0,2},{1,3},{2,0},{3,1},{4,6},{5,7},{6,4},{7,5},{8,10},{9,11},{10,... | collective-permute-start | bytes 393224 | tf_op jit(solution)/shard_map/ppermute | solution.py:353
  17.2 1.5 %collective-permute-start.2 = (bf16[128,384]{1,0:T(8,128)(2,1)S(1)}, bf16[128,384]{1,0:T(8,128)(2,1)S(1)}, u32[]{:S(2)}, u32[]{:S(2)}) collective-permute-start(bf16[128,384]{1,0:T(8,128)(2,1)S(1)} %get-tuple-element.30), channel_id=1, source_target_pairs={{0,4},{4,0},{8,12},{12,8},{1,5},{5,1},{9,13},{13,9},{2,6},{6,2},{1... | collective-permute-start | bytes 294920 | tf_op jit(solution)/shard_map/ppermute | solution.py:353
  18.7 1.6 %collective-permute-start.3 = (bf16[256,384]{1,0:T(8,128)(2,1)S(1)}, bf16[256,384]{1,0:T(8,128)(2,1)S(1)}, u32[]{:S(2)}, u32[]{:S(2)}) collective-permute-start(bf16[256,384]{1,0:T(8,128)(2,1)S(1)} %slice.21), channel_id=1, source_target_pairs={{0,16},{16,0},{1,17},{17,1},{2,18},{18,2},{3,19},{19,3},{4,20},{20... | collective-permute-start | bytes 589832 | tf_op jit(solution)/shard_map/ppermute | solution.py:353
  20.3 0.0 collective-permute-done.5.refs_6_
  20.3 0.0 copy-start.1
  20.3 1.7 %collective-permute-start.7 = (bf16[128,256]{1,0:T(8,128)(2,1)S(1)}, bf16[128,256]{1,0:T(8,128)(2,1)S(1)}, u32[]{:S(2)}, u32[]{:S(2)}) collective-permute-start(bf16[128,256]{1,0:T(8,128)(2,1)S(1)} %slice.24), channel_id=1, source_target_pairs={{0,2},{1,3},{2,0},{3,1},{4,6},{5,7},{6,4},{7,5},{8,10},{9,11},{10,... | collective-permute-start | bytes 196616 | tf_op jit(solution)/shard_map/ppermute | solution.py:353
  22.0 0.0 collective-permute-done.2.far
  22.0 1.5 %collective-permute-start.4 = (bf16[128,384]{1,0:T(8,128)(2,1)S(1)}, bf16[128,384]{1,0:T(8,128)(2,1)S(1)}, u32[]{:S(2)}, u32[]{:S(2)}) collective-permute-start(bf16[128,384]{1,0:T(8,128)(2,1)S(1)} %collective-permute-done.2.far), channel_id=1, source_target_pairs={{0,16},{16,0},{1,17},{17,1},{2,18},{18,2},{3,19},{19,3},{4,20},{20... | collective-permute-start | bytes 294920 | tf_op jit(solution)/shard_map/ppermute | solution.py:353
  23.5 0.0 collective-permute-done.6.refs_7_
  23.5 1.1 %collective-permute-done.7.refs_8_ = bf16[128,256]{1,0:T(8,128)(2,1)S(1)} collective-permute-done((bf16[128,256]{1,0:T(8,128)(2,1)S(1)}, bf16[128,256]{1,0:T(8,128)(2,1)S(1)}, u32[]{:S(2)}, u32[]{:S(2)}) %collective-permute-start.7) | collective-permute-done | bytes 65568 | tf_op jit(solution)/shard_map/ppermute | solution.py:353
  24.7 0.0 copy-start
  24.7 0.0 copy-start.2
  24.7 0.0 copy-start.3
  24.7 0.0 copy-start.4
  24.7 0.1 collective-permute-start.8
  24.8 1.8 %collective-permute-done.4.far_half = bf16[128,384]{1,0:T(8,128)(2,1)S(1)} collective-permute-done((bf16[128,384]{1,0:T(8,128)(2,1)S(1)}, bf16[128,384]{1,0:T(8,128)(2,1)S(1)}, u32[]{:S(2)}, u32[]{:S(2)}) %collective-permute-start.4) | collective-permute-done | bytes 98336 | tf_op jit(solution)/shard_map/ppermute | solution.py:353
  26.6 0.0 collective-permute-done.3.near_half
  26.6 0.0 copy-done.1
  26.6 0.1 weight.1.refs_4_
  26.7 0.0 collective-permute-done.8.refs_9_
  26.7 0.0 copy-done
  26.7 0.0 copy-done.2
  26.7 0.0 copy-done.3
  26.7 0.0 copy-done.4
  26.8 3.3 %heads.1 = (bf16[2,512,512]{2,1,0:T(8,128)(2,1)S(1)}, bf16[2,512,512]{2,1,0:T(8,128)(2,1)S(1)}, f32[2,1,512]{2,1,0:T(1,128)S(1)}, bf16[128,128]{1,0:T(8,128)(2,1...) custom-call(s32[4,4]{1,0:T(4,128)S(1)} %copy-done.3, ...), custom_call_target="tpu_custom_call" | custom-call | tf_op jit(solution)/shard_map/heads/pallas_call | solution.py:408
  30.0 0.1 collective-permute-start.10
  30.1 0.5 %collective-permute-start.9 = (bf16[128,256]{1,0:T(8,128)(2,1)S(1)}, bf16[128,256]{1,0:T(8,128)(2,1)S(1)}, u32[]{:S(2)}, u32[]{:S(2)}) collective-permute-start(bf16[128,256]{1,0:T(8,128)(2,1)S(1)} %get-tuple-element.25), channel_id=1, source_target_pairs={{0,1},{1,0},{2,3},{3,2},{4,5},{5,4},{6,7},{7,6},{8,9},{9,8},{10,11... | collective-permute-start | bytes 196616 | tf_op jit(solution)/shard_map/ppermute | solution.py:353
  30.6 0.7 %collective-permute-done.10 = bf16[128,256]{1,0:T(8,128)(2,1)S(1)} collective-permute-done((bf16[128,256]{1,0:T(8,128)(2,1)S(1)}, bf16[128,256]{1,0:T(8,128)(2,1)S(1)}, u32[]{:S(2)}, u32[]{:S(2)}) %collective-permute-start.10) | collective-permute-done | bytes 65568 | tf_op jit(solution)/shard_map/ppermute | solution.py:353
  31.4 1.5 %collective-permute-start.11 = (bf16[128,256]{1,0:T(8,128)(2,1)S(1)}, bf16[128,256]{1,0:T(8,128)(2,1)S(1)}, u32[]{:S(2)}, u32[]{:S(2)}) collective-permute-start(bf16[128,256]{1,0:T(8,128)(2,1)S(1)} %add_convert_fusion.1), channel_id=1, source_target_pairs={{0,2},{1,3},{2,0},{3,1},{4,6},{5,7},{6,4},{7,5},{8,10},{9,11},{10,... | collective-permute-start | bytes 196616 | tf_op jit(solution)/shard_map/ppermute | solution.py:353
  32.8 2.5 %rest.1 = (bf16[128,128]{1,0:T(8,128)(2,1)}, f32[256,384]{1,0:T(8,128)}) custom-call(bf16[2,512,512]{2,1,0:T(8,128)(2,1)S(1)} %get-tuple-element.16.p_b_ref, bf16[2,512,512]{2,1,0:T(8,128)(2,1)S(1)} %get-tuple-element.17.p_rest_ref, f32[2,1,512]{2,1,0:T(1,128)S(1)} %get-tuple-element.18.grad_dot_ref, bf16[128,128]{1,0:T(8,128)(2,1)S(1)} %get-tuple-element.19.attention_t, ...), custom_call_target="tpu_custom_call" | custom-call | tf_op jit(solution)/shard_map/rest/pallas_call | solution.py:420
  35.3 0.0 collective-permute-done.9
  35.3 0.4 %collective-permute-done.11 = bf16[128,256]{1,0:T(8,128)(2,1)S(1)} collective-permute-done((bf16[128,256]{1,0:T(8,128)(2,1)S(1)}, bf16[128,256]{1,0:T(8,128)(2,1)S(1)}, u32[]{:S(2)}, u32[]{:S(2)}) %collective-permute-start.11) | collective-permute-done | bytes 65568 | tf_op jit(solution)/shard_map/ppermute | solution.py:353
  35.7 0.7 %add_convert_fusion = bf16[128,256]{1,0:T(8,128)(2,1)} fusion(bf16[128,256]{1,0:T(8,128)(2,1)S(1)} %collective-permute-done.11, f32[128,256]{1,0:T(8,128)S(1)} %get-tuple-element.24, bf16[128,256]{1,0:T(8,128)(2,1)S(1)} %collective-permute-done.9), kind=kLoop, calls=%fused_computation.1 | loop fusion | flops 163840 | bytes 327680 | tf_op jit(solution)/shard_map/convert_element_type | solution.py:419
  (8 shorter events, 0.1 us)
Async XLA Ops:
  1.6 13.3 %collective-permute-start.1 = (bf16[128,768]{1,0:T(8,128)(2,1)S(1)}, bf16[128,768]{1,0:T(8,128)(2,1)S(1)}, u32[]{:S(2)}, u32[]{:S(2)}) collective-permute-start(bf16[128,768]{1,0:T(8,128)(2,1)S(1)} %pack.1), channel_id=1, source_target_pairs={{0,8},{4,12},{8,0},{12,4},{1,9},{5,13},{9,1},{13,5},{2,10},{6,14},... | collective-permute-start | bytes 589832 | tf_op jit(solution)/shard_map/ppermute | solution.py:353
  5.7 9.9 %collective-permute-start = (bf16[128,768]{1,0:T(8,128)(2,1)S(1)}, bf16[128,768]{1,0:T(8,128)(2,1)S(1)}, u32[]{:S(2)}, u32[]{:S(2)}) collective-permute-start(bf16[128,768]{1,0:T(8,128)(2,1)S(1)} %pack.1), channel_id=1, source_target_pairs={{0,4},{4,0},{8,12},{12,8},{1,5},{5,1},{9,13},{13,9},{2,6},{6,2},{1... | collective-permute-start | bytes 589832 | tf_op jit(solution)/shard_map/ppermute | solution.py:353
  14.9 5.4 %collective-permute-start.5 = (bf16[128,384]{1,0:T(8,128)(2,1)S(1)}, bf16[128,384]{1,0:T(8,128)(2,1)S(1)}, u32[]{:S(2)}, u32[]{:S(2)}) collective-permute-start(bf16[128,384]{1,0:T(8,128)(2,1)S(1)} %get-tuple-element.29), channel_id=1, source_target_pairs={{0,4},{4,0},{8,12},{12,8},{1,5},{5,1},{9,13},{13,9},{2,6},{6,2},{1... | collective-permute-start | bytes 294920 | tf_op jit(solution)/shard_map/ppermute | solution.py:353
  15.7 7.9 %collective-permute-start.6 = (bf16[256,256]{1,0:T(8,128)(2,1)S(1)}, bf16[256,256]{1,0:T(8,128)(2,1)S(1)}, u32[]{:S(2)}, u32[]{:S(2)}) collective-permute-start(bf16[256,256]{1,0:T(8,128)(2,1)S(1)} %slice.23), channel_id=1, source_target_pairs={{0,2},{1,3},{2,0},{3,1},{4,6},{5,7},{6,4},{7,5},{8,10},{9,11},{10,... | collective-permute-start | bytes 393224 | tf_op jit(solution)/shard_map/ppermute | solution.py:353
  17.2 4.8 %collective-permute-start.2 = (bf16[128,384]{1,0:T(8,128)(2,1)S(1)}, bf16[128,384]{1,0:T(8,128)(2,1)S(1)}, u32[]{:S(2)}, u32[]{:S(2)}) collective-permute-start(bf16[128,384]{1,0:T(8,128)(2,1)S(1)} %get-tuple-element.30), channel_id=1, source_target_pairs={{0,4},{4,0},{8,12},{12,8},{1,5},{5,1},{9,13},{13,9},{2,6},{6,2},{1... | collective-permute-start | bytes 294920 | tf_op jit(solution)/shard_map/ppermute | solution.py:353
  18.7 7.9 %collective-permute-start.3 = (bf16[256,384]{1,0:T(8,128)(2,1)S(1)}, bf16[256,384]{1,0:T(8,128)(2,1)S(1)}, u32[]{:S(2)}, u32[]{:S(2)}) collective-permute-start(bf16[256,384]{1,0:T(8,128)(2,1)S(1)} %slice.21), channel_id=1, source_target_pairs={{0,16},{16,0},{1,17},{17,1},{2,18},{18,2},{3,19},{19,3},{4,20},{20... | collective-permute-start | bytes 589832 | tf_op jit(solution)/shard_map/ppermute | solution.py:353
  20.3 6.3 %copy-start.1 = (bf16[256,384]{1,0:T(8,128)(2,1)S(1)}, bf16[256,384]{1,0:T(8,128)(2,1)}, u32[]{:S(2)}) copy-start(bf16[256,384]{1,0:T(8,128)(2,1)} %w0.1) | copy-start | bytes 589828
  20.3 4.3 %collective-permute-start.7 = (bf16[128,256]{1,0:T(8,128)(2,1)S(1)}, bf16[128,256]{1,0:T(8,128)(2,1)S(1)}, u32[]{:S(2)}, u32[]{:S(2)}) collective-permute-start(bf16[128,256]{1,0:T(8,128)(2,1)S(1)} %slice.24), channel_id=1, source_target_pairs={{0,2},{1,3},{2,0},{3,1},{4,6},{5,7},{6,4},{7,5},{8,10},{9,11},{10,... | collective-permute-start | bytes 196616 | tf_op jit(solution)/shard_map/ppermute | solution.py:353
  22.0 4.6 %collective-permute-start.4 = (bf16[128,384]{1,0:T(8,128)(2,1)S(1)}, bf16[128,384]{1,0:T(8,128)(2,1)S(1)}, u32[]{:S(2)}, u32[]{:S(2)}) collective-permute-start(bf16[128,384]{1,0:T(8,128)(2,1)S(1)} %collective-permute-done.2.far), channel_id=1, source_target_pairs={{0,16},{16,0},{1,17},{17,1},{2,18},{18,2},{3,19},{19,3},{4,20},{20... | collective-permute-start | bytes 294920 | tf_op jit(solution)/shard_map/ppermute | solution.py:353
  24.7 2.0 %copy-start = (bf16[128,1024]{1,0:T(8,128)(2,1)S(1)}, bf16[128,1024]{1,0:T(8,128)(2,1)}, u32[]{:S(2)}) copy-start(bf16[128,1024]{1,0:T(8,128)(2,1)} %refs_2_.1) | copy-start | bytes 786436
  24.7 2.0 %copy-start.2 = (bf16[128,128]{1,0:T(8,128)(2,1)S(1)}, bf16[128,128]{1,0:T(8,128)(2,1)}, u32[]{:S(2)}) copy-start(bf16[128,128]{1,0:T(8,128)(2,1)} %refs_3_.1) | copy-start | bytes 98308
  24.7 2.0 %copy-start.3 = (s32[4,4]{1,0:T(4,128)S(1)}, s32[4,4]{1,0:T(4,128)}, u32[]{:S(2)}) copy-start(s32[4,4]{1,0:T(4,128)} %refs_0_.1) | copy-start | bytes 196
  24.7 2.0 %copy-start.4 = (s32[4]{0:T(128)S(1)}, s32[4]{0:T(128)}, u32[]{:S(2)}) copy-start(s32[4]{0:T(128)} %refs_1_.1) | copy-start | bytes 52
  24.7 2.0 %collective-permute-start.8 = (bf16[768,256]{1,0:T(8,128)(2,1)S(1)}, bf16[768,256]{1,0:T(8,128)(2,1)S(1)}, u32[]{:S(2)}, u32[]{:S(2)}) collective-permute-start(bf16[768,256]{1,0:T(8,128)(2,1)S(1)} %pad_maximum_fusion), channel_id=1, source_target_pairs={{0,1},{1,0},{2,3},{3,2},{4,5},{5,4},{6,7},{7,6},{8,9},{9,8},{10,11... | collective-permute-start | bytes 1179656 | tf_op jit(solution)/shard_map/ppermute | solution.py:353
  30.0 1.3 %collective-permute-start.10 = (bf16[128,256]{1,0:T(8,128)(2,1)S(1)}, bf16[128,256]{1,0:T(8,128)(2,1)S(1)}, u32[]{:S(2)}, u32[]{:S(2)}) collective-permute-start(bf16[128,256]{1,0:T(8,128)(2,1)S(1)} %get-tuple-element.27), channel_id=1, source_target_pairs={{0,1},{1,0},{2,3},{3,2},{4,5},{5,4},{6,7},{7,6},{8,9},{9,8},{10,11... | collective-permute-start | bytes 196616 | tf_op jit(solution)/shard_map/ppermute | solution.py:353
  30.1 5.2 %collective-permute-start.9 = (bf16[128,256]{1,0:T(8,128)(2,1)S(1)}, bf16[128,256]{1,0:T(8,128)(2,1)S(1)}, u32[]{:S(2)}, u32[]{:S(2)}) collective-permute-start(bf16[128,256]{1,0:T(8,128)(2,1)S(1)} %get-tuple-element.25), channel_id=1, source_target_pairs={{0,1},{1,0},{2,3},{3,2},{4,5},{5,4},{6,7},{7,6},{8,9},{9,8},{10,11... | collective-permute-start | bytes 196616 | tf_op jit(solution)/shard_map/ppermute | solution.py:353
  31.4 4.3 %collective-permute-start.11 = (bf16[128,256]{1,0:T(8,128)(2,1)S(1)}, bf16[128,256]{1,0:T(8,128)(2,1)S(1)}, u32[]{:S(2)}, u32[]{:S(2)}) collective-permute-start(bf16[128,256]{1,0:T(8,128)(2,1)S(1)} %add_convert_fusion.1), channel_id=1, source_target_pairs={{0,2},{1,3},{2,0},{3,1},{4,6},{5,7},{6,4},{7,5},{8,10},{9,11},{10,... | collective-permute-start | bytes 196616 | tf_op jit(solution)/shard_map/ppermute | solution.py:353

commit v8 on v7

--- a/solution.py
+++ b/solution.py
@@ -398,7 +398,7 @@
         ("pieces", (4, length, depth), BF),
         ("part0", (rows, depth), F32),
         ("part1", (rows, depth), BF),
-        ("part2", (rows, depth), F32),
+        ("part2", (rows, depth), BF),
         ("part3", (rows, depth), BF),
     ]
     scratch = []
@@ -414,9 +414,10 @@
         compiler_params=pltpu.CompilerParams(vmem_limit_bytes=16 << 20),
         name="heads",
     )(*values)
-    pair = (part2 + swap(part3, "fsdp", 1).astype(F32)).astype(BF)
-    far = swap(pair, "fsdp", 2).astype(F32)
-    grad_input = (part0 + swap(part1, "fsdp", 1).astype(F32) + far).astype(BF)
+    total = part0
+    for m, part in ((1, part1), (2, part2), (3, part3)):
+        total = total + swap(part, "fsdp", m).astype(F32)
+    grad_input = total.astype(BF)
     attention, grad_weight = pl.pallas_call(
         rest_kernel,
         out_shape=[

time: 36.5 us -> 36.6 us (level)
  no operation moved by 1% of the time
where the time goes in v8:
time: 36.6 us; the launch traced here: 36.4 us
  starting transfers between devices  16.2 us (44%)
  waiting for transfers between devices  11.9 us (33%)
  Pallas kernels  6.77 us (18%)
  between operations  0.79 us (2%)
  other arithmetic  0.69 us (2%)
    ppermute x12, starting transfers between devices, swap(): return lax.ppermute(x, axis, [(i, i ^ bit) for i in range(n)])  16.2 us
    ppermute x12, waiting for transfers between devices, swap(): return lax.ppermute(x, axis, [(i, i ^ bit) for i in range(n)])  11.9 us
    pallas_call x1, Pallas kernels, short(): pl.pallas_call(functools.partial(heads_kernel, slots, refs_of, where), ou...  3.28 us
    pallas_call x1, Pallas kernels, short(): pl.pallas_call(rest_kernel, out_shape=[jax.ShapeDtypeStruct(grad_out.shap...  2.47 us
    pallas_call x1, Pallas kernels, pack(): pl.pallas_call(pack_kernel, out_shape=pltpu.VMEM((rows, columns), BF), in...  0.94 us
  transfers between devices with their start and end apart: 12, of which 5 were waited for; matrix products, arithmetic and copies ran while one was open for 0% of the time, Pallas kernels for 7%

profile of v8, /device:TPU:0, one launch (start us, length us, event | category | flops | bytes accessed | tf_op | source)
XLA Modules:
  0.0 36.4 jit_solution(13789740687370420677)
XLA Ops:
  0.6 0.9 %pack.1 = bf16[128,768]{1,0:T(8,128)(2,1)S(1)} custom-call(bf16[256,384]{1,0:T(8,128)(2,1)} %w0.1, bf16[128,1024]{1,0:T(8,128)(2,1)} %refs_2_.1, bf16[128,128]{1,0:T(8,128)(2,1)} %refs_3_.1), custom_call_target="tpu_custom_call" | custom-call | tf_op jit(solution)/shard_map/pack/pallas_call | solution.py:331
  1.6 4.1 %collective-permute-start.1 = (bf16[128,768]{1,0:T(8,128)(2,1)S(1)}, bf16[128,768]{1,0:T(8,128)(2,1)S(1)}, u32[]{:S(2)}, u32[]{:S(2)}) collective-permute-start(bf16[128,768]{1,0:T(8,128)(2,1)S(1)} %pack.1), channel_id=1, source_target_pairs={{0,8},{4,12},{8,0},{12,4},{1,9},{5,13},{9,1},{13,5},{2,10},{6,14},... | collective-permute-start | bytes 589832 | tf_op jit(solution)/shard_map/ppermute | solution.py:353
  5.7 1.6 %collective-permute-start = (bf16[128,768]{1,0:T(8,128)(2,1)S(1)}, bf16[128,768]{1,0:T(8,128)(2,1)S(1)}, u32[]{:S(2)}, u32[]{:S(2)}) collective-permute-start(bf16[128,768]{1,0:T(8,128)(2,1)S(1)} %pack.1), channel_id=1, source_target_pairs={{0,4},{4,0},{8,12},{12,8},{1,5},{5,1},{9,13},{13,9},{2,6},{6,2},{1... | collective-permute-start | bytes 589832 | tf_op jit(solution)/shard_map/ppermute | solution.py:353
  7.3 7.6 %collective-permute-done.1 = bf16[128,768]{1,0:T(8,128)(2,1)S(1)} collective-permute-done((bf16[128,768]{1,0:T(8,128)(2,1)S(1)}, bf16[128,768]{1,0:T(8,128)(2,1)S(1)}, u32[]{:S(2)}, u32[]{:S(2)}) %collective-permute-start.1) | collective-permute-done | bytes 196640 | tf_op jit(solution)/shard_map/ppermute | solution.py:353
  14.9 0.7 %collective-permute-start.5 = (bf16[128,384]{1,0:T(8,128)(2,1)S(1)}, bf16[128,384]{1,0:T(8,128)(2,1)S(1)}, u32[]{:S(2)}, u32[]{:S(2)}) collective-permute-start(bf16[128,384]{1,0:T(8,128)(2,1)S(1)} %get-tuple-element.29), channel_id=1, source_target_pairs={{0,4},{4,0},{8,12},{12,8},{1,5},{5,1},{9,13},{13,9},{2,6},{6,2},{1... | collective-permute-start | bytes 294920 | tf_op jit(solution)/shard_map/ppermute | solution.py:353
  15.6 0.0 collective-permute-done
  15.7 1.6 %collective-permute-start.6 = (bf16[256,256]{1,0:T(8,128)(2,1)S(1)}, bf16[256,256]{1,0:T(8,128)(2,1)S(1)}, u32[]{:S(2)}, u32[]{:S(2)}) collective-permute-start(bf16[256,256]{1,0:T(8,128)(2,1)S(1)} %slice.23), channel_id=1, source_target_pairs={{0,2},{1,3},{2,0},{3,1},{4,6},{5,7},{6,4},{7,5},{8,10},{9,11},{10,... | collective-permute-start | bytes 393224 | tf_op jit(solution)/shard_map/ppermute | solution.py:353
  17.2 1.5 %collective-permute-start.2 = (bf16[128,384]{1,0:T(8,128)(2,1)S(1)}, bf16[128,384]{1,0:T(8,128)(2,1)S(1)}, u32[]{:S(2)}, u32[]{:S(2)}) collective-permute-start(bf16[128,384]{1,0:T(8,128)(2,1)S(1)} %get-tuple-element.30), channel_id=1, source_target_pairs={{0,4},{4,0},{8,12},{12,8},{1,5},{5,1},{9,13},{13,9},{2,6},{6,2},{1... | collective-permute-start | bytes 294920 | tf_op jit(solution)/shard_map/ppermute | solution.py:353
  18.7 1.6 %collective-permute-start.3 = (bf16[256,384]{1,0:T(8,128)(2,1)S(1)}, bf16[256,384]{1,0:T(8,128)(2,1)S(1)}, u32[]{:S(2)}, u32[]{:S(2)}) collective-permute-start(bf16[256,384]{1,0:T(8,128)(2,1)S(1)} %slice.21), channel_id=1, source_target_pairs={{0,16},{16,0},{1,17},{17,1},{2,18},{18,2},{3,19},{19,3},{4,20},{20... | collective-permute-start | bytes 589832 | tf_op jit(solution)/shard_map/ppermute | solution.py:353
  20.3 0.0 collective-permute-done.5.refs_6_
  20.3 0.0 copy-start.1
  20.3 1.7 %collective-permute-start.7 = (bf16[128,256]{1,0:T(8,128)(2,1)S(1)}, bf16[128,256]{1,0:T(8,128)(2,1)S(1)}, u32[]{:S(2)}, u32[]{:S(2)}) collective-permute-start(bf16[128,256]{1,0:T(8,128)(2,1)S(1)} %slice.24), channel_id=1, source_target_pairs={{0,2},{1,3},{2,0},{3,1},{4,6},{5,7},{6,4},{7,5},{8,10},{9,11},{10,... | collective-permute-start | bytes 196616 | tf_op jit(solution)/shard_map/ppermute | solution.py:353
  22.0 0.0 collective-permute-done.2.far
  22.0 1.5 %collective-permute-start.4 = (bf16[128,384]{1,0:T(8,128)(2,1)S(1)}, bf16[128,384]{1,0:T(8,128)(2,1)S(1)}, u32[]{:S(2)}, u32[]{:S(2)}) collective-permute-start(bf16[128,384]{1,0:T(8,128)(2,1)S(1)} %collective-permute-done.2.far), channel_id=1, source_target_pairs={{0,16},{16,0},{1,17},{17,1},{2,18},{18,2},{3,19},{19,3},{4,20},{20... | collective-permute-start | bytes 294920 | tf_op jit(solution)/shard_map/ppermute | solution.py:353
  23.5 0.0 collective-permute-done.6.refs_7_
  23.5 1.1 %collective-permute-done.7.refs_8_ = bf16[128,256]{1,0:T(8,128)(2,1)S(1)} collective-permute-done((bf16[128,256]{1,0:T(8,128)(2,1)S(1)}, bf16[128,256]{1,0:T(8,128)(2,1)S(1)}, u32[]{:S(2)}, u32[]{:S(2)}) %collective-permute-start.7) | collective-permute-done | bytes 65568 | tf_op jit(solution)/shard_map/ppermute | solution.py:353
  24.7 0.0 copy-start
  24.7 0.0 copy-start.2
  24.7 0.0 copy-start.3
  24.7 0.0 copy-start.4
  24.7 0.1 collective-permute-start.8
  24.8 1.8 %collective-permute-done.4.far_half = bf16[128,384]{1,0:T(8,128)(2,1)S(1)} collective-permute-done((bf16[128,384]{1,0:T(8,128)(2,1)S(1)}, bf16[128,384]{1,0:T(8,128)(2,1)S(1)}, u32[]{:S(2)}, u32[]{:S(2)}) %collective-permute-start.4) | collective-permute-done | bytes 98336 | tf_op jit(solution)/shard_map/ppermute | solution.py:353
  26.6 0.0 collective-permute-done.3.near_half
  26.6 0.0 copy-done.1
  26.6 0.1 weight.1.refs_4_
  26.7 0.0 collective-permute-done.8.refs_9_
  26.7 0.0 copy-done
  26.7 0.0 copy-done.2
  26.7 0.0 copy-done.3
  26.7 0.0 copy-done.4
  26.8 3.3 %heads.1 = (bf16[2,512,512]{2,1,0:T(8,128)(2,1)S(1)}, bf16[2,512,512]{2,1,0:T(8,128)(2,1)S(1)}, f32[2,1,512]{2,1,0:T(1,128)S(1)}, bf16[128,128]{1,0:T(8,128)(2,1...) custom-call(s32[4,4]{1,0:T(4,128)S(1)} %copy-done.3, ...), custom_call_target="tpu_custom_call" | custom-call | tf_op jit(solution)/shard_map/heads/pallas_call | solution.py:408
  30.0 0.1 collective-permute-start.9
  30.1 1.5 %collective-permute-start.10 = (bf16[128,256]{1,0:T(8,128)(2,1)S(1)}, bf16[128,256]{1,0:T(8,128)(2,1)S(1)}, u32[]{:S(2)}, u32[]{:S(2)}) collective-permute-start(bf16[128,256]{1,0:T(8,128)(2,1)S(1)} %get-tuple-element.26), channel_id=1, source_target_pairs={{0,2},{1,3},{2,0},{3,1},{4,6},{5,7},{6,4},{7,5},{8,10},{9,11},{10,... | collective-permute-start | bytes 196616 | tf_op jit(solution)/shard_map/ppermute | solution.py:353
  31.6 0.3 collective-permute-start.11
  32.0 2.5 %rest.1 = (bf16[128,128]{1,0:T(8,128)(2,1)}, f32[256,384]{1,0:T(8,128)}) custom-call(bf16[2,512,512]{2,1,0:T(8,128)(2,1)S(1)} %get-tuple-element.16.p_b_ref, bf16[2,512,512]{2,1,0:T(8,128)(2,1)S(1)} %get-tuple-element.17.p_rest_ref, f32[2,1,512]{2,1,0:T(1,128)S(1)} %get-tuple-element.18.grad_dot_ref, bf16[128,128]{1,0:T(8,128)(2,1)S(1)} %get-tuple-element.19.attention_t, ...), custom_call_target="tpu_custom_call" | custom-call | tf_op jit(solution)/shard_map/rest/pallas_call | solution.py:421
  34.5 0.0 collective-permute-done.9
  34.5 0.2 collective-permute-done.10
  34.6 1.1 %collective-permute-done.11 = bf16[128,256]{1,0:T(8,128)(2,1)S(1)} collective-permute-done((bf16[128,256]{1,0:T(8,128)(2,1)S(1)}, bf16[128,256]{1,0:T(8,128)(2,1)S(1)}, u32[]{:S(2)}, u32[]{:S(2)}) %collective-permute-start.11) | collective-permute-done | bytes 65568 | tf_op jit(solution)/shard_map/ppermute | solution.py:353
  35.8 0.7 %add_convert_fusion = bf16[128,256]{1,0:T(8,128)(2,1)} fusion(bf16[128,256]{1,0:T(8,128)(2,1)S(1)} %collective-permute-done.11, bf16[128,256]{1,0:T(8,128)(2,1)S(1)} %collective-permute-done.10, f32[128,256]{1,0:T(8,128)S(1)} %get-tuple-element.24, bf16[128,256]{1,0:T(8,128)(2,1)S(1)} %collective-permute-done.9), kind=kLoop, calls=%fused_computation.1 | loop fusion | flops 229376 | bytes 393216 | tf_op jit(solution)/shard_map/convert_element_type | solution.py:420
  (7 shorter events, 0.1 us)
Async XLA Ops:
  1.6 13.3 %collective-permute-start.1 = (bf16[128,768]{1,0:T(8,128)(2,1)S(1)}, bf16[128,768]{1,0:T(8,128)(2,1)S(1)}, u32[]{:S(2)}, u32[]{:S(2)}) collective-permute-start(bf16[128,768]{1,0:T(8,128)(2,1)S(1)} %pack.1), channel_id=1, source_target_pairs={{0,8},{4,12},{8,0},{12,4},{1,9},{5,13},{9,1},{13,5},{2,10},{6,14},... | collective-permute-start | bytes 589832 | tf_op jit(solution)/shard_map/ppermute | solution.py:353
  5.7 9.9 %collective-permute-start = (bf16[128,768]{1,0:T(8,128)(2,1)S(1)}, bf16[128,768]{1,0:T(8,128)(2,1)S(1)}, u32[]{:S(2)}, u32[]{:S(2)}) collective-permute-start(bf16[128,768]{1,0:T(8,128)(2,1)S(1)} %pack.1), channel_id=1, source_target_pairs={{0,4},{4,0},{8,12},{12,8},{1,5},{5,1},{9,13},{13,9},{2,6},{6,2},{1... | collective-permute-start | bytes 589832 | tf_op jit(solution)/shard_map/ppermute | solution.py:353
  14.9 5.4 %collective-permute-start.5 = (bf16[128,384]{1,0:T(8,128)(2,1)S(1)}, bf16[128,384]{1,0:T(8,128)(2,1)S(1)}, u32[]{:S(2)}, u32[]{:S(2)}) collective-permute-start(bf16[128,384]{1,0:T(8,128)(2,1)S(1)} %get-tuple-element.29), channel_id=1, source_target_pairs={{0,4},{4,0},{8,12},{12,8},{1,5},{5,1},{9,13},{13,9},{2,6},{6,2},{1... | collective-permute-start | bytes 294920 | tf_op jit(solution)/shard_map/ppermute | solution.py:353
  15.7 7.9 %collective-permute-start.6 = (bf16[256,256]{1,0:T(8,128)(2,1)S(1)}, bf16[256,256]{1,0:T(8,128)(2,1)S(1)}, u32[]{:S(2)}, u32[]{:S(2)}) collective-permute-start(bf16[256,256]{1,0:T(8,128)(2,1)S(1)} %slice.23), channel_id=1, source_target_pairs={{0,2},{1,3},{2,0},{3,1},{4,6},{5,7},{6,4},{7,5},{8,10},{9,11},{10,... | collective-permute-start | bytes 393224 | tf_op jit(solution)/shard_map/ppermute | solution.py:353
  17.2 4.8 %collective-permute-start.2 = (bf16[128,384]{1,0:T(8,128)(2,1)S(1)}, bf16[128,384]{1,0:T(8,128)(2,1)S(1)}, u32[]{:S(2)}, u32[]{:S(2)}) collective-permute-start(bf16[128,384]{1,0:T(8,128)(2,1)S(1)} %get-tuple-element.30), channel_id=1, source_target_pairs={{0,4},{4,0},{8,12},{12,8},{1,5},{5,1},{9,13},{13,9},{2,6},{6,2},{1... | collective-permute-start | bytes 294920 | tf_op jit(solution)/shard_map/ppermute | solution.py:353
  18.7 7.9 %collective-permute-start.3 = (bf16[256,384]{1,0:T(8,128)(2,1)S(1)}, bf16[256,384]{1,0:T(8,128)(2,1)S(1)}, u32[]{:S(2)}, u32[]{:S(2)}) collective-permute-start(bf16[256,384]{1,0:T(8,128)(2,1)S(1)} %slice.21), channel_id=1, source_target_pairs={{0,16},{16,0},{1,17},{17,1},{2,18},{18,2},{3,19},{19,3},{4,20},{20... | collective-permute-start | bytes 589832 | tf_op jit(solution)/shard_map/ppermute | solution.py:353
  20.3 6.3 %copy-start.1 = (bf16[256,384]{1,0:T(8,128)(2,1)S(1)}, bf16[256,384]{1,0:T(8,128)(2,1)}, u32[]{:S(2)}) copy-start(bf16[256,384]{1,0:T(8,128)(2,1)} %w0.1) | copy-start | bytes 589828
  20.3 4.3 %collective-permute-start.7 = (bf16[128,256]{1,0:T(8,128)(2,1)S(1)}, bf16[128,256]{1,0:T(8,128)(2,1)S(1)}, u32[]{:S(2)}, u32[]{:S(2)}) collective-permute-start(bf16[128,256]{1,0:T(8,128)(2,1)S(1)} %slice.24), channel_id=1, source_target_pairs={{0,2},{1,3},{2,0},{3,1},{4,6},{5,7},{6,4},{7,5},{8,10},{9,11},{10,... | collective-permute-start | bytes 196616 | tf_op jit(solution)/shard_map/ppermute | solution.py:353
  22.0 4.6 %collective-permute-start.4 = (bf16[128,384]{1,0:T(8,128)(2,1)S(1)}, bf16[128,384]{1,0:T(8,128)(2,1)S(1)}, u32[]{:S(2)}, u32[]{:S(2)}) collective-permute-start(bf16[128,384]{1,0:T(8,128)(2,1)S(1)} %collective-permute-done.2.far), channel_id=1, source_target_pairs={{0,16},{16,0},{1,17},{17,1},{2,18},{18,2},{3,19},{19,3},{4,20},{20... | collective-permute-start | bytes 294920 | tf_op jit(solution)/shard_map/ppermute | solution.py:353
  24.7 2.0 %copy-start = (bf16[128,1024]{1,0:T(8,128)(2,1)S(1)}, bf16[128,1024]{1,0:T(8,128)(2,1)}, u32[]{:S(2)}) copy-start(bf16[128,1024]{1,0:T(8,128)(2,1)} %refs_2_.1) | copy-start | bytes 786436
  24.7 2.0 %copy-start.2 = (bf16[128,128]{1,0:T(8,128)(2,1)S(1)}, bf16[128,128]{1,0:T(8,128)(2,1)}, u32[]{:S(2)}) copy-start(bf16[128,128]{1,0:T(8,128)(2,1)} %refs_3_.1) | copy-start | bytes 98308
  24.7 2.0 %copy-start.3 = (s32[4,4]{1,0:T(4,128)S(1)}, s32[4,4]{1,0:T(4,128)}, u32[]{:S(2)}) copy-start(s32[4,4]{1,0:T(4,128)} %refs_0_.1) | copy-start | bytes 196
  24.7 2.0 %copy-start.4 = (s32[4]{0:T(128)S(1)}, s32[4]{0:T(128)}, u32[]{:S(2)}) copy-start(s32[4]{0:T(128)} %refs_1_.1) | copy-start | bytes 52
  24.7 2.0 %collective-permute-start.8 = (bf16[768,256]{1,0:T(8,128)(2,1)S(1)}, bf16[768,256]{1,0:T(8,128)(2,1)S(1)}, u32[]{:S(2)}, u32[]{:S(2)}) collective-permute-start(bf16[768,256]{1,0:T(8,128)(2,1)S(1)} %pad_maximum_fusion), channel_id=1, source_target_pairs={{0,1},{1,0},{2,3},{3,2},{4,5},{5,4},{6,7},{7,6},{8,9},{9,8},{10,11... | collective-permute-start | bytes 1179656 | tf_op jit(solution)/shard_map/ppermute | solution.py:353
  30.0 4.4 %collective-permute-start.9 = (bf16[128,256]{1,0:T(8,128)(2,1)S(1)}, bf16[128,256]{1,0:T(8,128)(2,1)S(1)}, u32[]{:S(2)}, u32[]{:S(2)}) collective-permute-start(bf16[128,256]{1,0:T(8,128)(2,1)S(1)} %get-tuple-element.25), channel_id=1, source_target_pairs={{0,1},{1,0},{2,3},{3,2},{4,5},{5,4},{6,7},{7,6},{8,9},{9,8},{10,11... | collective-permute-start | bytes 196616 | tf_op jit(solution)/shard_map/ppermute | solution.py:353
  30.1 4.5 %collective-permute-start.10 = (bf16[128,256]{1,0:T(8,128)(2,1)S(1)}, bf16[128,256]{1,0:T(8,128)(2,1)S(1)}, u32[]{:S(2)}, u32[]{:S(2)}) collective-permute-start(bf16[128,256]{1,0:T(8,128)(2,1)S(1)} %get-tuple-element.26), channel_id=1, source_target_pairs={{0,2},{1,3},{2,0},{3,1},{4,6},{5,7},{6,4},{7,5},{8,10},{9,11},{10,... | collective-permute-start | bytes 196616 | tf_op jit(solution)/shard_map/ppermute | solution.py:353
  31.6 4.1 %collective-permute-start.11 = (bf16[128,256]{1,0:T(8,128)(2,1)S(1)}, bf16[128,256]{1,0:T(8,128)(2,1)S(1)}, u32[]{:S(2)}, u32[]{:S(2)}) collective-permute-start(bf16[128,256]{1,0:T(8,128)(2,1)S(1)} %get-tuple-element.27), channel_id=1, source_target_pairs={{0,3},{1,2},{2,1},{3,0},{4,7},{5,6},{6,5},{7,4},{8,11},{9,10},{10,... | collective-permute-start | bytes 196616 | tf_op jit(solution)/shard_map/ppermute | solution.py:353
